TPU v7x, 32 devices: a whole 2x2x4 slice. The times are simulated.
32 devices in a mesh: row: 4 (over y, core), col: 8 (over z, x).
Axes of the slice: x: 2, y: 2, z: 4, core: 2. Of those that a mesh axis runs over, the one named last changes fastest.
Arguments:
- ainv_top: float32 [4096, 4096], P('row', 'col'), may hold values from -0.25 to 0.25
- par_struct: int32 [8, 16], replicated, may hold values from 0 to 31, as said below
- par_panel: float32 [8, 16, 128, 128], P('col', 'row'), may hold values from -6 to 6
- par_linv: float32 [8, 128, 128], P('col', 'row'), may hold values from -0.0625 to 0.0625
- par_dinv: float32 [8, 128, 128], P('col', 'row'), may hold values from -192 to 192
- kid_panel: float32 [16, 16, 128, 128], P('col', 'row'), may hold values from -6 to 6
- kid_upper: float32 [16, 128, 128], P('col', 'row'), may hold values from -6 to 6
- kid_linv: float32 [16, 128, 128], P('col', 'row'), may hold values from -0.0625 to 0.0625
- kid_dinv: float32 [16, 128, 128], P('col', 'row'), may hold values from -192 to 192
Outputs:
- par_offdiag: float32 [8, 16, 128, 128], P('col', 'row')
- par_diag: float32 [8, 128, 128], P('col', 'row')
- kid_offdiag: float32 [16, 16, 128, 128], P('col', 'row')
- kid_parent: float32 [16, 128, 128], P('col', 'row')
- kid_diag: float32 [16, 128, 128], P('col', 'row')
Inputs may be any that keep to these rules, and one draw needn't show every extreme that they name: `par_struct`: in every row, entries 2j and 2j + 1 are two different ancestors among j * 4 to (j + 1) * 4 - 1.
All inputs are finite; a program needn't handle non-finite values.
Results may differ from a plain program's by a relative error of at most 0.00014.
Values sent between devices are 32-bit elements; how exact they have to be, the bound alone decides.
No kernel may reach another device: no remote copies, remote signals or barrier semaphores. Data moves between devices by JAX's collectives and lax.ppermute only.
A program may use at most 128 MiB of HBM per device.

v0:
```python
import jax
import jax.numpy as jnp
from jax import lax
from jax.sharding import PartitionSpec as P

highest = lax.Precision.HIGHEST


def spread(array, axis, root):
    mine = lax.axis_index(axis) == root
    return lax.psum(jnp.where(mine, array, jnp.zeros_like(array)), axis)


def on_device(
    ainv_top, par_struct, par_panel, par_linv, par_dinv, kid_panel, kid_upper, kid_linv, kid_dinv
):
    grid_rows = lax.axis_size("row")
    grid_cols = lax.axis_size("col")
    my_row = lax.axis_index("row")
    my_col = lax.axis_index("col")
    tile_width = par_panel.shape[-1]
    band_rows = tile_width // grid_rows
    parents = par_panel.shape[0]
    slot_share = par_panel.shape[1]
    children = kid_panel.shape[0]
    brood = children // parents
    slots_all = par_struct.shape[1]
    pair_width = slots_all // grid_cols
    tile_rows = ainv_top.shape[0] // tile_width
    tile_cols = ainv_top.shape[1] // tile_width
    local_tiles = ainv_top.reshape(tile_rows, tile_width, tile_cols, tile_width)
    row_base = my_row * tile_rows
    col_base = my_col * tile_cols
    band_start = my_row * band_rows
    par_linv_full, par_dinv_full = (
        lax.all_gather(par_linv, "row", axis=1, tiled=True),
        lax.all_gather(par_dinv, "row", axis=1, tiled=True),
    )
    par_hat = jnp.einsum("psij,pjk->psik", par_panel, par_linv_full, precision=highest)
    owner_rows = lax.dynamic_slice_in_dim(par_struct, my_row * slot_share, slot_share, 1) - row_base
    owner_cols = lax.dynamic_slice_in_dim(par_struct, my_col * pair_width, pair_width, 1) - col_base
    root_row = my_col * pair_width // slot_share
    within = my_col * pair_width - root_row * slot_share
    every_hat = lax.all_gather(par_hat, "col", axis=0, tiled=True)
    picked = lax.dynamic_slice_in_dim(every_hat, within, pair_width, 1)
    picked = spread(picked, "row", root_row)
    rows_here = owner_rows
    cols_here = owner_cols
    picks_here = picked
    tiles_here = local_tiles[rows_here[:, :, None], :, cols_here[:, None, :], :]
    par_prod = lax.psum_scatter(
        jnp.einsum("pjkab,pkbc->pjac", tiles_here, picks_here, precision=highest),
        "col",
        scatter_dimension=0,
        tiled=True,
    )
    par_off = -par_prod
    pivot_term = jnp.einsum(
        "pji,pjk,pkl->pil", par_linv_full, par_dinv_full, par_linv_full, precision=highest
    )
    diag_part = -jnp.einsum("psji,psjk->pik", par_hat, par_off, precision=highest)
    par_diag_full = pivot_term + lax.psum(diag_part, "row")
    par_diag_band = lax.dynamic_slice_in_dim(par_diag_full, band_start, band_rows, 1)
    kid_upper_full, kid_linv_full, kid_dinv_full = (
        lax.all_gather(kid_upper, "row", axis=1, tiled=True),
        lax.all_gather(kid_linv, "row", axis=1, tiled=True),
        lax.all_gather(kid_dinv, "row", axis=1, tiled=True),
    )
    kid_hat = jnp.einsum("csij,cjk->csik", kid_panel, kid_linv_full, precision=highest)
    kid_uphat = jnp.einsum("cij,cjk->cik", kid_upper_full, kid_linv_full, precision=highest)
    kid_rows = jnp.repeat(owner_rows, brood, axis=0)
    kid_cols = jnp.repeat(owner_cols, brood, axis=0)
    every_kid = lax.all_gather(kid_hat, "col", axis=0, tiled=True)
    kid_picked = lax.dynamic_slice_in_dim(every_kid, within, pair_width, 1)
    kid_picked = spread(kid_picked, "row", root_row)
    rows_here = kid_rows
    cols_here = kid_cols
    picks_here = kid_picked
    tiles_here = local_tiles[rows_here[:, :, None], :, cols_here[:, None, :], :]
    kid_prod = lax.psum_scatter(
        jnp.einsum("pjkab,pkbc->pjac", tiles_here, picks_here, precision=highest),
        "col",
        scatter_dimension=0,
        tiled=True,
    )
    uphat_grouped = kid_uphat.reshape(parents, brood, tile_width, tile_width)
    kid_off = -(
        kid_prod.reshape(parents, brood, slot_share, tile_width, tile_width)
        + jnp.einsum("pjab,pibc->pijac", par_off, uphat_grouped, precision=highest)
    )
    kid_off = kid_off.reshape(children, slot_share, tile_width, tile_width)
    linv_band = lax.dynamic_slice_in_dim(kid_linv_full, band_start, band_rows, 2)
    kid_pivot_band = jnp.einsum(
        "cji,cjk,ckl->cil", linv_band, kid_dinv_full, kid_linv_full, precision=highest
    )
    parent_part = jnp.einsum(
        "pjba,pijbc->piac",
        par_off,
        kid_hat.reshape(parents, brood, slot_share, tile_width, tile_width),
        precision=highest,
    ).reshape(children, tile_width, tile_width)
    hat_part = -jnp.einsum("csji,csjk->cik", kid_hat, kid_off, precision=highest)
    diag_times = jnp.einsum(
        "pab,pibc->piac", par_diag_full, uphat_grouped, precision=highest
    ).reshape(children, tile_width, tile_width)
    uphat_band = lax.dynamic_slice_in_dim(kid_uphat, band_start, band_rows, 2)
    parent_sum = lax.psum(parent_part, "row")
    kid_par_full = -(parent_sum + diag_times)
    diag_sum = lax.psum_scatter(hat_part, "row", scatter_dimension=1, tiled=True)
    kid_diag_band = (
        kid_pivot_band
        + diag_sum
        - jnp.einsum("cji,cjk->cik", uphat_band, kid_par_full, precision=highest)
    )
    kid_par_band = lax.dynamic_slice_in_dim(kid_par_full, band_start, band_rows, 1)
    return (par_off, par_diag_band, kid_off, kid_par_band, kid_diag_band)


def solution(mesh):
    placed = (
        P("row", "col"),
        P(),
        P("col", "row", None, None),
        P("col", "row", None),
        P("col", "row", None),
        P("col", "row", None, None),
        P("col", "row", None),
        P("col", "row", None),
        P("col", "row", None),
    )
    return jax.shard_map(
        on_device,
        mesh=mesh,
        in_specs=placed,
        out_specs=(
            P("col", "row", None, None),
            P("col", "row", None),
            P("col", "row", None, None),
            P("col", "row", None),
            P("col", "row", None),
        ),
        check_vma=False,
    )
```

profile of v0, /device:TPU:0, one launch (start us, length us, event | category | flops | bytes accessed | tf_op | source)
XLA Modules:
  0.0 442.1 jit_solution(8733068069592860143)
XLA Ops:
  7.2 6.6 %all_gather.21 = f32[1,128,128]{2,1,0:T(8,128)S(1)} all-gather(f32[1,32,128]{2,1,0:T(8,128)} %param.12), channel_id=1, replica_groups=mesh['row'=4,'col'=8] {'row'}, dimensions={1}, use_global_device_ids=true | all-gather | bytes 81920 | tf_op jit(solution)/shard_map/all_gather | solution.py:36
  14.4 2.0 fusion.14
  16.6 51.1 %all-gather.6.cloned.1.call-done = f32[32,128,128]{2,1,0:T(8,128)} async-done(((f32[4,128,128]{2,1,0:T(8,128)}), f32[32,128,128]{2,1,0:T(8,128)}) %all-gather.6.cloned.1.call-update) | async-done | bytes 2097168 | tf_op jit(solution)/shard_map/all_gather | solution.py:44
  67.7 2.3 dynamic-slice_select_fusion.1
  70.1 5.6 %all_gather.24 = f32[2,128,128]{2,1,0:T(8,128)S(1)} all-gather(f32[2,32,128]{2,1,0:T(8,128)} %param.16), channel_id=1, replica_groups=mesh['row'=4,'col'=8] {'row'}, dimensions={1}, use_global_device_ids=true | all-gather | bytes 163840 | tf_op jit(solution)/shard_map/all_gather | solution.py:66
  75.7 1.4 fusion.17
  77.2 1.7 reshape.154
  78.9 1.9 copy.51
  81.2 2.9 gather_fusion
  84.0 20.7 %all-reduce.4.cloned.1.call-done = f32[8,2,128,128]{3,2,1,0:T(8,128)} async-done(((f32[8,2,128,128]{3,2,1,0:T(8,128)}), f32[8,2,128,128]{3,2,1,0:T(8,128)}) %all-reduce.4.cloned.1.call-update) | async-done | bytes 1048592 | tf_op jit(solution)/shard_map/psum | solution.py:11
  104.7 7.5 %convolution_bitcast_fusion.1 = f32[8,4,128,128]{3,2,1,0:T(8,128)} fusion(f32[8,4,2,128,128]{4,3,2,1,0:T(8,128)} %bitcast.127, f32[8,2,128,128]{3,2,1,0:T(8,128)} %all-reduce.4.cloned.1.call-done), kind=kOutput, calls=%fused_computation.5 | convolution fusion | flops 1610612736 | bytes 7340032 | tf_op jit(solution)/shard_map/pjkab,pkbc->pjac/dot_general | solution.py:52
  112.3 69.1 %all-gather.4.cloned.1.call-done = f32[16,4,128,128]{3,2,1,0:T(8,128)} async-done(((f32[2,4,128,128]{3,2,1,0:T(8,128)}), f32[16,4,128,128]{3,2,1,0:T(8,128)}) %all-gather.4.cloned.1.call-update) | async-done | bytes 4194320 | tf_op jit(solution)/shard_map/all_gather | solution.py:73
  181.5 3.2 dynamic-slice_select_fusion
  184.7 66.5 %reduce-scatter.4.cloned.1.call-done = f32[1,4,128,128]{3,2,1,0:T(8,128)} async-done(((f32[8,4,128,128]{3,2,1,0:T(8,128)}), f32[1,4,128,128]{3,2,1,0:T(8,128)}) %reduce-scatter.4.cloned.1.call-update) | async-done | bytes 262160 | tf_op jit(solution)/shard_map/reduce_scatter | solution.py:51
  251.2 1.0 neg.18
  252.2 2.3 fusion.8
  254.5 1.7 convolution_bitcast_fusion.4
  257.2 0.8 copy.54
  258.0 0.7 broadcast_or_fusion
  258.7 0.9 reshape.135
  259.6 4.5 %gather_fusion.1 = f32[128,128,128]{2,1,0:T(8,128)} fusion(f32[8,128,4,128]{3,1,2,0:T(8,128)S(1)} %copy.51, s32[128]{0:T(128)S(1)} %reshape.135), kind=kCustom, calls=%fused_computation.1 | custom fusion | bytes 16778240 | tf_op jit(solution)/shard_map/gather | solution.py:79
  264.0 46.2 %all-reduce.6.cloned.1.call-done = (f32[1,128,128]{2,1,0:T(8,128)}, f32[16,2,128,128]{3,2,1,0:T(8,128)}, f32[2,128,128]{1,2,0:T(8,128)}) async-done(((f32[1,128,128]{2,1,0:T(8,128)}, f32[16,2,128,128]{3,2,1,0:T(8,128)}, f32[2,128,128]{1,2,0:T(8,128)}), (f32[1,128,128]{2,1,0:T(8,128)}, f32[16,2,128,128]{3,2,1,0:T(8,128)}, f32[2,128,128]{1,2,0:T(8,128)})) %all-reduce.6.cloned.1.call-update) | async-done | bytes 2293776 | tf_op jit(solution)/shard_map/psum | solution.py:62
  310.3 12.1 %convolution_bitcast_fusion = f32[16,4,128,128]{3,2,1,0:T(8,128)} fusion(f32[16,4,2,128,128]{4,3,2,1,0:T(8,128)} %bitcast.126, f32[16,2,128,128]{3,2,1,0:T(8,128)} %get-tuple-element.26), kind=kOutput, calls=%fused_computation.2 | convolution fusion | flops 3221225472 | bytes 14680064 | tf_op jit(solution)/shard_map/pjkab,pkbc->pjac/dot_general | solution.py:81
  323.0 5.2 %all_gather.23 = f32[1,128,128]{2,1,0:T(8,128)S(1)} all-gather(f32[1,32,128]{2,1,0:T(8,128)S(1)} %copy-done.11), channel_id=1, replica_groups=mesh['row'=4,'col'=8] {'row'}, dimensions={1}, use_global_device_ids=true | all-gather | bytes 81920 | tf_op jit(solution)/shard_map/all_gather | solution.py:37
  328.3 5.4 %all_gather.26 = f32[2,128,128]{2,1,0:T(8,128)S(1)} all-gather(f32[2,32,128]{2,1,0:T(8,128)S(1)} %copy-done.9), channel_id=1, replica_groups=mesh['row'=4,'col'=8] {'row'}, dimensions={1}, use_global_device_ids=true | all-gather | bytes 163840 | tf_op jit(solution)/shard_map/all_gather | solution.py:65
  333.7 5.4 %all_gather.27 = f32[2,128,128]{2,1,0:T(8,128)S(1)} all-gather(f32[2,32,128]{2,1,0:T(8,128)S(1)} %copy-done.10), channel_id=1, replica_groups=mesh['row'=4,'col'=8] {'row'}, dimensions={1}, use_global_device_ids=true | all-gather | bytes 163840 | tf_op jit(solution)/shard_map/all_gather | solution.py:67
  340.5 70.0 %reduce-scatter.6.cloned.1.call-done = f32[2,4,128,128]{3,2,1,0:T(8,128)} async-done(((f32[16,4,128,128]{3,2,1,0:T(8,128)}), f32[2,4,128,128]{3,2,1,0:T(8,128)}) %reduce-scatter.6.cloned.1.call-update) | async-done | bytes 524304 | tf_op jit(solution)/shard_map/reduce_scatter | solution.py:80
  410.5 1.6 fusion.3
  412.2 1.7 fusion.4
  415.6 17.8 %reduce-scatter.8.cloned.1.call-done = f32[2,32,128]{2,1,0:T(8,128)} async-done(((f32[2,128,128]{2,1,0:T(8,128)}), f32[2,32,128]{2,1,0:T(8,128)}) %reduce-scatter.8.cloned.1.call-update) | async-done | bytes 32784 | tf_op jit(solution)/shard_map/reduce_scatter | solution.py:109
  433.4 1.0 convolution_add_fusion
  434.3 0.9 convolution_subtract_fusion
  (58 shorter events, 6.1 us)
Async XLA Ops:
  7.2 68.5 %copy-start = (f32[2,4,128,128]{3,2,1,0:T(8,128)S(1)}, f32[2,4,128,128]{3,2,1,0:T(8,128)}, u32[]{:S(2)}) copy-start(f32[2,4,128,128]{3,2,1,0:T(8,128)} %param.14) | copy-start | bytes 1572868
  7.2 70.0 %copy-start.3 = (f32[1024,512]{1,0:T(8,128)S(1)}, f32[1024,512]{1,0:T(8,128)}, u32[]{:S(2)}) copy-start(f32[1024,512]{1,0:T(8,128)} %param.9) | copy-start | bytes 6291460
  7.2 60.5 %all-gather.6.cloned.1.call-start = ((), (), s32[]{:S(2)}) async-start(), calls=%async_computation.8 | async-start | bytes 2359296 | tf_op jit(solution)/shard_map/all_gather | solution.py:44
  13.8 0.6 copy-start.5
  16.5 88.2 %all-reduce.4.cloned.1.call-start = ((), (), s32[]{:S(2)}) async-start(), calls=%async_computation.3 | async-start | bytes 2097152 | tf_op jit(solution)/shard_map/psum | solution.py:11
  70.0 111.5 %all-gather.4.cloned.1.call-start = ((), (), s32[]{:S(2)}) async-start(), calls=%async_computation.5 | async-start | bytes 4718592 | tf_op jit(solution)/shard_map/all_gather | solution.py:73
  77.1 174.1 %reduce-scatter.4.cloned.1.call-start = ((), (), s32[]{:S(2)}) async-start(), calls=%async_computation.4 | async-start | bytes 2359296 | tf_op jit(solution)/shard_map/reduce_scatter | solution.py:51
  77.2 3.6 copy-start.12
  112.3 142.2 %copy-start.1 = (f32[2,4,128,128]{3,2,1,0:T(8,128)S(1)}, f32[2,4,128,128]{3,2,1,0:T(8,128)}, u32[]{:S(2)}) copy-start(f32[2,4,128,128]{3,2,1,0:T(8,128)} %fusion.17) | copy-start | bytes 1572868
  112.3 198.0 %all-reduce.6.cloned.1.call-start = ((), (), s32[]{:S(2)}) async-start(), calls=%async_computation.9 | async-start | bytes 4587520 | tf_op jit(solution)/shard_map/psum | solution.py:62
  252.2 158.4 %copy-start.2 = (f32[1,4,128,128]{3,2,1,0:T(8,128)}, f32[1,4,128,128]{3,2,1,0:T(8,128)S(1)}, u32[]{:S(2)}) copy-start(f32[1,4,128,128]{3,2,1,0:T(8,128)S(1)} %neg.18) | copy-start | bytes 786436
  256.1 154.4 %reduce-scatter.6.cloned.1.call-start = ((), (), s32[]{:S(2)}) async-start(), calls=%async_computation.6 | async-start | bytes 4718592 | tf_op jit(solution)/shard_map/reduce_scatter | solution.py:80
  322.3 0.7 copy-start.11
  322.3 5.9 %copy-start.9 = (f32[2,32,128]{2,1,0:T(8,128)S(1)}, f32[2,32,128]{2,1,0:T(8,128)}, u32[]{:S(2)}) copy-start(f32[2,32,128]{2,1,0:T(8,128)} %param.15) | copy-start | bytes 98308
  322.3 11.4 %copy-start.10 = (f32[2,32,128]{2,1,0:T(8,128)S(1)}, f32[2,32,128]{2,1,0:T(8,128)}, u32[]{:S(2)}) copy-start(f32[2,32,128]{2,1,0:T(8,128)} %param.17) | copy-start | bytes 98308
  322.3 17.2 %copy-start.6 = (f32[1,128,128]{2,1,0:T(8,128)S(1)}, f32[1,128,128]{2,1,0:T(8,128)}, u32[]{:S(2)}) copy-start(f32[1,128,128]{2,1,0:T(8,128)} %copy-done.5) | copy-start | bytes 196612
  322.4 17.9 %copy-start.8 = (f32[1,128,128]{2,1,0:T(8,128)S(1)}, f32[1,128,128]{2,1,0:T(8,128)}, u32[]{:S(2)}) copy-start(f32[1,128,128]{2,1,0:T(8,128)} %get-tuple-element.25) | copy-start | bytes 196612
  322.4 91.5 %copy-start.7 = (f32[2,128,128]{1,2,0:T(8,128)S(1)}, f32[2,128,128]{1,2,0:T(8,128)}, u32[]{:S(2)}) copy-start(f32[2,128,128]{1,2,0:T(8,128)} %get-tuple-element.27) | copy-start | bytes 393220
  322.4 111.0 %reduce-scatter.8.cloned.1.call-start = ((), (), s32[]{:S(2)}) async-start(), calls=%async_computation.7 | async-start | bytes 163840 | tf_op jit(solution)/shard_map/reduce_scatter | solution.py:109
  412.2 23.1 %copy-start.4 = (f32[2,4,128,128]{3,2,1,0:T(8,128)}, f32[2,4,128,128]{3,2,1,0:T(8,128)S(1)}, u32[]{:S(2)}) copy-start(f32[2,4,128,128]{3,2,1,0:T(8,128)S(1)} %fusion.3) | copy-start | bytes 1572868
Sparse Core Ops, SparseCore 0:
  16.6 50.9 all-gather.5
  70.1 34.5 all-reduce.3
  107.7 73.7 all-gather.3
  185.3 65.8 reduce-scatter.3
  256.3 53.9 all-reduce.5
  322.5 87.9 reduce-scatter.5
  414.0 19.3 reduce-scatter.7
where the time goes:
time: 443 us; the launch traced here: 442 us
  waiting for transfers between devices  342 us (77%)
  matrix products  33.7 us (8%)
  blocking collectives  28.3 us (6%)
  local copies, waits for them, and re-layouts  15.7 us (4%)
  between operations  14.3 us (3%)
  other arithmetic  8.02 us (2%)
    reduce_scatter x2, waiting for transfers between devices, on_device(): lax.psum_scatter(jnp.einsum('pjkab,pkbc->pjac', tiles_here, picks_here, p...  137 us
    all_gather x1, waiting for transfers between devices, on_device(): every_kid = lax.all_gather(kid_hat, 'col', axis=0, tiled=True)  69.1 us
    all_gather x1, waiting for transfers between devices, on_device(): every_hat = lax.all_gather(par_hat, 'col', axis=0, tiled=True)  51.1 us
    psum x1, waiting for transfers between devices, on_device(): par_diag_full = pivot_term + lax.psum(diag_part, 'row')  46.2 us
    psum x1, waiting for transfers between devices, spread(): return lax.psum(jnp.where(mine, array, jnp.zeros_like(array)), axis)  20.7 us
    dot_general x2, matrix products, on_device(): jnp.einsum('pjkab,pkbc->pjac', tiles_here, picks_here, precision=highest)  19.6 us
    reduce_scatter x1, waiting for transfers between devices, on_device(): lax.psum_scatter(hat_part, 'row', scatter_dimension=1, tiled=True)  17.8 us
  transfers between devices with their start and end apart: 7, of which 7 were waited for; matrix products, arithmetic and copies ran while one was open for 7% of the time, Pallas kernels for 0%

commit v1 on v0

v1 whole, which is shorter than its diff:
```python
import jax
import jax.numpy as jnp
from jax import lax
from jax.sharding import PartitionSpec as P

high = lax.Precision.HIGH
highest = lax.Precision.HIGHEST


def mm(spec, *operands, precision=high):
    return jnp.einsum(spec, *operands, precision=precision)


def on_device(
    ainv_top, par_struct, par_panel, par_linv, par_dinv, kid_panel, kid_upper, kid_linv, kid_dinv
):
    grid_rows = lax.axis_size("row")
    grid_cols = lax.axis_size("col")
    my_row = lax.axis_index("row")
    my_col = lax.axis_index("col")
    width = par_panel.shape[-1]
    band_rows = width // grid_rows
    slot_share = par_panel.shape[1]
    children = kid_panel.shape[0]
    pair_width = par_struct.shape[1] // grid_cols
    tile_rows = ainv_top.shape[0] // width
    tile_cols = ainv_top.shape[1] // width

    local_tiles = ainv_top.reshape(tile_rows, width, tile_cols, width)
    pick_rows = lax.dynamic_slice_in_dim(par_struct, my_row * slot_share, slot_share, 1)
    pick_cols = lax.dynamic_slice_in_dim(par_struct, my_col * pair_width, pair_width, 1)
    pick_rows = pick_rows - my_row * tile_rows
    pick_cols = pick_cols - my_col * tile_cols
    tiles = local_tiles[pick_rows[:, :, None], :, pick_cols[:, None, :], :]

    small = jnp.concatenate([par_linv, par_dinv, kid_upper, kid_linv, kid_dinv], axis=0)
    small = lax.all_gather(small, "row", axis=1, tiled=True)
    plinv, pdinv = small[0], small[1]
    kupper = small[2 : 2 + children]
    klinv = small[2 + children : 2 + 2 * children]
    kdinv = small[2 + 2 * children :]
    panels = jnp.concatenate([par_panel, kid_panel], axis=0)
    every = lax.all_gather(panels, "row", axis=1, tiled=True)

    moved = lax.all_to_all(tiles, "col", 0, 0, tiled=True)
    every = every.reshape(1 + children, grid_cols, pair_width, width, width)
    prod = mm("cjkab,nckbd->njad", moved, every)

    par_off = -mm("jab,bc->jac", prod[0], plinv)
    par_hat = mm("jab,bc->jac", par_panel[0], plinv)
    kid_hat = mm("njab,nbc->njac", kid_panel, klinv)
    kuphat = mm("nab,nbc->nac", kupper, klinv)
    kid_sum = prod[1:] + mm("jab,nbc->njac", par_off, kupper)
    kid_off = -mm("njab,nbc->njac", kid_sum, klinv)

    diag_part = mm("jba,jbc->ac", par_hat, par_off)
    parent_part = mm("jba,njbc->nac", par_off, kid_hat)
    hat_part = mm("njba,njbc->nac", kid_hat, kid_off)
    inner = parent_part - mm("ab,nbc->nac", diag_part, kuphat)
    edge_part = mm("nba,nbc->nac", kuphat, inner) - hat_part
    parts = jnp.concatenate([diag_part[None], parent_part, edge_part], axis=0)
    parts = parts.reshape(1 + 2 * children, grid_rows, band_rows, width)
    parts = lax.all_to_all(parts, "row", 1, 1, tiled=True)
    sums = parts.sum(axis=1)

    par_pivot = mm("ba,bc,cd->ad", plinv, pdinv, plinv)
    kid_pivot = mm("nba,nbc,ncd->nad", klinv, kdinv, klinv)
    kid_pivot = kid_pivot + mm("nba,bc,ncd->nad", kuphat, par_pivot, kuphat)
    start = my_row * band_rows
    par_diag = lax.dynamic_slice_in_dim(par_pivot, start, band_rows, 0) - sums[0]
    kid_par = -(sums[1 : 1 + children] + mm("ab,nbc->nac", par_diag, kuphat))
    kid_diag = lax.dynamic_slice_in_dim(kid_pivot, start, band_rows, 1) + sums[1 + children :]
    return par_off[None], par_diag[None], kid_off, kid_par, kid_diag


def solution(mesh):
    placed = (
        P("row", "col"),
        P(),
        P("col", "row", None, None),
        P("col", "row", None),
        P("col", "row", None),
        P("col", "row", None, None),
        P("col", "row", None),
        P("col", "row", None),
        P("col", "row", None),
    )
    return jax.shard_map(
        on_device,
        mesh=mesh,
        in_specs=placed,
        out_specs=(
            P("col", "row", None, None),
            P("col", "row", None),
            P("col", "row", None, None),
            P("col", "row", None),
            P("col", "row", None),
        ),
        check_vma=False,
    )
```

time: 443 us -> 148 us (0.33)
  waiting for transfers between devices: 342 us -> 89.2 us
  blocking collectives: 28.3 us -> 7.2 us
  matrix products: 33.7 us -> 13.9 us
  starting transfers between devices: 0.47 us -> 10.9 us
  local copies, waits for them, and re-layouts: 15.7 us -> 7.82 us
    reduce_scatter x3 -> x0, waiting for transfers between devices: 154 us -> none  [the longest x2 137 us: on_device(): lax.psum_scatter(jnp.einsum('pjkab,pkbc->pjac', tiles_here, picks_here, p...]
    all_gather x2 -> x1, waiting for transfers between devices: 120 us -> 22.1 us  [on_device(): every = lax.all_gather(panels, 'row', axis=1, tiled=True)]
    all_to_all x0 -> x2, waiting for transfers between devices: none -> 67 us  [the longest x1 60.8 us: on_device(): moved = lax.all_to_all(tiles, 'col', 0, 0, tiled=True)]
    psum x2 -> x0, waiting for transfers between devices: 66.9 us -> none  [the longest x1 46.2 us: on_device(): par_diag_full = pivot_term + lax.psum(diag_part, 'row')]
    all_gather x5 -> x1, blocking collectives: 28.3 us -> 7.2 us  [on_device(): small = lax.all_gather(small, 'row', axis=1, tiled=True)]
    dot_general x15 -> x19, matrix products: 33.7 us -> 13.9 us  [mm(): return jnp.einsum(spec, *operands, precision=precision)]
    all_to_all x0 -> x2, starting transfers between devices: none -> 10.8 us  [the longest x1 7.4 us: on_device(): moved = lax.all_to_all(tiles, 'col', 0, 0, tiled=True)]
    select_n x2 -> x0, other arithmetic: 5.53 us -> none  [spread(): return lax.psum(jnp.where(mine, array, jnp.zeros_like(array)), axis)]
  transfers between devices with their start and end apart: 7 -> 3, of which waited for: 7 -> 3; matrix products, arithmetic and copies ran while one was open for 7% -> 2% of each run, Pallas kernels for 0% -> 0%
where the time goes in v1:
time: 148 us
  waiting for transfers between devices  89.2 us (60%)
  between operations  14.3 us (10%)
  matrix products  13.9 us (9%)
  starting transfers between devices  10.9 us (7%)
  local copies, waits for them, and re-layouts  7.82 us (5%)
  blocking collectives  7.2 us (5%)
  other arithmetic  4.55 us (3%)
    all_to_all x1, waiting for transfers between devices, on_device(): moved = lax.all_to_all(tiles, 'col', 0, 0, tiled=True)  60.8 us
    all_gather x1, waiting for transfers between devices, on_device(): every = lax.all_gather(panels, 'row', axis=1, tiled=True)  22.1 us
    dot_general x19, matrix products, mm(): return jnp.einsum(spec, *operands, precision=precision)  13.9 us
    all_to_all x1, starting transfers between devices, on_device(): moved = lax.all_to_all(tiles, 'col', 0, 0, tiled=True)  7.4 us
    all_gather x1, blocking collectives, on_device(): small = lax.all_gather(small, 'row', axis=1, tiled=True)  7.2 us
    all_to_all x1, waiting for transfers between devices, on_device(): parts = lax.all_to_all(parts, 'row', 1, 1, tiled=True)  6.27 us
    reshape x2, local copies, waits for them, and re-layouts, on_device(): local_tiles = ainv_top.reshape(tile_rows, width, tile_cols, width)  4.78 us
    all_to_all x1, starting transfers between devices, on_device(): parts = lax.all_to_all(parts, 'row', 1, 1, tiled=True)  3.45 us
  transfers between devices with their start and end apart: 3, of which 3 were waited for; matrix products, arithmetic and copies ran while one was open for 2% of the time, Pallas kernels for 0%

profile of v1, /device:TPU:0, one launch (start us, length us, event | category | flops | bytes accessed | tf_op | source)
XLA Modules:
  0.0 147.9 jit_solution(1128994719983951276)
XLA Ops:
  7.2 0.8 fusion.41
  7.9 0.8 fusion.43
  8.9 2.9 %reshape.58 = f32[8,128,4,128]{3,2,1,0:T(4,128)} reshape(f32[1024,512]{1,0:T(8,128)} %param.9) | data formatting | bytes 4194304 | tf_op jit(solution)/shard_map/reshape | solution.py:29
  11.8 1.9 %copy.49 = f32[8,128,4,128]{3,1,2,0:T(8,128)S(1)} copy(f32[8,128,4,128]{3,2,1,0:T(4,128)} %reshape.58) | data formatting | bytes 4194304 | tf_op jit(solution)/shard_map/reshape | solution.py:29
  13.7 2.9 %gather_fusion = f32[64,128,128]{2,1,0:T(8,128)} fusion(f32[8,128,4,128]{3,1,2,0:T(8,128)S(1)} %copy.49, s32[64]{0:T(128)S(1)} %reshape.36), kind=kCustom, calls=%fused_computation | custom fusion | bytes 8389120 | tf_op jit(solution)/shard_map/gather | solution.py:34
  16.6 7.4 %all-to-all-start = ((f32[8,4,2,128,128]{4,3,2,1,0:T(8,128)}), f32[8,4,2,128,128]{4,3,2,1,0:T(8,128)}, u32[]{:S(2)}, u32[]{:S(2)}) async-start(f32[8,4,2,128,128]{4,3,2,1,0:T(8,128)} %bitcast.134), calls=%async_computation | async-start | bytes 8388608 | tf_op jit(solution)/shard_map/all_to_all | solution.py:45
  24.0 1.0 pad_maximum_fusion
  25.1 7.2 %all_gather.7 = f32[8,128,128]{2,1,0:T(8,128)S(1)} all-gather(f32[8,32,128]{2,1,0:T(8,128)S(1)} %constant_dynamic-update-slice_fusion), channel_id=1, replica_groups=mesh['row'=4,'col'=8] {'row'}, dimensions={1}, use_global_device_ids=true | all-gather | bytes 655360 | tf_op jit(solution)/shard_map/all_gather | solution.py:37
  32.3 0.3 fusion.24
  32.6 0.2 fusion.30
  32.8 0.2 fusion.21
  33.0 0.3 fusion.25
  33.3 0.3 convolution_bitcast_fusion.2
  33.7 0.3 fusion.17
  34.0 0.4 convolution_bitcast_fusion.1
  34.4 22.1 %all-gather.2.cloned.1.call-done = f32[3,16,128,128]{3,2,1,0:T(8,128)} async-done(((f32[3,4,128,128]{3,2,1,0:T(8,128)}), f32[3,16,128,128]{3,2,1,0:T(8,128)}) %all-gather.2.cloned.1.call-update) | async-done | bytes 3145744 | tf_op jit(solution)/shard_map/all_gather | solution.py:43
  56.5 60.8 %all-to-all-done = f32[8,4,2,128,128]{4,3,2,1,0:T(8,128)} async-done(((f32[8,4,2,128,128]{4,3,2,1,0:T(8,128)}), f32[8,4,2,128,128]{4,3,2,1,0:T(8,128)}, u32[]{:S(2)}, u32[]{:S(2)}) %all-to-all-start) | async-done | bytes 4194336 | tf_op jit(solution)/shard_map/all_to_all | solution.py:45
  117.3 7.8 %fusion.3 = f32[3,4,128,128]{2,3,1,0:T(8,128)S(1)} fusion(f32[3,8,2,128,128,1]{4,3,2,1,5,0:T(8,128)} %bitcast.136, f32[8,4,2,128,128]{4,3,2,1,0:T(8,128)} %all-to-all-done), kind=kOutput, calls=%fused_computation.4 | convolution fusion | flops 2415919104 | bytes 8126464 | tf_op jit(solution)/shard_map/cjkab,nckbd->njad/dot_general | solution.py:11
  125.1 0.4 convolution_negate_fusion.1
  125.5 0.4 fusion.6
  126.0 0.4 fusion.11
  126.3 0.3 fusion.45
  126.6 0.6 convolution_negate_fusion
  127.2 0.4 convolution_bitcast_fusion.3
  127.6 0.2 fusion.7
  127.8 0.3 convolution_subtract_fusion
  128.1 0.7 pad_maximum_fusion.1
  128.8 3.5 %all-to-all-start.1 = ((f32[5,4,32,128]{3,2,0,1:T(8,128)}), f32[5,4,32,128]{3,2,0,1:T(8,128)S(1)}, u32[]{:S(2)}, u32[]{:S(2)}) async-start(f32[5,4,32,128]{3,2,0,1:T(8,128)} %pad_maximum_fusion.1), calls=%async_computation.1 | async-start | bytes 655360 | tf_op jit(solution)/shard_map/all_to_all | solution.py:63
  132.7 6.3 %all-to-all-done.1 = f32[5,4,32,128]{3,2,0,1:T(8,128)S(1)} async-done(((f32[5,4,32,128]{3,2,0,1:T(8,128)}), f32[5,4,32,128]{3,2,0,1:T(8,128)S(1)}, u32[]{:S(2)}, u32[]{:S(2)}) %all-to-all-start.1) | async-done | bytes 327712 | tf_op jit(solution)/shard_map/all_to_all | solution.py:63
  139.0 0.8 fusion.9
  139.8 0.6 fusion.39
  140.4 0.6 slice_add_fusion
  (30 shorter events, 0.7 us)
Async XLA Ops:
  16.5 7.5 %copy-start.1 = (f32[2,4,128,128]{3,2,1,0:T(8,128)S(1)}, f32[2,4,128,128]{3,2,1,0:T(8,128)}, u32[]{:S(2)}) copy-start(f32[2,4,128,128]{3,2,1,0:T(8,128)} %param.14) | copy-start | bytes 1572868
  16.5 7.5 %copy-start.3 = (f32[1,4,128,128]{3,2,1,0:T(8,128)S(1)}, f32[1,4,128,128]{3,2,1,0:T(8,128)}, u32[]{:S(2)}) copy-start(f32[1,4,128,128]{3,2,1,0:T(8,128)} %param.11) | copy-start | bytes 786436
  16.5 8.5 %copy-start.7 = (f32[1,32,128]{2,1,0:T(8,128)S(1)}, f32[1,32,128]{2,1,0:T(8,128)}, u32[]{:S(2)}) copy-start(f32[1,32,128]{2,1,0:T(8,128)} %param.12) | copy-start | bytes 49156
  16.5 8.5 %copy-start.8 = (f32[1,32,128]{2,1,0:T(8,128)S(1)}, f32[1,32,128]{2,1,0:T(8,128)}, u32[]{:S(2)}) copy-start(f32[1,32,128]{2,1,0:T(8,128)} %param.13) | copy-start | bytes 49156
  16.5 8.5 %copy-start.4 = (f32[2,32,128]{2,1,0:T(8,128)S(1)}, f32[2,32,128]{2,1,0:T(8,128)}, u32[]{:S(2)}) copy-start(f32[2,32,128]{2,1,0:T(8,128)} %param.15) | copy-start | bytes 98308
  16.6 8.5 %copy-start.5 = (f32[2,32,128]{2,1,0:T(8,128)S(1)}, f32[2,32,128]{2,1,0:T(8,128)}, u32[]{:S(2)}) copy-start(f32[2,32,128]{2,1,0:T(8,128)} %param.16) | copy-start | bytes 98308
  16.6 8.5 %copy-start.6 = (f32[2,32,128]{2,1,0:T(8,128)S(1)}, f32[2,32,128]{2,1,0:T(8,128)}, u32[]{:S(2)}) copy-start(f32[2,32,128]{2,1,0:T(8,128)} %param.17) | copy-start | bytes 98308
  16.6 100.7 %all-to-all-start = ((f32[8,4,2,128,128]{4,3,2,1,0:T(8,128)}), f32[8,4,2,128,128]{4,3,2,1,0:T(8,128)}, u32[]{:S(2)}, u32[]{:S(2)}) async-start(f32[8,4,2,128,128]{4,3,2,1,0:T(8,128)} %bitcast.134), calls=%async_computation | async-start | bytes 8388608 | tf_op jit(solution)/shard_map/all_to_all | solution.py:45
  24.0 32.5 %all-gather.2.cloned.1.call-start = ((), (), s32[]{:S(2)}) async-start(), calls=%async_computation.2 | async-start | bytes 3932160 | tf_op jit(solution)/shard_map/all_gather | solution.py:43
  125.5 7.2 %copy-start = (f32[4,128,128]{2,1,0:T(8,128)}, f32[4,128,128]{2,1,0:T(8,128)S(1)}, u32[]{:S(2)}) copy-start(f32[4,128,128]{2,1,0:T(8,128)S(1)} %convolution_negate_fusion.1) | copy-start | bytes 786436
  127.2 13.8 %copy-start.2 = (f32[2,4,128,128]{3,2,1,0:T(8,128)}, f32[2,4,128,128]{3,2,1,0:T(8,128)S(1)}, u32[]{:S(2)}) copy-start(f32[2,4,128,128]{3,2,1,0:T(8,128)S(1)} %convolution_negate_fusion) | copy-start | bytes 1572868
  128.8 10.2 %all-to-all-start.1 = ((f32[5,4,32,128]{3,2,0,1:T(8,128)}), f32[5,4,32,128]{3,2,0,1:T(8,128)S(1)}, u32[]{:S(2)}, u32[]{:S(2)}) async-start(f32[5,4,32,128]{3,2,0,1:T(8,128)} %pad_maximum_fusion.1), calls=%async_computation.1 | async-start | bytes 655360 | tf_op jit(solution)/shard_map/all_to_all | solution.py:63
Sparse Core Ops, SparseCore 0:
  26.4 30.0 all-gather.1

commit v2 on v1

v2 whole, which is shorter than its diff:
```python
import functools

import jax
import jax.numpy as jnp
from jax import lax
from jax.experimental import pallas as pl
from jax.experimental.pallas import tpu as pltpu
from jax.sharding import PartitionSpec as P

highest = lax.Precision.HIGHEST
VMEM = pl.BlockSpec(memory_space=pltpu.VMEM)
SMEM = pl.BlockSpec(memory_space=pltpu.SMEM)


def mm(spec, *operands, precision=highest):
    return jnp.einsum(spec, *operands, precision=precision)


def swap(array, row_bits, col_bits):
    rows, cols = lax.axis_size("row"), lax.axis_size("col")
    pairs = [
        (r * cols + c, (r ^ row_bits) * cols + (c ^ col_bits))
        for r in range(rows)
        for c in range(cols)
    ]
    return lax.ppermute(array, ("row", "col"), pairs)


def pick_kernel(plan, place, struct, ainv, *outs):
    width, tile_rows, tile_cols = plan
    row, col, base = place[0], place[1], place[2]
    members, slot_share, pair_width = outs[0].shape[:3]
    for member in range(members):
        for side, out in enumerate(outs):
            u = jnp.bitwise_xor(base, (1 - side) * members) + member
            for k in range(pair_width):
                at_col = struct[u, col * pair_width + k] - col * tile_cols
                for j in range(slot_share):
                    at_row = struct[u, row * slot_share + j] - row * tile_rows
                    out[member, j, k] = ainv[
                        pl.ds(pl.multiple_of(at_row * width, width), width),
                        pl.ds(pl.multiple_of(at_col * width, width), width),
                    ]


def split(value):
    top = value.astype(jnp.bfloat16)
    return top, (value - top.astype(jnp.float32)).astype(jnp.bfloat16)


def product_kernel(start, place, tiles, *refs):
    panels, out = refs[:-1], refs[-1]
    members, slot_share, pair_width, width, _ = tiles.shape
    count, halves = out.shape[0], panels[0].shape[0]
    lhs, rhs = [], []
    for member in range(members):
        at = jnp.bitwise_xor(place[0], member)
        for k in range(pair_width):
            lhs.append(jnp.concatenate([tiles[member, j, k] for j in range(slot_share)], axis=0))
            blocks = []
            for n in range(start, start + count):
                block = panels[0][0, n, k]
                for d in range(1, members):
                    block = jnp.where(at == d, panels[d // halves][d % halves, n, k], block)
                blocks.append(block)
            rhs.append(jnp.concatenate(blocks, axis=1))
    lhs_top, lhs_rest = split(jnp.concatenate(lhs, axis=1))
    rhs_top, rhs_rest = split(jnp.concatenate(rhs, axis=0))
    dot = functools.partial(jnp.dot, preferred_element_type=jnp.float32)
    total = dot(lhs_top, rhs_rest) + dot(lhs_rest, rhs_top) + dot(lhs_top, rhs_top)
    for n in range(count):
        for j in range(slot_share):
            out[n, j] = total[j * width : (j + 1) * width, n * width : (n + 1) * width]


def product(place, tiles, panels, start, stop):
    members, slot_share, pair_width, width, _ = tiles.shape
    count = stop - start
    flops = 6 * members * pair_width * slot_share * count * width**3
    return pl.pallas_call(
        functools.partial(product_kernel, start),
        out_shape=jax.ShapeDtypeStruct((count, slot_share, width, width), jnp.float32),
        in_specs=[SMEM] + [VMEM] * (1 + len(panels)),
        out_specs=VMEM,
        compiler_params=pltpu.CompilerParams(vmem_limit_bytes=40 * 2**20),
        cost_estimate=pl.CostEstimate(flops=flops, bytes_accessed=4 * 2**20, transcendentals=0),
    )(place, tiles, *panels)


def after(value, *earlier):
    return lax.optimization_barrier((value, *earlier))[0]


def on_device(
    ainv_top, par_struct, par_panel, par_linv, par_dinv, kid_panel, kid_upper, kid_linv, kid_dinv
):
    grid_rows, grid_cols = lax.axis_size("row"), lax.axis_size("col")
    my_row, my_col = lax.axis_index("row"), lax.axis_index("col")
    width = par_panel.shape[-1]
    band_rows = width // grid_rows
    slot_share = par_panel.shape[1]
    children = kid_panel.shape[0]
    pair_width = par_struct.shape[1] // grid_cols
    tile_rows = ainv_top.shape[0] // width
    tile_cols = ainv_top.shape[1] // width
    halves = grid_cols // grid_rows
    lows = grid_rows // 2
    far_bits = lows * halves
    my_high, my_lane = my_col // halves, my_col % halves
    top = my_row // lows
    match = top == my_high // lows

    def take(half):
        par = lax.dynamic_slice_in_dim(par_panel, half * pair_width, pair_width, 1)
        kid = lax.dynamic_slice_in_dim(kid_panel, half * pair_width, pair_width, 1)
        return jnp.concatenate([par, kid], axis=0)

    def gather(mine, theirs, *earlier):
        both = after(jnp.stack([mine, theirs]), *earlier)
        return [both] + [swap(both, d, 0) for d in range(1, lows)]

    sent, kept = take(1 - top), take(top)
    got = swap(sent, lows, 0)
    away, near = jnp.where(match, got, kept), jnp.where(match, kept, got)
    far = swap(away, 0, far_bits)
    near_other = swap(near, lows, 0)

    small = jnp.concatenate([par_linv, par_dinv, kid_upper, kid_linv, kid_dinv], axis=0)
    small_other = swap(after(small, got), lows, 0)
    far_other = swap(after(far, near_other, small_other), lows, 0)
    far_panels = gather(far, far_other)

    members = far_bits
    groups = [list(range(0, members)), list(range(members, 2 * members))]
    piece = jax.ShapeDtypeStruct((members, slot_share, pair_width, width, width), jnp.float32)
    far_tiles, near_tiles = pl.pallas_call(
        functools.partial(pick_kernel, (width, tile_rows, tile_cols)),
        out_shape=[piece] * 2,
        in_specs=[SMEM, SMEM, VMEM],
        out_specs=[VMEM] * 2,
        compiler_params=pltpu.CompilerParams(vmem_limit_bytes=24 * 2**20),
        cost_estimate=pl.CostEstimate(flops=0, bytes_accessed=6 * 2**20, transcendentals=0),
    )(jnp.stack([my_row, my_col, my_col // members * members]), par_struct, after(ainv_top, sent))
    far_tiles = lax.all_to_all(far_tiles, "col", 0, 0, axis_index_groups=groups, tiled=True)
    near_tiles = after(near_tiles, far_tiles, small_other)
    near_tiles = lax.all_to_all(near_tiles, "col", 0, 0, axis_index_groups=groups, tiled=True)

    place = ((my_row % lows) * halves + top).reshape(1)
    par_away = product(place, far_tiles, far_panels, 0, 1)
    par_back = swap(par_away, 0, far_bits)
    kid_back = swap(product(place, far_tiles, far_panels, 1, 1 + children), 0, far_bits)

    near_panels = gather(near, near_other, par_away)
    small, order, bit = jnp.stack([small, small_other]), [0, lows], lows // 2
    small = after(small, par_away)
    while bit:
        small = jnp.concatenate([small, swap(small, bit, 0)], axis=0)
        order += [d ^ bit for d in order]
        bit //= 2
    inverse = sorted(range(grid_rows), key=order.__getitem__)
    at = jnp.asarray(inverse)[jnp.arange(grid_rows) ^ my_row]
    small = small[at].swapaxes(0, 1).reshape(small.shape[1], width, width)

    sums = product(place, near_tiles, near_panels, 0, 1 + children)
    par_sum = sums[:1] + par_back
    kid_sum = sums[1:] + kid_back
    plinv, pdinv = small[0], small[1]
    kupper = small[2 : 2 + children]
    klinv = small[2 + children : 2 + 2 * children]
    kdinv = small[2 + 2 * children :]

    par_off = -mm("jab,bc->jac", par_sum[0], plinv)
    par_hat = mm("jab,bc->jac", par_panel[0], plinv)
    kid_hat = mm("njab,nbc->njac", kid_panel, klinv)
    kuphat = mm("nab,nbc->nac", kupper, klinv)
    kid_sum = kid_sum + mm("jab,nbc->njac", par_off, kupper)
    kid_off = -mm("njab,nbc->njac", kid_sum, klinv)

    diag_part = mm("jba,jbc->ac", par_hat, par_off)
    parent_part = mm("jba,njbc->nac", par_off, kid_hat)
    hat_part = mm("njba,njbc->nac", kid_hat, kid_off)
    inner = parent_part - mm("ab,nbc->nac", diag_part, kuphat)
    edge_part = mm("nba,nbc->nac", kuphat, inner) - hat_part
    terms = jnp.concatenate([diag_part[None], parent_part, edge_part], axis=0)
    terms = terms.reshape(1 + 2 * children, grid_rows, band_rows, width)
    sums = lax.dynamic_index_in_dim(terms, my_row, 1, keepdims=False)
    for d in range(1, grid_rows):
        sums += swap(lax.dynamic_index_in_dim(terms, my_row ^ d, 1, keepdims=False), d, 0)

    par_pivot = mm("ba,bc,cd->ad", plinv, pdinv, plinv)
    kid_pivot = mm("nba,nbc,ncd->nad", klinv, kdinv, klinv)
    kid_pivot = kid_pivot + mm("nba,bc,ncd->nad", kuphat, par_pivot, kuphat)
    start = my_row * band_rows
    par_diag = lax.dynamic_slice_in_dim(par_pivot, start, band_rows, 0) - sums[0]
    kid_par = -(sums[1 : 1 + children] + mm("ab,nbc->nac", par_diag, kuphat))
    kid_diag = lax.dynamic_slice_in_dim(kid_pivot, start, band_rows, 1) + sums[1 + children :]
    return par_off[None], par_diag[None], kid_off, kid_par, kid_diag


def solution(mesh):
    placed = (
        P("row", "col"),
        P(),
        P("col", "row", None, None),
        P("col", "row", None),
        P("col", "row", None),
        P("col", "row", None, None),
        P("col", "row", None),
        P("col", "row", None),
        P("col", "row", None),
    )
    return jax.shard_map(
        on_device,
        mesh=mesh,
        in_specs=placed,
        out_specs=(
            P("col", "row", None, None),
            P("col", "row", None),
            P("col", "row", None, None),
            P("col", "row", None),
            P("col", "row", None),
        ),
        check_vma=False,
    )
```

time: 148 us -> 123 us (0.83)
  waiting for transfers between devices: 89.2 us -> 61.3 us
  starting transfers between devices: 10.9 us -> 25.9 us
  between operations: 14.3 us -> 1.1 us
  Pallas kernels: 0 us -> 9.88 us
  blocking collectives: 7.2 us -> 0 us
  matrix products: 13.9 us -> 10.5 us
  other arithmetic: 4.55 us -> 7.01 us
  local copies, waits for them, and re-layouts: 7.82 us -> 6.26 us
    all_to_all x2, waiting for transfers between devices: 67 us -> 25.3 us  [the longest x1 25.3 us: on_device(): lax.all_to_all(near_tiles, 'col', 0, 0, axis_index_groups=groups, tiled=T...]
    ppermute x0 -> x13, waiting for transfers between devices: none -> 36.1 us  [swap(): return lax.ppermute(array, ('row', 'col'), pairs)]
    all_gather x1 -> x0, waiting for transfers between devices: 22.1 us -> none  [on_device(): every = lax.all_gather(panels, 'row', axis=1, tiled=True)]
    ppermute x0 -> x13, starting transfers between devices: none -> 13.7 us  [swap(): return lax.ppermute(array, ('row', 'col'), pairs)]
    pallas_call x0 -> x4, Pallas kernels: none -> 9.88 us  [the longest x3 8.72 us: product(): pl.pallas_call(functools.partial(product_kernel, start), out_shape=jax.Sh...]
    all_gather x1 -> x0, blocking collectives: 7.2 us -> none  [on_device(): small = lax.all_gather(small, 'row', axis=1, tiled=True)]
    reshape x2 -> x0, local copies, waits for them, and re-layouts: 4.78 us -> none  [on_device(): local_tiles = ainv_top.reshape(tile_rows, width, tile_cols, width)]
    dot_general x19 -> x18, matrix products: 13.9 us -> 10.5 us  [mm(): return jnp.einsum(spec, *operands, precision=precision)]
  transfers between devices with their start and end apart: 3 -> 15, of which waited for: 3 -> 7; matrix products, arithmetic and copies ran while one was open for 2% -> 11% of each run, Pallas kernels for 0% -> 7%
where the time goes in v2:
time: 123 us; the launch traced here: 122 us
  waiting for transfers between devices  61.3 us (50%)
  starting transfers between devices  25.9 us (21%)
  matrix products  10.5 us (9%)
  Pallas kernels  9.88 us (8%)
  other arithmetic  7.01 us (6%)
  local copies, waits for them, and re-layouts  6.26 us (5%)
    ppermute x13, waiting for transfers between devices, swap(): return lax.ppermute(array, ('row', 'col'), pairs)  36.1 us
    all_to_all x1, waiting for transfers between devices, on_device(): lax.all_to_all(near_tiles, 'col', 0, 0, axis_index_groups=groups, tiled=T...  25.3 us
    ppermute x13, starting transfers between devices, swap(): return lax.ppermute(array, ('row', 'col'), pairs)  13.7 us
    dot_general x18, matrix products, mm(): return jnp.einsum(spec, *operands, precision=precision)  10.5 us
    pallas_call x3, Pallas kernels, product(): pl.pallas_call(functools.partial(product_kernel, start), out_shape=jax.Sh...  8.72 us
    all_to_all x1, starting transfers between devices, on_device(): lax.all_to_all(near_tiles, 'col', 0, 0, axis_index_groups=groups, tiled=T...  6.88 us
    all_to_all x1, starting transfers between devices, on_device(): lax.all_to_all(far_tiles, 'col', 0, 0, axis_index_groups=groups, tiled=True)  5.36 us
    unnamed x32, local copies, waits for them, and re-layouts  2.73 us
  transfers between devices with their start and end apart: 15, of which 7 were waited for; matrix products, arithmetic and copies ran while one was open for 11% of the time, Pallas kernels for 7%

profile of v2, /device:TPU:0, one launch (start us, length us, event | category | flops | bytes accessed | tf_op | source)
XLA Modules:
  0.0 122.0 jit_solution(437003530683425374)
XLA Ops:
  0.7 1.1 constant_dynamic-slice_fusion.1
  1.8 1.1 constant_dynamic-slice_fusion
  3.0 1.2 shard_map.137
  4.2 1.3 %copy-done.1 = f32[4,4,2,128,128]{4,3,2,1,0:T(8,128)} copy-done((f32[4,4,2,128,128]{4,3,2,1,0:T(8,128)}, f32[4,4,2,128,128]{4,3,2,1,0:T(8,128)S(1)}, u32[]{:S(2)}) %copy-start.1) | copy-done | bytes 2097176
  5.5 1.3 %copy-done.2 = f32[4,4,2,128,128]{4,3,2,1,0:T(8,128)} copy-done((f32[4,4,2,128,128]{4,3,2,1,0:T(8,128)}, f32[4,4,2,128,128]{4,3,2,1,0:T(8,128)S(1)}, u32[]{:S(2)}) %copy-start.2) | copy-done | bytes 2097176
  6.9 5.4 %all-to-all-start = ((f32[4,4,2,128,128]{4,3,2,1,0:T(8,128)}), f32[4,4,2,128,128]{4,3,2,1,0:T(8,128)S(1)}, u32[]{:S(2)}, u32[]{:S(2)}) async-start(f32[4,4,2,128,128]{4,3,2,1,0:T(8,128)} %copy-done.2), calls=%async_computation | async-start | bytes 4194304 | tf_op jit(solution)/shard_map/all_to_all | solution.py:144
  12.3 1.5 %collective-permute-start = (f32[3,2,128,128]{3,2,1,0:T(8,128)S(1)}, f32[3,2,128,128]{3,2,1,0:T(8,128)}, u32[]{:S(2)}, u32[]{:S(2)}) collective-permute-start(f32[3,2,128,128]{3,2,1,0:T(8,128)S(1)} %pad_maximum_fusion.3), channel_id=1, source_target_pairs={{0,16},{1,17},{2,18},{3,19},{4,20},{5,21},{6,22},{7,23},{8,24},{9,... | collective-permute-start | bytes 1179656 | tf_op jit(solution)/shard_map/ppermute | solution.py:26
  13.8 9.1 %collective-permute-done = f32[3,2,128,128]{3,2,1,0:T(8,128)} collective-permute-done((f32[3,2,128,128]{3,2,1,0:T(8,128)S(1)}, f32[3,2,128,128]{3,2,1,0:T(8,128)}, u32[]{:S(2)}, u32[]{:S(2)}) %collective-permute-start) | collective-permute-done | bytes 393248 | tf_op jit(solution)/shard_map/ppermute | solution.py:26
  22.9 1.1 fusion.4
  24.0 2.8 %collective-permute-start.3 = (f32[3,2,128,128]{3,2,1,0:T(8,128)S(1)}, f32[3,2,128,128]{3,2,1,0:T(8,128)S(1)}, u32[]{:S(2)}, u32[]{:S(2)}) collective-permute-start(f32[3,2,128,128]{3,2,1,0:T(8,128)S(1)} %get-tuple-element.22), channel_id=1, source_target_pairs={{0,4},{1,5},{2,6},{3,7},{4,0},{5,1},{6,2},{7,3},{8,12},{9,13},{10,... | collective-permute-start | bytes 1179656 | tf_op jit(solution)/shard_map/ppermute | solution.py:26
  26.8 1.5 %collective-permute-start.2 = (f32[3,2,128,128]{3,2,1,0:T(8,128)S(1)}, f32[3,2,128,128]{3,2,1,0:T(8,128)}, u32[]{:S(2)}, u32[]{:S(2)}) collective-permute-start(f32[3,2,128,128]{3,2,1,0:T(8,128)S(1)} %get-tuple-element.21), channel_id=1, source_target_pairs={{0,16},{1,17},{2,18},{3,19},{4,20},{5,21},{6,22},{7,23},{8,24},{9,... | collective-permute-start | bytes 1179656 | tf_op jit(solution)/shard_map/ppermute | solution.py:26
  29.0 10.3 %collective-permute-done.1 = f32[8,32,128]{2,1,0:T(8,128)S(1)} collective-permute-done((f32[8,32,128]{2,1,0:T(8,128)S(1)}, f32[8,32,128]{2,1,0:T(8,128)S(1)}, u32[]{:S(2)}, u32[]{:S(2)}) %collective-permute-start.1) | collective-permute-done | bytes 131104 | tf_op jit(solution)/shard_map/ppermute | solution.py:26
  39.2 4.1 %collective-permute-done.3 = f32[3,2,128,128]{3,2,1,0:T(8,128)S(1)} collective-permute-done((f32[3,2,128,128]{3,2,1,0:T(8,128)S(1)}, f32[3,2,128,128]{3,2,1,0:T(8,128)S(1)}, u32[]{:S(2)}, u32[]{:S(2)}) %collective-permute-start.3) | collective-permute-done | bytes 393248 | tf_op jit(solution)/shard_map/ppermute | solution.py:26
  43.4 1.6 %collective-permute-start.4 = (f32[3,2,128,128]{3,2,1,0:T(8,128)S(1)}, f32[3,2,128,128]{3,2,1,0:T(8,128)S(1)}, u32[]{:S(2)}, u32[]{:S(2)}) collective-permute-start(f32[3,2,128,128]{3,2,1,0:T(8,128)S(1)} %collective-permute-done.3), channel_id=1, source_target_pairs={{0,16},{1,17},{2,18},{3,19},{4,20},{5,21},{6,22},{7,23},{8,24},{9,... | collective-permute-start | bytes 1179656 | tf_op jit(solution)/shard_map/ppermute | solution.py:26
  45.0 8.4 %collective-permute-done.4 = f32[3,2,128,128]{3,2,1,0:T(8,128)S(1)} collective-permute-done((f32[3,2,128,128]{3,2,1,0:T(8,128)S(1)}, f32[3,2,128,128]{3,2,1,0:T(8,128)S(1)}, u32[]{:S(2)}, u32[]{:S(2)}) %collective-permute-start.4) | collective-permute-done | bytes 393248 | tf_op jit(solution)/shard_map/ppermute | solution.py:26
  53.5 6.9 %all-to-all-start.1 = ((f32[4,4,2,128,128]{4,3,2,1,0:T(8,128)}), f32[4,4,2,128,128]{4,3,2,1,0:T(8,128)}, u32[]{:S(2)}, u32[]{:S(2)}) async-start(f32[4,4,2,128,128]{4,3,2,1,0:T(8,128)} %copy-done.1), calls=%async_computation.1 | async-start | bytes 4194304 | tf_op jit(solution)/shard_map/all_to_all | solution.py:146
  61.8 2.8 %shard_map.138 = f32[1,4,128,128]{3,2,1,0:T(8,128)} custom-call(s32[1]{0:T(128)} %bitcast.place, f32[4,4,2,128,128]{4,3,2,1,0:T(8,128)S(1)} %all-to-all-done.tiles, f32[2,3,2,128,128]{4,3,2,1,0:T(8,128)S(1)} %pad_maximum_fusion.1.refs_0_, f32[2,3,2,128,128]{4,3,2,1,0:T(8,128)} %collective-permute-done.5.refs_1_), custom_call_target="tpu_custom_call" | custom-call | flops 402653184 | bytes 4194304 | tf_op jit(solution)/shard_map/pallas_call | solution.py:80
  64.9 1.9 %pad_maximum_fusion.refs_0_ = f32[2,3,2,128,128]{4,3,2,1,0:T(8,128)} fusion(f32[1,3,2,128,128]{4,3,2,1,0:T(8,128)} %bitcast.5, f32[1,3,2,128,128]{4,3,2,1,0:T(8,128)S(1)} %bitcast.155), kind=kLoop, calls=%fused_computation.13 | loop fusion | flops 196608 | bytes 1572864 | tf_op jit(solution)/shard_map/stack | solution.py:119
  66.9 1.3 %collective-permute-start.7 = (f32[1,4,128,128]{3,2,1,0:T(8,128)}, f32[1,4,128,128]{3,2,1,0:T(8,128)}, u32[]{:S(2)}, u32[]{:S(2)}) collective-permute-start(f32[1,4,128,128]{3,2,1,0:T(8,128)} %shard_map.138), channel_id=1, source_target_pairs={{0,4},{1,5},{2,6},{3,7},{4,0},{5,1},{6,2},{7,3},{8,12},{9,13},{10,... | collective-permute-start | bytes 786440 | tf_op jit(solution)/shard_map/ppermute | solution.py:26
  68.2 2.2 %shard_map.140 = f32[2,4,128,128]{3,2,1,0:T(8,128)S(1)} custom-call(s32[1]{0:T(128)} %bitcast.place, f32[4,4,2,128,128]{4,3,2,1,0:T(8,128)S(1)} %all-to-all-done.tiles, f32[2,3,2,128,128]{4,3,2,1,0:T(8,128)S(1)} %pad_maximum_fusion.1.refs_0_, f32[2,3,2,128,128]{4,3,2,1,0:T(8,128)} %collective-permute-done.5.refs_1_), custom_call_target="tpu_custom_call" | custom-call | flops 805306368 | bytes 4194304 | tf_op jit(solution)/shard_map/pallas_call | solution.py:80
  70.4 1.7 %collective-permute-start.9 = (f32[2,4,128,128]{3,2,1,0:T(8,128)S(1)}, f32[2,4,128,128]{3,2,1,0:T(8,128)}, u32[]{:S(2)}, u32[]{:S(2)}) collective-permute-start(f32[2,4,128,128]{3,2,1,0:T(8,128)S(1)} %shard_map.140), channel_id=1, source_target_pairs={{0,4},{1,5},{2,6},{3,7},{4,0},{5,1},{6,2},{7,3},{8,12},{9,13},{10,... | collective-permute-start | bytes 1572872 | tf_op jit(solution)/shard_map/ppermute | solution.py:26
  72.1 1.1 pad_maximum_fusion.2
  74.5 0.9 fusion.32
  77.6 25.3 %all-to-all-done.1.tiles = f32[4,4,2,128,128]{4,3,2,1,0:T(8,128)} async-done(((f32[4,4,2,128,128]{4,3,2,1,0:T(8,128)}), f32[4,4,2,128,128]{4,3,2,1,0:T(8,128)}, u32[]{:S(2)}, u32[]{:S(2)}) %all-to-all-start.1) | async-done | bytes 2097184 | tf_op jit(solution)/shard_map/all_to_all | solution.py:146
  102.8 3.7 %shard_map.139 = f32[3,4,128,128]{3,2,1,0:T(8,128)S(1)} custom-call(s32[1]{0:T(128)} %bitcast.place, f32[4,4,2,128,128]{4,3,2,1,0:T(8,128)} %all-to-all-done.1.tiles, f32[2,3,2,128,128]{4,3,2,1,0:T(8,128)} %pad_maximum_fusion.refs_0_, f32[2,3,2,128,128]{4,3,2,1,0:T(8,128)S(1)} %collective-permute-done.6.refs_1_), custom_call_target="tpu_custom_call" | custom-call | flops 1207959552 | bytes 4194304 | tf_op jit(solution)/shard_map/pallas_call | solution.py:80
  106.5 1.3 %convolution_negate_fusion.1 = f32[4,128,128]{2,1,0:T(8,128)S(1)} fusion(f32[128,128,1]{1,0,2:T(8,128)S(1)} %bitcast.161, f32[1,4,128,128]{3,2,1,0:T(8,128)} %collective-permute-done.7, f32[3,4,128,128]{3,2,1,0:T(8,128)S(1)} %shard_map.139), kind=kOutput, calls=%fused_computation.6 | convolution fusion | flops 100794368 | bytes 851968 | tf_op jit(solution)/shard_map/jab,bc->jac/dot_general | solution.py:16
  109.5 1.7 %convolution_negate_fusion = f32[2,4,128,128]{3,2,1,0:T(8,128)S(1)} fusion(f32[2,128,128,1]{2,1,3,0:T(8,128)S(1)} %bitcast.150, f32[2,4,128,128]{3,2,1,0:T(8,128)S(1)} %convolution_bitcast_fusion, f32[2,4,128,128]{3,2,1,0:T(8,128)} %collective-permute-done.9, f32[3,4,128,128]{3,2,1,0:T(8,128)S(1)} %shard_map.139), kind=kOutput, calls=%fused_computation.2 | convolution fusion | flops 201719808 | bytes 2228224 | tf_op jit(solution)/shard_map/njab,nbc->njac/dot_general | solution.py:16
  112.6 1.8 %collective-permute-start.12 = (f32[5,32,128]{2,1,0:T(8,128)S(1)}, f32[5,32,128]{2,1,0:T(8,128)S(1)}, u32[]{:S(2)}, u32[]{:S(2)}) collective-permute-start(f32[5,32,128]{2,1,0:T(8,128)S(1)} %get-tuple-element.29), channel_id=1, source_target_pairs={{0,24},{1,25},{2,26},{3,27},{4,28},{5,29},{6,30},{7,31},{8,16},{9,... | collective-permute-start | bytes 245768 | tf_op jit(solution)/shard_map/ppermute | solution.py:26
  115.0 2.2 %collective-permute-done.12 = f32[5,32,128]{2,1,0:T(8,128)S(1)} collective-permute-done((f32[5,32,128]{2,1,0:T(8,128)S(1)}, f32[5,32,128]{2,1,0:T(8,128)S(1)}, u32[]{:S(2)}, u32[]{:S(2)}) %collective-permute-start.12) | collective-permute-done | bytes 81952 | tf_op jit(solution)/shard_map/ppermute | solution.py:26
  117.2 2.0 %collective-permute-done.11 = f32[5,32,128]{2,1,0:T(8,128)S(1)} collective-permute-done((f32[5,32,128]{2,1,0:T(8,128)S(1)}, f32[5,32,128]{2,1,0:T(8,128)S(1)}, u32[]{:S(2)}, u32[]{:S(2)}) %collective-permute-start.11) | collective-permute-done | bytes 81952 | tf_op jit(solution)/shard_map/ppermute | solution.py:26
  119.2 0.8 fusion.16
  120.7 1.4 %slice_add_fusion.2 = f32[2,32,128]{2,1,0:T(8,128)} fusion(f32[5,32,128]{2,1,0:T(8,128)S(1)} %fusion.12, f32[2,128,128]{2,1,0:T(8,128)S(1)} %fusion.33, s32[]{:T(128)S(6)} %select_n.89, f32[2,128,128]{2,1,0:T(8,128)} %fusion.32), kind=kLoop, calls=%fused_computation.41 | loop fusion | flops 16384 | bytes 131076 | tf_op jit(solution)/shard_map/add | solution.py:196
  (76 shorter events, 10.1 us)
Async XLA Ops:
  0.6 2.4 %copy-start = (f32[1024,512]{1,0:T(8,128)S(1)}, f32[1024,512]{1,0:T(8,128)}, u32[]{:S(2)}) copy-start(f32[1024,512]{1,0:T(8,128)} %ainv) | copy-start | bytes 6291460
  0.6 2.4 %copy-start.3 = (s32[8,16]{1,0:T(8,128)S(1)}, s32[8,16]{1,0:T(8,128)}, u32[]{:S(2)}) copy-start(s32[8,16]{1,0:T(8,128)} %struct.1) | copy-start | bytes 1540
  4.2 1.3 %copy-start.1 = (f32[4,4,2,128,128]{4,3,2,1,0:T(8,128)}, f32[4,4,2,128,128]{4,3,2,1,0:T(8,128)S(1)}, u32[]{:S(2)}) copy-start(f32[4,4,2,128,128]{4,3,2,1,0:T(8,128)S(1)} %get-tuple-element.17) | copy-start | bytes 6291460
  5.5 1.3 %copy-start.2 = (f32[4,4,2,128,128]{4,3,2,1,0:T(8,128)}, f32[4,4,2,128,128]{4,3,2,1,0:T(8,128)S(1)}, u32[]{:S(2)}) copy-start(f32[4,4,2,128,128]{4,3,2,1,0:T(8,128)S(1)} %get-tuple-element.15) | copy-start | bytes 6291460
  6.9 6.9 %copy-start.12 = (f32[1,32,128]{2,1,0:T(8,128)S(1)}, f32[1,32,128]{2,1,0:T(8,128)}, u32[]{:S(2)}) copy-start(f32[1,32,128]{2,1,0:T(8,128)} %param.13) | copy-start | bytes 49156
  6.9 6.9 %copy-start.13 = (f32[1,32,128]{2,1,0:T(8,128)S(1)}, f32[1,32,128]{2,1,0:T(8,128)}, u32[]{:S(2)}) copy-start(f32[1,32,128]{2,1,0:T(8,128)} %param.14) | copy-start | bytes 49156
  6.9 21.5 %copy-start.9 = (f32[2,32,128]{2,1,0:T(8,128)S(1)}, f32[2,32,128]{2,1,0:T(8,128)}, u32[]{:S(2)}) copy-start(f32[2,32,128]{2,1,0:T(8,128)} %param.16) | copy-start | bytes 98308
  6.9 21.5 %copy-start.10 = (f32[2,32,128]{2,1,0:T(8,128)S(1)}, f32[2,32,128]{2,1,0:T(8,128)}, u32[]{:S(2)}) copy-start(f32[2,32,128]{2,1,0:T(8,128)} %param.17) | copy-start | bytes 98308
  6.9 21.5 %copy-start.11 = (f32[2,32,128]{2,1,0:T(8,128)S(1)}, f32[2,32,128]{2,1,0:T(8,128)}, u32[]{:S(2)}) copy-start(f32[2,32,128]{2,1,0:T(8,128)} %param.18) | copy-start | bytes 98308
  6.9 46.6 %all-to-all-start = ((f32[4,4,2,128,128]{4,3,2,1,0:T(8,128)}), f32[4,4,2,128,128]{4,3,2,1,0:T(8,128)S(1)}, u32[]{:S(2)}, u32[]{:S(2)}) async-start(f32[4,4,2,128,128]{4,3,2,1,0:T(8,128)} %copy-done.2), calls=%async_computation | async-start | bytes 4194304 | tf_op jit(solution)/shard_map/all_to_all | solution.py:144
  12.3 10.7 %collective-permute-start = (f32[3,2,128,128]{3,2,1,0:T(8,128)S(1)}, f32[3,2,128,128]{3,2,1,0:T(8,128)}, u32[]{:S(2)}, u32[]{:S(2)}) collective-permute-start(f32[3,2,128,128]{3,2,1,0:T(8,128)S(1)} %pad_maximum_fusion.3), channel_id=1, source_target_pairs={{0,16},{1,17},{2,18},{3,19},{4,20},{5,21},{6,22},{7,23},{8,24},{9,... | collective-permute-start | bytes 1179656 | tf_op jit(solution)/shard_map/ppermute | solution.py:26
  24.0 19.4 %collective-permute-start.3 = (f32[3,2,128,128]{3,2,1,0:T(8,128)S(1)}, f32[3,2,128,128]{3,2,1,0:T(8,128)S(1)}, u32[]{:S(2)}, u32[]{:S(2)}) collective-permute-start(f32[3,2,128,128]{3,2,1,0:T(8,128)S(1)} %get-tuple-element.22), channel_id=1, source_target_pairs={{0,4},{1,5},{2,6},{3,7},{4,0},{5,1},{6,2},{7,3},{8,12},{9,13},{10,... | collective-permute-start | bytes 1179656 | tf_op jit(solution)/shard_map/ppermute | solution.py:26
  26.8 16.5 %collective-permute-start.2 = (f32[3,2,128,128]{3,2,1,0:T(8,128)S(1)}, f32[3,2,128,128]{3,2,1,0:T(8,128)}, u32[]{:S(2)}, u32[]{:S(2)}) collective-permute-start(f32[3,2,128,128]{3,2,1,0:T(8,128)S(1)} %get-tuple-element.21), channel_id=1, source_target_pairs={{0,16},{1,17},{2,18},{3,19},{4,20},{5,21},{6,22},{7,23},{8,24},{9,... | collective-permute-start | bytes 1179656 | tf_op jit(solution)/shard_map/ppermute | solution.py:26
  28.4 10.8 %collective-permute-start.1 = (f32[8,32,128]{2,1,0:T(8,128)S(1)}, f32[8,32,128]{2,1,0:T(8,128)S(1)}, u32[]{:S(2)}, u32[]{:S(2)}) collective-permute-start(f32[8,32,128]{2,1,0:T(8,128)S(1)} %constant_dynamic-update-slice_fusion), channel_id=1, source_target_pairs={{0,16},{1,17},{2,18},{3,19},{4,20},{5,21},{6,22},{7,23},{8,24},{9,... | collective-permute-start | bytes 393224 | tf_op jit(solution)/shard_map/ppermute | solution.py:26
  43.4 10.0 %collective-permute-start.4 = (f32[3,2,128,128]{3,2,1,0:T(8,128)S(1)}, f32[3,2,128,128]{3,2,1,0:T(8,128)S(1)}, u32[]{:S(2)}, u32[]{:S(2)}) collective-permute-start(f32[3,2,128,128]{3,2,1,0:T(8,128)S(1)} %collective-permute-done.3), channel_id=1, source_target_pairs={{0,16},{1,17},{2,18},{3,19},{4,20},{5,21},{6,22},{7,23},{8,24},{9,... | collective-permute-start | bytes 1179656 | tf_op jit(solution)/shard_map/ppermute | solution.py:26
  53.4 8.4 %collective-permute-start.5 = (f32[2,3,2,128,128]{4,3,2,1,0:T(8,128)S(1)}, f32[2,3,2,128,128]{4,3,2,1,0:T(8,128)}, u32[]{:S(2)}, u32[]{:S(2)}) collective-permute-start(f32[2,3,2,128,128]{4,3,2,1,0:T(8,128)S(1)} %pad_maximum_fusion.1.refs_0_), channel_id=1, source_target_pairs={{0,8},{1,9},{2,10},{3,11},{4,12},{5,13},{6,14},{7,15},{8,0},{9,1},... | collective-permute-start | bytes 2359304 | tf_op jit(solution)/shard_map/ppermute | solution.py:26
  53.5 6.9 %copy-start.4 = (s32[4]{0:T(128)S(1)}, s32[4]{0:T(128)}, u32[]{:S(2)}) copy-start(s32[4]{0:T(128)} %constant.78.clone) | copy-start | bytes 52
  53.5 49.3 %all-to-all-start.1 = ((f32[4,4,2,128,128]{4,3,2,1,0:T(8,128)}), f32[4,4,2,128,128]{4,3,2,1,0:T(8,128)}, u32[]{:S(2)}, u32[]{:S(2)}) async-start(f32[4,4,2,128,128]{4,3,2,1,0:T(8,128)} %copy-done.1), calls=%async_computation.1 | async-start | bytes 4194304 | tf_op jit(solution)/shard_map/all_to_all | solution.py:146
  64.6 7.5 %collective-permute-start.8 = (f32[2,8,32,128]{3,2,1,0:T(8,128)}, f32[2,8,32,128]{3,2,1,0:T(8,128)}, u32[]{:S(2)}, u32[]{:S(2)}) collective-permute-start(f32[2,8,32,128]{3,2,1,0:T(8,128)} %pad_maximum_fusion.6), channel_id=1, source_target_pairs={{0,8},{1,9},{2,10},{3,11},{4,12},{5,13},{6,14},{7,15},{8,0},{9,1},... | collective-permute-start | bytes 786440 | tf_op jit(solution)/shard_map/ppermute | solution.py:26
  66.9 39.6 %collective-permute-start.7 = (f32[1,4,128,128]{3,2,1,0:T(8,128)}, f32[1,4,128,128]{3,2,1,0:T(8,128)}, u32[]{:S(2)}, u32[]{:S(2)}) collective-permute-start(f32[1,4,128,128]{3,2,1,0:T(8,128)} %shard_map.138), channel_id=1, source_target_pairs={{0,4},{1,5},{2,6},{3,7},{4,0},{5,1},{6,2},{7,3},{8,12},{9,13},{10,... | collective-permute-start | bytes 786440 | tf_op jit(solution)/shard_map/ppermute | solution.py:26
  70.4 39.1 %collective-permute-start.9 = (f32[2,4,128,128]{3,2,1,0:T(8,128)S(1)}, f32[2,4,128,128]{3,2,1,0:T(8,128)}, u32[]{:S(2)}, u32[]{:S(2)}) collective-permute-start(f32[2,4,128,128]{3,2,1,0:T(8,128)S(1)} %shard_map.140), channel_id=1, source_target_pairs={{0,4},{1,5},{2,6},{3,7},{4,0},{5,1},{6,2},{7,3},{8,12},{9,13},{10,... | collective-permute-start | bytes 1572872 | tf_op jit(solution)/shard_map/ppermute | solution.py:26
  72.1 5.5 %collective-permute-start.6 = (f32[2,3,2,128,128]{4,3,2,1,0:T(8,128)}, f32[2,3,2,128,128]{4,3,2,1,0:T(8,128)S(1)}, u32[]{:S(2)}, u32[]{:S(2)}) collective-permute-start(f32[2,3,2,128,128]{4,3,2,1,0:T(8,128)} %pad_maximum_fusion.refs_0_), channel_id=1, source_target_pairs={{0,8},{1,9},{2,10},{3,11},{4,12},{5,13},{6,14},{7,15},{8,0},{9,1},... | collective-permute-start | bytes 2359304 | tf_op jit(solution)/shard_map/ppermute | solution.py:26
  73.2 2.9 %copy-start.8 = (f32[1,4,128,128]{3,2,1,0:T(8,128)S(1)}, f32[1,4,128,128]{3,2,1,0:T(8,128)}, u32[]{:S(2)}) copy-start(f32[1,4,128,128]{3,2,1,0:T(8,128)} %param.12) | copy-start | bytes 786436
  73.8 2.7 %copy-start.7 = (f32[2,4,128,128]{3,2,1,0:T(8,128)S(1)}, f32[2,4,128,128]{3,2,1,0:T(8,128)}, u32[]{:S(2)}) copy-start(f32[2,4,128,128]{3,2,1,0:T(8,128)} %param.15) | copy-start | bytes 1572868
  107.9 3.3 %copy-start.5 = (f32[4,128,128]{2,1,0:T(8,128)}, f32[4,128,128]{2,1,0:T(8,128)S(1)}, u32[]{:S(2)}) copy-start(f32[4,128,128]{2,1,0:T(8,128)S(1)} %convolution_negate_fusion.1) | copy-start | bytes 786436
  111.1 8.9 %copy-start.6 = (f32[2,4,128,128]{3,2,1,0:T(8,128)}, f32[2,4,128,128]{3,2,1,0:T(8,128)S(1)}, u32[]{:S(2)}) copy-start(f32[2,4,128,128]{3,2,1,0:T(8,128)S(1)} %convolution_negate_fusion) | copy-start | bytes 1572868
  112.5 2.5 %collective-permute-start.10 = (f32[5,32,128]{2,1,0:T(8,128)S(1)}, f32[5,32,128]{2,1,0:T(8,128)S(1)}, u32[]{:S(2)}, u32[]{:S(2)}) collective-permute-start(f32[5,32,128]{2,1,0:T(8,128)S(1)} %get-tuple-element.28), channel_id=1, source_target_pairs={{0,8},{1,9},{2,10},{3,11},{4,12},{5,13},{6,14},{7,15},{8,0},{9,1},... | collective-permute-start | bytes 245768 | tf_op jit(solution)/shard_map/ppermute | solution.py:26
  112.6 4.6 %collective-permute-start.12 = (f32[5,32,128]{2,1,0:T(8,128)S(1)}, f32[5,32,128]{2,1,0:T(8,128)S(1)}, u32[]{:S(2)}, u32[]{:S(2)}) collective-permute-start(f32[5,32,128]{2,1,0:T(8,128)S(1)} %get-tuple-element.29), channel_id=1, source_target_pairs={{0,24},{1,25},{2,26},{3,27},{4,28},{5,29},{6,30},{7,31},{8,16},{9,... | collective-permute-start | bytes 245768 | tf_op jit(solution)/shard_map/ppermute | solution.py:26
  114.5 4.7 %collective-permute-start.11 = (f32[5,32,128]{2,1,0:T(8,128)S(1)}, f32[5,32,128]{2,1,0:T(8,128)S(1)}, u32[]{:S(2)}, u32[]{:S(2)}) collective-permute-start(f32[5,32,128]{2,1,0:T(8,128)S(1)} %get-tuple-element.30), channel_id=1, source_target_pairs={{0,16},{1,17},{2,18},{3,19},{4,20},{5,21},{6,22},{7,23},{8,24},{9,... | collective-permute-start | bytes 245768 | tf_op jit(solution)/shard_map/ppermute | solution.py:26

commit v3 on v2

--- a/solution.py
+++ b/solution.py
@@ -48,43 +48,111 @@
     return top, (value - top.astype(jnp.float32)).astype(jnp.bfloat16)
 
 
-def product_kernel(start, place, tiles, *refs):
-    panels, out = refs[:-1], refs[-1]
+def product_kernel(plan, place, tiles, *refs):
+    start, first, count_panels = plan
+    panels, out = refs[:count_panels], refs[-1]
     members, slot_share, pair_width, width, _ = tiles.shape
-    count, halves = out.shape[0], panels[0].shape[0]
+    count = out.shape[0]
     lhs, rhs = [], []
-    for member in range(members):
-        at = jnp.bitwise_xor(place[0], member)
+    for i, panel in enumerate(panels):
+        at = jnp.bitwise_xor(place[0], first + i)
         for k in range(pair_width):
-            lhs.append(jnp.concatenate([tiles[member, j, k] for j in range(slot_share)], axis=0))
-            blocks = []
-            for n in range(start, start + count):
-                block = panels[0][0, n, k]
-                for d in range(1, members):
-                    block = jnp.where(at == d, panels[d // halves][d % halves, n, k], block)
-                blocks.append(block)
+            lhs.append(jnp.concatenate([tiles[at, j, k] for j in range(slot_share)], axis=0))
+            blocks = [panel[n, k] for n in range(start, start + count)]
             rhs.append(jnp.concatenate(blocks, axis=1))
     lhs_top, lhs_rest = split(jnp.concatenate(lhs, axis=1))
     rhs_top, rhs_rest = split(jnp.concatenate(rhs, axis=0))
-    dot = functools.partial(jnp.dot, preferred_element_type=jnp.float32)
-    total = dot(lhs_top, rhs_rest) + dot(lhs_rest, rhs_top) + dot(lhs_top, rhs_top)
+    mul = functools.partial(jnp.dot, preferred_element_type=jnp.float32)
+    total = mul(lhs_top, rhs_rest) + mul(lhs_rest, rhs_top) + mul(lhs_top, rhs_top)
     for n in range(count):
         for j in range(slot_share):
-            out[n, j] = total[j * width : (j + 1) * width, n * width : (n + 1) * width]
-
-
-def product(place, tiles, panels, start, stop):
+            value = total[j * width : (j + 1) * width, n * width : (n + 1) * width]
+            if len(refs) > count_panels + 1:
+                value += refs[count_panels][start + n, j]
+            out[n, j] = value
+
+
+def product(place, tiles, panels, start, stop, first=0, so_far=()):
     members, slot_share, pair_width, width, _ = tiles.shape
     count = stop - start
-    flops = 6 * members * pair_width * slot_share * count * width**3
+    flops = 6 * len(panels) * pair_width * slot_share * count * width**3
     return pl.pallas_call(
-        functools.partial(product_kernel, start),
+        functools.partial(product_kernel, (start, first, len(panels))),
         out_shape=jax.ShapeDtypeStruct((count, slot_share, width, width), jnp.float32),
-        in_specs=[SMEM] + [VMEM] * (1 + len(panels)),
+        in_specs=[SMEM] + [VMEM] * (1 + len(panels) + len(so_far)),
         out_specs=VMEM,
         compiler_params=pltpu.CompilerParams(vmem_limit_bytes=40 * 2**20),
         cost_estimate=pl.CostEstimate(flops=flops, bytes_accessed=4 * 2**20, transcendentals=0),
-    )(place, tiles, *panels)
+    )(place, tiles, *panels, *so_far)
+
+
+def dot(a, b):
+    return jnp.dot(a, b, precision=highest, preferred_element_type=jnp.float32)
+
+
+def rows_of(ref, *at):
+    slots = ref.shape[-3]
+    return jnp.concatenate([ref[(*at, s)] for s in range(slots)], axis=0)
+
+
+def parent_kernel(near, back, linv, upper, uphat, par_hat, kid_hat, off, part, kid_sum):
+    slots, width = off.shape[1], off.shape[2]
+    kids = upper.shape[0]
+    value = -dot(rows_of(near, 0) + rows_of(back, 0), linv[...])
+    turned = value.T
+    diag = dot(rows_of(par_hat).T, value)
+    part[0] = diag
+    for s in range(slots):
+        off[0, s] = value[s * width : (s + 1) * width]
+    for c in range(kids):
+        cross = dot(turned, rows_of(kid_hat, c))
+        part[1 + c] = cross
+        part[1 + kids + c] = dot(uphat[c].T, cross - dot(diag, uphat[c]))
+        total = rows_of(near, 1 + c) + dot(value, upper[c])
+        for s in range(slots):
+            kid_sum[c, s] = total[s * width : (s + 1) * width]
+
+
+def kid_kernel(place, kid_sum, back, linv, kid_hat, part, off, *bands):
+    kids, slots, width, _ = off.shape
+    height = bands[0].shape[1]
+    bands, terms = bands[:-1], bands[-1]
+    terms[...] = part[...]
+    for c in range(kids):
+        value = -dot(rows_of(kid_sum, c) + rows_of(back, c), linv[c])
+        terms[1 + kids + c] = part[1 + kids + c] - dot(rows_of(kid_hat, c).T, value)
+        for s in range(slots):
+            off[c, s] = value[s * width : (s + 1) * width]
+    for d, band in enumerate(bands):
+        at = pl.multiple_of(jnp.bitwise_xor(place[0], d) * height, height)
+        for i in range(terms.shape[0]):
+            band[i] = terms[i, pl.ds(at, height), :]
+
+
+def band_kernel(par_pivot, kid_pivot, uphat, *refs):
+    bands, (par_diag, kid_par, kid_diag) = refs[:-3], refs[-3:]
+    kids = uphat.shape[0]
+
+    def total(i):
+        return functools.reduce(lambda a, b: a + b, [band[i] for band in bands])
+
+    diag = par_pivot[...] - total(0)
+    par_diag[0] = diag
+    for c in range(kids):
+        kid_par[c] = -(total(1 + c) + dot(diag, uphat[c]))
+        kid_diag[c] = kid_pivot[c] + total(1 + kids + c)
+
+
+def local(kernel, shapes, *operands, scalars=0, scratch=()):
+    return pl.pallas_call(
+        kernel,
+        out_shape=[jax.ShapeDtypeStruct(shape, jnp.float32) for shape in shapes],
+        in_specs=[SMEM] * scalars + [VMEM] * (len(operands) - scalars),
+        out_specs=[VMEM] * len(shapes),
+        scratch_shapes=[pltpu.VMEM(shape, jnp.float32) for shape in scratch],
+        compiler_params=pltpu.CompilerParams(vmem_limit_bytes=24 * 2**20),
+        cost_estimate=pl.CostEstimate(flops=10**8, bytes_accessed=2 * 2**20, transcendentals=0),
+    )(*operands)
 
 
 def after(value, *earlier):
@@ -116,8 +184,10 @@
         return jnp.concatenate([par, kid], axis=0)
 
     def gather(mine, theirs, *earlier):
-        both = after(jnp.stack([mine, theirs]), *earlier)
-        return [both] + [swap(both, d, 0) for d in range(1, lows)]
+        pieces = [mine, theirs]
+        return pieces + [
+            swap(after(piece, *earlier), d, 0) for d in range(1, lows) for piece in pieces
+        ]
 
     sent, kept = take(1 - top), take(top)
     got = swap(sent, lows, 0)
@@ -128,7 +198,6 @@
     small = jnp.concatenate([par_linv, par_dinv, kid_upper, kid_linv, kid_dinv], axis=0)
     small_other = swap(after(small, got), lows, 0)
     far_other = swap(after(far, near_other, small_other), lows, 0)
-    far_panels = gather(far, far_other)
 
     members = far_bits
     groups = [list(range(0, members)), list(range(members, 2 * members))]
@@ -146,13 +215,18 @@
     near_tiles = lax.all_to_all(near_tiles, "col", 0, 0, axis_index_groups=groups, tiled=True)
 
     place = ((my_row % lows) * halves + top).reshape(1)
-    par_away = product(place, far_tiles, far_panels, 0, 1)
+    so_far = [product(place, far_tiles, [far], 0, 1 + children)]
+    far_panels = gather(far, after(far_other, so_far[0]))
+    so_far = [product(place, far_tiles, far_panels[1:-1], 0, 1 + children, 1, so_far)]
+    last = (len(far_panels) - 1, so_far)
+    par_away = product(place, far_tiles, far_panels[-1:], 0, 1, *last)
     par_back = swap(par_away, 0, far_bits)
-    kid_back = swap(product(place, far_tiles, far_panels, 1, 1 + children), 0, far_bits)
-
-    near_panels = gather(near, near_other, par_away)
+    kid_away = product(place, far_tiles, far_panels[-1:], 1, 1 + children, *last)
+    kid_back = swap(kid_away, 0, far_bits)
+
+    near_panels = gather(near, near_other, kid_away)
     small, order, bit = jnp.stack([small, small_other]), [0, lows], lows // 2
-    small = after(small, par_away)
+    small = after(small, kid_away)
     while bit:
         small = jnp.concatenate([small, swap(small, bit, 0)], axis=0)
         order += [d ^ bit for d in order]
@@ -162,39 +236,41 @@
     small = small[at].swapaxes(0, 1).reshape(small.shape[1], width, width)
 
     sums = product(place, near_tiles, near_panels, 0, 1 + children)
-    par_sum = sums[:1] + par_back
-    kid_sum = sums[1:] + kid_back
     plinv, pdinv = small[0], small[1]
     kupper = small[2 : 2 + children]
     klinv = small[2 + children : 2 + 2 * children]
     kdinv = small[2 + 2 * children :]
 
-    par_off = -mm("jab,bc->jac", par_sum[0], plinv)
     par_hat = mm("jab,bc->jac", par_panel[0], plinv)
     kid_hat = mm("njab,nbc->njac", kid_panel, klinv)
     kuphat = mm("nab,nbc->nac", kupper, klinv)
-    kid_sum = kid_sum + mm("jab,nbc->njac", par_off, kupper)
-    kid_off = -mm("njab,nbc->njac", kid_sum, klinv)
-
-    diag_part = mm("jba,jbc->ac", par_hat, par_off)
-    parent_part = mm("jba,njbc->nac", par_off, kid_hat)
-    hat_part = mm("njba,njbc->nac", kid_hat, kid_off)
-    inner = parent_part - mm("ab,nbc->nac", diag_part, kuphat)
-    edge_part = mm("nba,nbc->nac", kuphat, inner) - hat_part
-    terms = jnp.concatenate([diag_part[None], parent_part, edge_part], axis=0)
-    terms = terms.reshape(1 + 2 * children, grid_rows, band_rows, width)
-    sums = lax.dynamic_index_in_dim(terms, my_row, 1, keepdims=False)
-    for d in range(1, grid_rows):
-        sums += swap(lax.dynamic_index_in_dim(terms, my_row ^ d, 1, keepdims=False), d, 0)
-
+    start = my_row * band_rows
     par_pivot = mm("ba,bc,cd->ad", plinv, pdinv, plinv)
     kid_pivot = mm("nba,nbc,ncd->nad", klinv, kdinv, klinv)
     kid_pivot = kid_pivot + mm("nba,bc,ncd->nad", kuphat, par_pivot, kuphat)
-    start = my_row * band_rows
-    par_diag = lax.dynamic_slice_in_dim(par_pivot, start, band_rows, 0) - sums[0]
-    kid_par = -(sums[1 : 1 + children] + mm("ab,nbc->nac", par_diag, kuphat))
-    kid_diag = lax.dynamic_slice_in_dim(kid_pivot, start, band_rows, 1) + sums[1 + children :]
-    return par_off[None], par_diag[None], kid_off, kid_par, kid_diag
+    par_pivot = lax.dynamic_slice_in_dim(par_pivot, start, band_rows, 0)
+    kid_pivot = lax.dynamic_slice_in_dim(kid_pivot, start, band_rows, 1)
+
+    terms = (1 + 2 * children, width, width)
+    par_off, part, kid_sum = local(
+        parent_kernel,
+        [par_panel.shape, terms, kid_panel.shape],
+        sums, par_back, plinv, kupper, kuphat, par_hat, kid_hat,
+    )
+    band = (1 + 2 * children, band_rows, width)
+    kid_off, *bands = local(
+        kid_kernel,
+        [kid_panel.shape] + [band] * grid_rows,
+        my_row.reshape(1), kid_sum, kid_back, klinv, kid_hat, part,
+        scalars=1,
+        scratch=[terms],
+    )
+    bands = [bands[0]] + [swap(bands[d], d, 0) for d in range(1, grid_rows)]
+    par_diag, kid_par, kid_diag = local(
+        band_kernel, [par_dinv.shape, kid_dinv.shape, kid_dinv.shape],
+        par_pivot, kid_pivot, kuphat, *bands,
+    )
+    return par_off, par_diag, kid_off, kid_par, kid_diag
 
 
 def solution(mesh):

time: 123 us -> 109 us (0.89)
  matrix products: 10.5 us -> 3.08 us
  other arithmetic: 7.01 us -> 1.04 us
  waiting for transfers between devices: 61.3 us -> 55.9 us
  Pallas kernels: 9.88 us -> 14.9 us
    ppermute x13 -> x15, waiting for transfers between devices: 36.1 us -> 28.2 us  [swap(): return lax.ppermute(array, ('row', 'col'), pairs)]
    dot_general x18 -> x9, matrix products: 10.5 us -> 3.08 us  [mm(): return jnp.einsum(spec, *operands, precision=precision)]
    pallas_call x3 -> x8, Pallas kernels: 8.72 us -> 13.7 us  [the longest x5 9.02 us: product(): pl.pallas_call(functools.partial(product_kernel, (start, first, len(panel...]
    another operation x2 -> x0, other arithmetic: 2 us -> none  [gather(): both = after(jnp.stack([mine, theirs]), *earlier)]
    all_to_all x1, waiting for transfers between devices: 25.3 us -> 27.2 us  [on_device(): lax.all_to_all(near_tiles, 'col', 0, 0, axis_index_groups=groups, tiled=T...]
    add x2 -> x1, other arithmetic: 1.4 us -> 0.02 us  [on_device(): kid_pivot = kid_pivot + mm('nba,bc,ncd->nad', kuphat, par_pivot, kuphat)]
    ppermute x13 -> x15, starting transfers between devices: 13.7 us -> 14.6 us  [swap(): return lax.ppermute(array, ('row', 'col'), pairs)]
    unnamed x32 -> x28, local copies, waits for them, and re-layouts: 2.73 us -> 2.75 us
  transfers between devices with their start and end apart: 15 -> 17, of which waited for: 7 -> 7; matrix products, arithmetic and copies ran while one was open for 11% -> 5% of each run, Pallas kernels for 7% -> 10%
where the time goes in v3:
time: 109 us
  waiting for transfers between devices  55.9 us (51%)
  starting transfers between devices  26.4 us (24%)
  Pallas kernels  14.9 us (14%)
  local copies, waits for them, and re-layouts  6.25 us (6%)
  matrix products  3.08 us (3%)
    ppermute x15, waiting for transfers between devices, swap(): return lax.ppermute(array, ('row', 'col'), pairs)  28.2 us
    all_to_all x1, waiting for transfers between devices, on_device(): lax.all_to_all(near_tiles, 'col', 0, 0, axis_index_groups=groups, tiled=T...  27.2 us
    ppermute x15, starting transfers between devices, swap(): return lax.ppermute(array, ('row', 'col'), pairs)  14.6 us
    pallas_call x5, Pallas kernels, product(): pl.pallas_call(functools.partial(product_kernel, (start, first, len(panel...  9.02 us
    all_to_all x1, starting transfers between devices, on_device(): lax.all_to_all(near_tiles, 'col', 0, 0, axis_index_groups=groups, tiled=T...  6.47 us
    all_to_all x1, starting transfers between devices, on_device(): lax.all_to_all(far_tiles, 'col', 0, 0, axis_index_groups=groups, tiled=True)  5.36 us
    pallas_call x3, Pallas kernels, local(): pl.pallas_call(kernel, out_shape=[jax.ShapeDtypeStruct(shape, jnp.float32...  4.67 us
    dot_general x9, matrix products, mm(): return jnp.einsum(spec, *operands, precision=precision)  3.08 us
  transfers between devices with their start and end apart: 17, of which 7 were waited for; matrix products, arithmetic and copies ran while one was open for 5% of the time, Pallas kernels for 10%

profile of v3, /device:TPU:0, one launch (start us, length us, event | category | flops | bytes accessed | tf_op | source)
XLA Modules:
  0.0 108.6 jit_solution(13093363253245744742)
XLA Ops:
  0.7 1.2 %constant_dynamic-slice_fusion.1 = (f32[2,2,128,128]{3,2,1,0:T(8,128)S(1)}, f32[2,2,128,128]{3,2,1,0:T(8,128)S(1)}) fusion(f32[2,4,128,128]{3,2,1,0:T(8,128)} %param.15, s32[]{:T(128)S(6)} %select_n.71, s32[]{:T(128)S(6)} %select_n.67), kind=kLoop, calls=%fused_computation.28 | loop fusion | bytes 1048584 | tf_op jit(solution)/shard_map/dynamic_slice | solution.py:183
  1.9 1.0 constant_dynamic-slice_fusion.2
  3.0 1.2 %shard_map.137 = (f32[4,4,2,128,128]{4,3,2,1,0:T(8,128)S(1)}, f32[4,4,2,128,128]{4,3,2,1,0:T(8,128)S(1)}) custom-call(s32[3]{0:T(128)S(1)} %pad_add_fusion.place, s32[8,16]{1,0:T(8,128)S(1)} %copy-done.3, f32[1024,512]{1,0:T(8,128)S(1)} %copy-done), custom_call_target="tpu_custom_call" | custom-call | bytes 6291456 | tf_op jit(solution)/shard_map/pallas_call | solution.py:205
  4.2 1.4 %copy-done.1 = f32[4,4,2,128,128]{4,3,2,1,0:T(8,128)} copy-done((f32[4,4,2,128,128]{4,3,2,1,0:T(8,128)}, f32[4,4,2,128,128]{4,3,2,1,0:T(8,128)S(1)}, u32[]{:S(2)}) %copy-start.1) | copy-done | bytes 2097176
  5.6 1.3 %copy-done.2 = f32[4,4,2,128,128]{4,3,2,1,0:T(8,128)} copy-done((f32[4,4,2,128,128]{4,3,2,1,0:T(8,128)}, f32[4,4,2,128,128]{4,3,2,1,0:T(8,128)S(1)}, u32[]{:S(2)}) %copy-start.2) | copy-done | bytes 2097176
  6.9 5.4 %all-to-all-start = ((f32[4,4,2,128,128]{4,3,2,1,0:T(8,128)}), f32[4,4,2,128,128]{4,3,2,1,0:T(8,128)S(1)}, u32[]{:S(2)}, u32[]{:S(2)}) async-start(f32[4,4,2,128,128]{4,3,2,1,0:T(8,128)} %copy-done.2), calls=%async_computation | async-start | bytes 4194304 | tf_op jit(solution)/shard_map/all_to_all | solution.py:213
  12.3 1.5 %collective-permute-start = (f32[3,2,128,128]{3,2,1,0:T(8,128)S(1)}, f32[3,2,128,128]{3,2,1,0:T(8,128)S(1)}, u32[]{:S(2)}, u32[]{:S(2)}) collective-permute-start(f32[3,2,128,128]{3,2,1,0:T(8,128)S(1)} %pad_maximum_fusion.1), channel_id=1, source_target_pairs={{0,16},{1,17},{2,18},{3,19},{4,20},{5,21},{6,22},{7,23},{8,24},{9,... | collective-permute-start | bytes 1179656 | tf_op jit(solution)/shard_map/ppermute | solution.py:26
  13.8 9.0 %collective-permute-done = f32[3,2,128,128]{3,2,1,0:T(8,128)S(1)} collective-permute-done((f32[3,2,128,128]{3,2,1,0:T(8,128)S(1)}, f32[3,2,128,128]{3,2,1,0:T(8,128)S(1)}, u32[]{:S(2)}, u32[]{:S(2)}) %collective-permute-start) | collective-permute-done | bytes 393248 | tf_op jit(solution)/shard_map/ppermute | solution.py:26
  22.9 0.8 fusion
  23.7 1.7 %collective-permute-start.2 = (f32[3,2,128,128]{3,2,1,0:T(8,128)}, f32[3,2,128,128]{3,2,1,0:T(8,128)}, u32[]{:S(2)}, u32[]{:S(2)}) collective-permute-start(f32[3,2,128,128]{3,2,1,0:T(8,128)} %get-tuple-element.33.refs_0_), channel_id=1, source_target_pairs={{0,16},{1,17},{2,18},{3,19},{4,20},{5,21},{6,22},{7,23},{8,24},{9,... | collective-permute-start | bytes 1179656 | tf_op jit(solution)/shard_map/ppermute | solution.py:26
  25.4 2.6 %collective-permute-start.3 = (f32[3,2,128,128]{3,2,1,0:T(8,128)S(1)}, f32[3,2,128,128]{3,2,1,0:T(8,128)}, u32[]{:S(2)}, u32[]{:S(2)}) collective-permute-start(f32[3,2,128,128]{3,2,1,0:T(8,128)S(1)} %get-tuple-element.47), channel_id=1, source_target_pairs={{0,4},{1,5},{2,6},{3,7},{4,0},{5,1},{6,2},{7,3},{8,12},{9,13},{10,... | collective-permute-start | bytes 1179656 | tf_op jit(solution)/shard_map/ppermute | solution.py:26
  28.6 7.9 %collective-permute-done.1 = f32[8,32,128]{2,1,0:T(8,128)S(1)} collective-permute-done((f32[8,32,128]{2,1,0:T(8,128)S(1)}, f32[8,32,128]{2,1,0:T(8,128)S(1)}, u32[]{:S(2)}, u32[]{:S(2)}) %collective-permute-start.1) | collective-permute-done | bytes 131104 | tf_op jit(solution)/shard_map/ppermute | solution.py:26
  36.6 6.8 %collective-permute-done.3.refs_0_ = f32[3,2,128,128]{3,2,1,0:T(8,128)} collective-permute-done((f32[3,2,128,128]{3,2,1,0:T(8,128)S(1)}, f32[3,2,128,128]{3,2,1,0:T(8,128)}, u32[]{:S(2)}, u32[]{:S(2)}) %collective-permute-start.3) | collective-permute-done | bytes 393248 | tf_op jit(solution)/shard_map/ppermute | solution.py:26
  43.4 1.6 %collective-permute-start.4 = (f32[3,2,128,128]{3,2,1,0:T(8,128)}, f32[3,2,128,128]{3,2,1,0:T(8,128)}, u32[]{:S(2)}, u32[]{:S(2)}) collective-permute-start(f32[3,2,128,128]{3,2,1,0:T(8,128)} %collective-permute-done.3.refs_0_), channel_id=1, source_target_pairs={{0,16},{1,17},{2,18},{3,19},{4,20},{5,21},{6,22},{7,23},{8,24},{9,... | collective-permute-start | bytes 1179656 | tf_op jit(solution)/shard_map/ppermute | solution.py:26
  45.0 0.6 all-to-all-done.tiles
  45.6 6.5 %all-to-all-start.1 = ((f32[4,4,2,128,128]{4,3,2,1,0:T(8,128)}), f32[4,4,2,128,128]{4,3,2,1,0:T(8,128)}, u32[]{:S(2)}, u32[]{:S(2)}) async-start(f32[4,4,2,128,128]{4,3,2,1,0:T(8,128)} %copy-done.1), calls=%async_computation.1 | async-start | bytes 4194304 | tf_op jit(solution)/shard_map/all_to_all | solution.py:215
  52.1 1.6 %shard_map.138.refs_2_ = f32[3,4,128,128]{3,2,1,0:T(8,128)S(1)} custom-call(s32[1]{0:T(128)} %bitcast.place, f32[4,4,2,128,128]{4,3,2,1,0:T(8,128)S(1)} %all-to-all-done.tiles, f32[3,2,128,128]{3,2,1,0:T(8,128)} %collective-permute-done.3.refs_0_), custom_call_target="tpu_custom_call" | custom-call | flops 301989888 | bytes 4194304 | tf_op jit(solution)/shard_map/pallas_call | solution.py:79
  54.0 0.6 gather_fusion
  54.7 2.1 %shard_map.139.refs_1_ = f32[3,4,128,128]{3,2,1,0:T(8,128)S(1)} custom-call(s32[1]{0:T(128)} %bitcast.place, f32[4,4,2,128,128]{4,3,2,1,0:T(8,128)S(1)} %all-to-all-done.tiles, f32[3,2,128,128]{3,2,1,0:T(8,128)} %collective-permute-done.4.refs_0_, f32[3,2,128,128]{3,2,1,0:T(8,128)} %collective-permute-done.6.refs_1_, f32[3,4,128,128]{3,2,1,0:T(8,128)S(1)} %shard_map.138.refs_2_), custom_call_target="tpu_custom_call" | custom-call | flops 603979776 | bytes 4194304 | tf_op jit(solution)/shard_map/pallas_call | solution.py:79
  56.8 1.2 %shard_map.140 = f32[2,4,128,128]{3,2,1,0:T(8,128)} custom-call(s32[1]{0:T(128)} %bitcast.place, f32[4,4,2,128,128]{4,3,2,1,0:T(8,128)S(1)} %all-to-all-done.tiles, f32[3,2,128,128]{3,2,1,0:T(8,128)S(1)} %collective-permute-done.5.refs_0_, f32[3,4,128,128]{3,2,1,0:T(8,128)S(1)} %shard_map.139.refs_1_), custom_call_target="tpu_custom_call" | custom-call | flops 201326592 | bytes 4194304 | tf_op jit(solution)/shard_map/pallas_call | solution.py:79
  58.3 3.5 %collective-permute-start.11 = (f32[2,4,128,128]{3,2,1,0:T(8,128)}, f32[2,4,128,128]{3,2,1,0:T(8,128)S(1)}, u32[]{:S(2)}, u32[]{:S(2)}) collective-permute-start(f32[2,4,128,128]{3,2,1,0:T(8,128)} %shard_map.140), channel_id=1, source_target_pairs={{0,4},{1,5},{2,6},{3,7},{4,0},{5,1},{6,2},{7,3},{8,12},{9,13},{10,... | collective-permute-start | bytes 1572872 | tf_op jit(solution)/shard_map/ppermute | solution.py:26
  62.8 0.6 gather_fusion.1
  65.5 0.6 convolution_bitcast_fusion.kid_hat
  66.8 27.2 %all-to-all-done.1.tiles = f32[4,4,2,128,128]{4,3,2,1,0:T(8,128)} async-done(((f32[4,4,2,128,128]{4,3,2,1,0:T(8,128)}), f32[4,4,2,128,128]{4,3,2,1,0:T(8,128)}, u32[]{:S(2)}, u32[]{:S(2)}) %all-to-all-start.1) | async-done | bytes 2097184 | tf_op jit(solution)/shard_map/all_to_all | solution.py:215
  93.9 3.8 %shard_map.141.near = f32[3,4,128,128]{3,2,1,0:T(8,128)S(1)} custom-call(s32[1]{0:T(128)} %bitcast.place, f32[4,4,2,128,128]{4,3,2,1,0:T(8,128)} %all-to-all-done.1.tiles, f32[3,2,128,128]{3,2,1,0:T(8,128)} %get-tuple-element.33.refs_0_, f32[3,2,128,128]{3,2,1,0:T(8,128)} %collective-permute-done.2.refs_1_, ...), custom_call_target="tpu_custom_call" | custom-call | flops 1207959552 | bytes 4194304 | tf_op jit(solution)/shard_map/pallas_call | solution.py:79
  97.7 2.0 %shard_map.143 = (f32[1,4,128,128]{3,2,1,0:T(8,128)}, f32[5,128,128]{2,1,0:T(8,128)S(1)}, f32[2,4,128,128]{3,2,1,0:T(8,128)S(1)}) custom-call(f32[3,4,128,128]{3,2,1,0:T(8,128)S(1)} %shard_map.141.near, f32[1,4,128,128]{3,2,1,0:T(8,128)S(1)} %collective-permute-done.9.back, f32[128,128]{1,0:T(8,128)S(1)} %bitcast.66, f32[2,128,128]{2,1,0:T(8,128)S(1)} %bitcast.63, ...), custom_call_target="tpu_custom_call" | custom-call | flops 100000000 | bytes 2097152 | tf_op jit(solution)/shard_map/pallas_call | solution.py:147
  99.8 1.8 %shard_map.144 = (f32[2,4,128,128]{3,2,1,0:T(8,128)}, f32[5,32,128]{2,1,0:T(8,128)S(1)}, f32[5,32,128]{2,1,0:T(8,128)S(1)}, f32[5,32,128]{2,1,0:T(8,128)S(1)}, f32[5,32,128]{2,1,0:T(8,128)S(1)}) custom-call(s32[1]{0:T(128)} %bitcast.1.place, f32[2,4,128,128]{3,2,1,0:T(8,128)S(1)} %get-tuple-element.37.kid_sum, ...), custom_call_target="tpu_custom_call" | custom-call | flops 100000000 | bytes 2097152 | tf_op jit(solution)/shard_map/pallas_call | solution.py:147
  101.5 0.6 collective-permute-start.13
  102.1 1.2 %collective-permute-start.14 = (f32[5,32,128]{2,1,0:T(8,128)S(1)}, f32[5,32,128]{2,1,0:T(8,128)S(1)}, u32[]{:S(2)}, u32[]{:S(2)}) collective-permute-start(f32[5,32,128]{2,1,0:T(8,128)S(1)} %get-tuple-element.42), channel_id=1, source_target_pairs={{0,24},{1,25},{2,26},{3,27},{4,28},{5,29},{6,30},{7,31},{8,16},{9,... | collective-permute-start | bytes 245768 | tf_op jit(solution)/shard_map/ppermute | solution.py:26
  103.4 3.4 %collective-permute-done.13.refs_2_ = f32[5,32,128]{2,1,0:T(8,128)S(1)} collective-permute-done((f32[5,32,128]{2,1,0:T(8,128)S(1)}, f32[5,32,128]{2,1,0:T(8,128)S(1)}, u32[]{:S(2)}, u32[]{:S(2)}) %collective-permute-start.13) | collective-permute-done | bytes 81952 | tf_op jit(solution)/shard_map/ppermute | solution.py:26
  106.8 1.0 collective-permute-done.14.refs_3_
  107.7 0.9 shard_map.145
  (67 shorter events, 5.1 us)
Async XLA Ops:
  0.6 2.4 %copy-start = (f32[1024,512]{1,0:T(8,128)S(1)}, f32[1024,512]{1,0:T(8,128)}, u32[]{:S(2)}) copy-start(f32[1024,512]{1,0:T(8,128)} %ainv) | copy-start | bytes 6291460
  0.6 2.4 %copy-start.3 = (s32[8,16]{1,0:T(8,128)S(1)}, s32[8,16]{1,0:T(8,128)}, u32[]{:S(2)}) copy-start(s32[8,16]{1,0:T(8,128)} %struct.1) | copy-start | bytes 1540
  4.2 1.4 %copy-start.1 = (f32[4,4,2,128,128]{4,3,2,1,0:T(8,128)}, f32[4,4,2,128,128]{4,3,2,1,0:T(8,128)S(1)}, u32[]{:S(2)}) copy-start(f32[4,4,2,128,128]{4,3,2,1,0:T(8,128)S(1)} %get-tuple-element.30) | copy-start | bytes 6291460
  5.6 1.3 %copy-start.2 = (f32[4,4,2,128,128]{4,3,2,1,0:T(8,128)}, f32[4,4,2,128,128]{4,3,2,1,0:T(8,128)S(1)}, u32[]{:S(2)}) copy-start(f32[4,4,2,128,128]{4,3,2,1,0:T(8,128)S(1)} %get-tuple-element.28) | copy-start | bytes 6291460
  6.9 6.9 %copy-start.10 = (f32[1,32,128]{2,1,0:T(8,128)S(1)}, f32[1,32,128]{2,1,0:T(8,128)}, u32[]{:S(2)}) copy-start(f32[1,32,128]{2,1,0:T(8,128)} %param.13) | copy-start | bytes 49156
  6.9 6.9 %copy-start.11 = (f32[1,32,128]{2,1,0:T(8,128)S(1)}, f32[1,32,128]{2,1,0:T(8,128)}, u32[]{:S(2)}) copy-start(f32[1,32,128]{2,1,0:T(8,128)} %param.14) | copy-start | bytes 49156
  6.9 21.1 %copy-start.7 = (f32[2,32,128]{2,1,0:T(8,128)S(1)}, f32[2,32,128]{2,1,0:T(8,128)}, u32[]{:S(2)}) copy-start(f32[2,32,128]{2,1,0:T(8,128)} %param.16) | copy-start | bytes 98308
  6.9 21.1 %copy-start.8 = (f32[2,32,128]{2,1,0:T(8,128)S(1)}, f32[2,32,128]{2,1,0:T(8,128)}, u32[]{:S(2)}) copy-start(f32[2,32,128]{2,1,0:T(8,128)} %param.17) | copy-start | bytes 98308
  6.9 21.1 %copy-start.9 = (f32[2,32,128]{2,1,0:T(8,128)S(1)}, f32[2,32,128]{2,1,0:T(8,128)}, u32[]{:S(2)}) copy-start(f32[2,32,128]{2,1,0:T(8,128)} %param.18) | copy-start | bytes 98308
  6.9 38.7 %all-to-all-start = ((f32[4,4,2,128,128]{4,3,2,1,0:T(8,128)}), f32[4,4,2,128,128]{4,3,2,1,0:T(8,128)S(1)}, u32[]{:S(2)}, u32[]{:S(2)}) async-start(f32[4,4,2,128,128]{4,3,2,1,0:T(8,128)} %copy-done.2), calls=%async_computation | async-start | bytes 4194304 | tf_op jit(solution)/shard_map/all_to_all | solution.py:213
  12.3 10.6 %collective-permute-start = (f32[3,2,128,128]{3,2,1,0:T(8,128)S(1)}, f32[3,2,128,128]{3,2,1,0:T(8,128)S(1)}, u32[]{:S(2)}, u32[]{:S(2)}) collective-permute-start(f32[3,2,128,128]{3,2,1,0:T(8,128)S(1)} %pad_maximum_fusion.1), channel_id=1, source_target_pairs={{0,16},{1,17},{2,18},{3,19},{4,20},{5,21},{6,22},{7,23},{8,24},{9,... | collective-permute-start | bytes 1179656 | tf_op jit(solution)/shard_map/ppermute | solution.py:26
  23.7 12.9 %collective-permute-start.2 = (f32[3,2,128,128]{3,2,1,0:T(8,128)}, f32[3,2,128,128]{3,2,1,0:T(8,128)}, u32[]{:S(2)}, u32[]{:S(2)}) collective-permute-start(f32[3,2,128,128]{3,2,1,0:T(8,128)} %get-tuple-element.33.refs_0_), channel_id=1, source_target_pairs={{0,16},{1,17},{2,18},{3,19},{4,20},{5,21},{6,22},{7,23},{8,24},{9,... | collective-permute-start | bytes 1179656 | tf_op jit(solution)/shard_map/ppermute | solution.py:26
  25.4 18.0 %collective-permute-start.3 = (f32[3,2,128,128]{3,2,1,0:T(8,128)S(1)}, f32[3,2,128,128]{3,2,1,0:T(8,128)}, u32[]{:S(2)}, u32[]{:S(2)}) collective-permute-start(f32[3,2,128,128]{3,2,1,0:T(8,128)S(1)} %get-tuple-element.47), channel_id=1, source_target_pairs={{0,4},{1,5},{2,6},{3,7},{4,0},{5,1},{6,2},{7,3},{8,12},{9,13},{10,... | collective-permute-start | bytes 1179656 | tf_op jit(solution)/shard_map/ppermute | solution.py:26
  28.0 8.5 %collective-permute-start.1 = (f32[8,32,128]{2,1,0:T(8,128)S(1)}, f32[8,32,128]{2,1,0:T(8,128)S(1)}, u32[]{:S(2)}, u32[]{:S(2)}) collective-permute-start(f32[8,32,128]{2,1,0:T(8,128)S(1)} %constant_dynamic-update-slice_fusion), channel_id=1, source_target_pairs={{0,16},{1,17},{2,18},{3,19},{4,20},{5,21},{6,22},{7,23},{8,24},{9,... | collective-permute-start | bytes 393224 | tf_op jit(solution)/shard_map/ppermute | solution.py:26
  43.4 10.3 %collective-permute-start.4 = (f32[3,2,128,128]{3,2,1,0:T(8,128)}, f32[3,2,128,128]{3,2,1,0:T(8,128)}, u32[]{:S(2)}, u32[]{:S(2)}) collective-permute-start(f32[3,2,128,128]{3,2,1,0:T(8,128)} %collective-permute-done.3.refs_0_), channel_id=1, source_target_pairs={{0,16},{1,17},{2,18},{3,19},{4,20},{5,21},{6,22},{7,23},{8,24},{9,... | collective-permute-start | bytes 1179656 | tf_op jit(solution)/shard_map/ppermute | solution.py:26
  45.0 9.6 %collective-permute-start.6 = (f32[3,2,128,128]{3,2,1,0:T(8,128)}, f32[3,2,128,128]{3,2,1,0:T(8,128)}, u32[]{:S(2)}, u32[]{:S(2)}) collective-permute-start(f32[3,2,128,128]{3,2,1,0:T(8,128)} %collective-permute-done.3.refs_0_), channel_id=1, source_target_pairs={{0,8},{1,9},{2,10},{3,11},{4,12},{5,13},{6,14},{7,15},{8,0},{9,1},... | collective-permute-start | bytes 1179656 | tf_op jit(solution)/shard_map/ppermute | solution.py:26
  45.6 48.3 %all-to-all-start.1 = ((f32[4,4,2,128,128]{4,3,2,1,0:T(8,128)}), f32[4,4,2,128,128]{4,3,2,1,0:T(8,128)}, u32[]{:S(2)}, u32[]{:S(2)}) async-start(f32[4,4,2,128,128]{4,3,2,1,0:T(8,128)} %copy-done.1), calls=%async_computation.1 | async-start | bytes 4194304 | tf_op jit(solution)/shard_map/all_to_all | solution.py:215
  52.1 1.9 %copy-start.4 = (s32[4]{0:T(128)S(1)}, s32[4]{0:T(128)}, u32[]{:S(2)}) copy-start(s32[4]{0:T(128)} %constant.67.clone) | copy-start | bytes 52
  53.7 3.1 %collective-permute-start.5 = (f32[3,2,128,128]{3,2,1,0:T(8,128)}, f32[3,2,128,128]{3,2,1,0:T(8,128)S(1)}, u32[]{:S(2)}, u32[]{:S(2)}) collective-permute-start(f32[3,2,128,128]{3,2,1,0:T(8,128)} %collective-permute-done.4.refs_0_), channel_id=1, source_target_pairs={{0,8},{1,9},{2,10},{3,11},{4,12},{5,13},{6,14},{7,15},{8,0},{9,1},... | collective-permute-start | bytes 1179656 | tf_op jit(solution)/shard_map/ppermute | solution.py:26
  58.0 4.8 %collective-permute-start.10 = (f32[2,8,32,128]{3,2,1,0:T(8,128)S(1)}, f32[2,8,32,128]{3,2,1,0:T(8,128)S(1)}, u32[]{:S(2)}, u32[]{:S(2)}) collective-permute-start(f32[2,8,32,128]{3,2,1,0:T(8,128)S(1)} %pad_maximum_fusion.3), channel_id=1, source_target_pairs={{0,8},{1,9},{2,10},{3,11},{4,12},{5,13},{6,14},{7,15},{8,0},{9,1},... | collective-permute-start | bytes 786440 | tf_op jit(solution)/shard_map/ppermute | solution.py:26
  58.3 41.5 %collective-permute-start.11 = (f32[2,4,128,128]{3,2,1,0:T(8,128)}, f32[2,4,128,128]{3,2,1,0:T(8,128)S(1)}, u32[]{:S(2)}, u32[]{:S(2)}) collective-permute-start(f32[2,4,128,128]{3,2,1,0:T(8,128)} %shard_map.140), channel_id=1, source_target_pairs={{0,4},{1,5},{2,6},{3,7},{4,0},{5,1},{6,2},{7,3},{8,12},{9,13},{10,... | collective-permute-start | bytes 1572872 | tf_op jit(solution)/shard_map/ppermute | solution.py:26
  61.8 5.0 %collective-permute-start.7 = (f32[3,2,128,128]{3,2,1,0:T(8,128)}, f32[3,2,128,128]{3,2,1,0:T(8,128)}, u32[]{:S(2)}, u32[]{:S(2)}) collective-permute-start(f32[3,2,128,128]{3,2,1,0:T(8,128)} %get-tuple-element.33.refs_0_), channel_id=1, source_target_pairs={{0,8},{1,9},{2,10},{3,11},{4,12},{5,13},{6,14},{7,15},{8,0},{9,1},... | collective-permute-start | bytes 1179656 | tf_op jit(solution)/shard_map/ppermute | solution.py:26
  61.8 5.0 %collective-permute-start.8 = (f32[3,2,128,128]{3,2,1,0:T(8,128)}, f32[3,2,128,128]{3,2,1,0:T(8,128)}, u32[]{:S(2)}, u32[]{:S(2)}) collective-permute-start(f32[3,2,128,128]{3,2,1,0:T(8,128)} %collective-permute-done.2.refs_1_), channel_id=1, source_target_pairs={{0,8},{1,9},{2,10},{3,11},{4,12},{5,13},{6,14},{7,15},{8,0},{9,1},... | collective-permute-start | bytes 1179656 | tf_op jit(solution)/shard_map/ppermute | solution.py:26
  62.6 35.0 %collective-permute-start.9 = (f32[1,4,128,128]{3,2,1,0:T(8,128)S(1)}, f32[1,4,128,128]{3,2,1,0:T(8,128)S(1)}, u32[]{:S(2)}, u32[]{:S(2)}) collective-permute-start(f32[1,4,128,128]{3,2,1,0:T(8,128)S(1)} %shard_map.142), channel_id=1, source_target_pairs={{0,4},{1,5},{2,6},{3,7},{4,0},{5,1},{6,2},{7,3},{8,12},{9,13},{10,... | collective-permute-start | bytes 786440 | tf_op jit(solution)/shard_map/ppermute | solution.py:26
  63.4 1.6 %copy-start.6 = (f32[1,4,128,128]{3,2,1,0:T(8,128)S(1)}, f32[1,4,128,128]{3,2,1,0:T(8,128)}, u32[]{:S(2)}) copy-start(f32[1,4,128,128]{3,2,1,0:T(8,128)} %param.12) | copy-start | bytes 786436
  63.4 2.0 %copy-start.5 = (f32[2,4,128,128]{3,2,1,0:T(8,128)S(1)}, f32[2,4,128,128]{3,2,1,0:T(8,128)}, u32[]{:S(2)}) copy-start(f32[2,4,128,128]{3,2,1,0:T(8,128)} %param.15) | copy-start | bytes 1572868
  101.5 1.9 %collective-permute-start.12 = (f32[5,32,128]{2,1,0:T(8,128)S(1)}, f32[5,32,128]{2,1,0:T(8,128)S(1)}, u32[]{:S(2)}, u32[]{:S(2)}) collective-permute-start(f32[5,32,128]{2,1,0:T(8,128)S(1)} %get-tuple-element.40), channel_id=1, source_target_pairs={{0,8},{1,9},{2,10},{3,11},{4,12},{5,13},{6,14},{7,15},{8,0},{9,1},... | collective-permute-start | bytes 245768 | tf_op jit(solution)/shard_map/ppermute | solution.py:26
  101.5 5.2 %collective-permute-start.13 = (f32[5,32,128]{2,1,0:T(8,128)S(1)}, f32[5,32,128]{2,1,0:T(8,128)S(1)}, u32[]{:S(2)}, u32[]{:S(2)}) collective-permute-start(f32[5,32,128]{2,1,0:T(8,128)S(1)} %get-tuple-element.41), channel_id=1, source_target_pairs={{0,16},{1,17},{2,18},{3,19},{4,20},{5,21},{6,22},{7,23},{8,24},{9,... | collective-permute-start | bytes 245768 | tf_op jit(solution)/shard_map/ppermute | solution.py:26
  102.1 5.6 %collective-permute-start.14 = (f32[5,32,128]{2,1,0:T(8,128)S(1)}, f32[5,32,128]{2,1,0:T(8,128)S(1)}, u32[]{:S(2)}, u32[]{:S(2)}) collective-permute-start(f32[5,32,128]{2,1,0:T(8,128)S(1)} %get-tuple-element.42), channel_id=1, source_target_pairs={{0,24},{1,25},{2,26},{3,27},{4,28},{5,29},{6,30},{7,31},{8,16},{9,... | collective-permute-start | bytes 245768 | tf_op jit(solution)/shard_map/ppermute | solution.py:26

commit v4 on v3

--- a/solution.py
+++ b/solution.py
@@ -26,21 +26,20 @@
     return lax.ppermute(array, ("row", "col"), pairs)
 
 
-def pick_kernel(plan, place, struct, ainv, *outs):
-    width, tile_rows, tile_cols = plan
+def pick_kernel(plan, place, struct, ainv, out):
+    width, tile_rows, tile_cols, flip = plan
     row, col, base = place[0], place[1], place[2]
-    members, slot_share, pair_width = outs[0].shape[:3]
+    members, slot_share, pair_width = out.shape[:3]
     for member in range(members):
-        for side, out in enumerate(outs):
-            u = jnp.bitwise_xor(base, (1 - side) * members) + member
-            for k in range(pair_width):
-                at_col = struct[u, col * pair_width + k] - col * tile_cols
-                for j in range(slot_share):
-                    at_row = struct[u, row * slot_share + j] - row * tile_rows
-                    out[member, j, k] = ainv[
-                        pl.ds(pl.multiple_of(at_row * width, width), width),
-                        pl.ds(pl.multiple_of(at_col * width, width), width),
-                    ]
+        u = jnp.bitwise_xor(base, flip) + member
+        for k in range(pair_width):
+            at_col = struct[u, col * pair_width + k] - col * tile_cols
+            for j in range(slot_share):
+                at_row = struct[u, row * slot_share + j] - row * tile_rows
+                out[member, j, k] = ainv[
+                    pl.ds(pl.multiple_of(at_row * width, width), width),
+                    pl.ds(pl.multiple_of(at_col * width, width), width),
+                ]
 
 
 def split(value):
@@ -48,42 +47,56 @@
     return top, (value - top.astype(jnp.float32)).astype(jnp.bfloat16)
 
 
-def product_kernel(plan, place, tiles, *refs):
-    start, first, count_panels = plan
-    panels, out = refs[:count_panels], refs[-1]
-    members, slot_share, pair_width, width, _ = tiles.shape
-    count = out.shape[0]
+def product_of(tiles, panels, start, count):
+    slot_share, pair_width = tiles[0].shape[:2]
     lhs, rhs = [], []
-    for i, panel in enumerate(panels):
-        at = jnp.bitwise_xor(place[0], first + i)
+    for tile, panel in zip(tiles, panels):
         for k in range(pair_width):
-            lhs.append(jnp.concatenate([tiles[at, j, k] for j in range(slot_share)], axis=0))
+            lhs.append(jnp.concatenate([tile[j, k] for j in range(slot_share)], axis=0))
             blocks = [panel[n, k] for n in range(start, start + count)]
             rhs.append(jnp.concatenate(blocks, axis=1))
     lhs_top, lhs_rest = split(jnp.concatenate(lhs, axis=1))
     rhs_top, rhs_rest = split(jnp.concatenate(rhs, axis=0))
     mul = functools.partial(jnp.dot, preferred_element_type=jnp.float32)
-    total = mul(lhs_top, rhs_rest) + mul(lhs_rest, rhs_top) + mul(lhs_top, rhs_top)
+    return mul(lhs_top, rhs_rest) + mul(lhs_rest, rhs_top) + mul(lhs_top, rhs_top)
+
+
+def product_kernel(plan, place, *refs):
+    start, used = plan
+    tiles, panels, out = [ref.at[0] for ref in refs[:used]], refs[used : 2 * used], refs[-1]
+    count, slot_share, width, _ = out.shape
+    total = product_of(tiles, panels, start, count)
     for n in range(count):
         for j in range(slot_share):
             value = total[j * width : (j + 1) * width, n * width : (n + 1) * width]
-            if len(refs) > count_panels + 1:
-                value += refs[count_panels][start + n, j]
+            if len(refs) > 2 * used + 1:
+                value += refs[2 * used][start + n, j]
             out[n, j] = value
 
 
 def product(place, tiles, panels, start, stop, first=0, so_far=()):
-    members, slot_share, pair_width, width, _ = tiles.shape
+    _, slot_share, pair_width, width, _ = tiles.shape
     count = stop - start
+    result = (count, slot_share, width, width)
     flops = 6 * len(panels) * pair_width * slot_share * count * width**3
+
+    def member(i):
+        return lambda _, place: (jnp.bitwise_xor(place[0], first + i), 0, 0, 0, 0)
+
+    whole = [pl.BlockSpec(a.shape, lambda *_: (0, 0, 0, 0)) for a in (*panels, *so_far)]
     return pl.pallas_call(
-        functools.partial(product_kernel, (start, first, len(panels))),
-        out_shape=jax.ShapeDtypeStruct((count, slot_share, width, width), jnp.float32),
-        in_specs=[SMEM] + [VMEM] * (1 + len(panels) + len(so_far)),
-        out_specs=VMEM,
+        functools.partial(product_kernel, (start, len(panels))),
+        out_shape=jax.ShapeDtypeStruct(result, jnp.float32),
+        grid_spec=pltpu.PrefetchScalarGridSpec(
+            num_scalar_prefetch=1,
+            grid=(1,),
+            in_specs=[pl.BlockSpec((1, *tiles.shape[1:]), member(i)) for i in range(len(panels))]
+            + whole,
+            out_specs=pl.BlockSpec(result, lambda *_: (0, 0, 0, 0)),
+        ),
         compiler_params=pltpu.CompilerParams(vmem_limit_bytes=40 * 2**20),
         cost_estimate=pl.CostEstimate(flops=flops, bytes_accessed=4 * 2**20, transcendentals=0),
-    )(place, tiles, *panels, *so_far)
+    )(place, *[tiles] * len(panels), *panels, *so_far)
 
 
 def dot(a, b):
@@ -95,10 +108,13 @@
     return jnp.concatenate([ref[(*at, s)] for s in range(slots)], axis=0)
 
 
-def parent_kernel(near, back, linv, upper, uphat, par_hat, kid_hat, off, part, kid_sum):
+def parent_kernel(place, tiles, back, linv, upper, uphat, par_hat, kid_hat, *refs):
+    panels, (off, part, kid_sum) = refs[:-3], refs[-3:]
     slots, width = off.shape[1], off.shape[2]
     kids = upper.shape[0]
-    value = -dot(rows_of(near, 0) + rows_of(back, 0), linv[...])
+    nears = [tiles.at[jnp.bitwise_xor(place[0], i)] for i in range(len(panels))]
+    near = product_of(nears, panels, 0, 1 + kids)
+    value = -dot(near[:, :width] + rows_of(back, 0), linv[...])
     turned = value.T
     diag = dot(rows_of(par_hat).T, value)
     part[0] = diag
@@ -108,7 +124,7 @@
         cross = dot(turned, rows_of(kid_hat, c))
         part[1 + c] = cross
         part[1 + kids + c] = dot(uphat[c].T, cross - dot(diag, uphat[c]))
-        total = rows_of(near, 1 + c) + dot(value, upper[c])
+        total = near[:, (1 + c) * width : (2 + c) * width] + dot(value, upper[c])
         for s in range(slots):
             kid_sum[c, s] = total[s * width : (s + 1) * width]
 
@@ -150,7 +166,7 @@
         in_specs=[SMEM] * scalars + [VMEM] * (len(operands) - scalars),
         out_specs=[VMEM] * len(shapes),
         scratch_shapes=[pltpu.VMEM(shape, jnp.float32) for shape in scratch],
-        compiler_params=pltpu.CompilerParams(vmem_limit_bytes=24 * 2**20),
+        compiler_params=pltpu.CompilerParams(vmem_limit_bytes=40 * 2**20),
         cost_estimate=pl.CostEstimate(flops=10**8, bytes_accessed=2 * 2**20, transcendentals=0),
     )(*operands)
 
@@ -178,6 +194,24 @@
     top = my_row // lows
     match = top == my_high // lows
 
+    members = far_bits
+    groups = [list(range(0, members)), list(range(members, 2 * members))]
+    piece = (members, slot_share, pair_width, width, width)
+    spot = jnp.stack([my_row, my_col, my_col // members * members])
+
+    def pick(flip, ainv):
+        return pl.pallas_call(
+            functools.partial(pick_kernel, (width, tile_rows, tile_cols, flip)),
+            out_shape=jax.ShapeDtypeStruct(piece, jnp.float32),
+            in_specs=[SMEM, SMEM, VMEM],
+            out_specs=VMEM,
+            compiler_params=pltpu.CompilerParams(vmem_limit_bytes=24 * 2**20),
+            cost_estimate=pl.CostEstimate(flops=0, bytes_accessed=4 * 2**20, transcendentals=0),
+        )(spot, par_struct, ainv)
+
+    def exchange(tiles):
+        return lax.all_to_all(tiles, "col", 0, 0, axis_index_groups=groups, tiled=True)
+
     def take(half):
         par = lax.dynamic_slice_in_dim(par_panel, half * pair_width, pair_width, 1)
         kid = lax.dynamic_slice_in_dim(kid_panel, half * pair_width, pair_width, 1)
@@ -197,22 +231,10 @@
 
     small = jnp.concatenate([par_linv, par_dinv, kid_upper, kid_linv, kid_dinv], axis=0)
     small_other = swap(after(small, got), lows, 0)
-    far_other = swap(after(far, near_other, small_other), lows, 0)
-
-    members = far_bits
-    groups = [list(range(0, members)), list(range(members, 2 * members))]
-    piece = jax.ShapeDtypeStruct((members, slot_share, pair_width, width, width), jnp.float32)
-    far_tiles, near_tiles = pl.pallas_call(
-        functools.partial(pick_kernel, (width, tile_rows, tile_cols)),
-        out_shape=[piece] * 2,
-        in_specs=[SMEM, SMEM, VMEM],
-        out_specs=[VMEM] * 2,
-        compiler_params=pltpu.CompilerParams(vmem_limit_bytes=24 * 2**20),
-        cost_estimate=pl.CostEstimate(flops=0, bytes_accessed=6 * 2**20, transcendentals=0),
-    )(jnp.stack([my_row, my_col, my_col // members * members]), par_struct, after(ainv_top, sent))
-    far_tiles = lax.all_to_all(far_tiles, "col", 0, 0, axis_index_groups=groups, tiled=True)
-    near_tiles = after(near_tiles, far_tiles, small_other)
-    near_tiles = lax.all_to_all(near_tiles, "col", 0, 0, axis_index_groups=groups, tiled=True)
+    far_tiles = exchange(pick(members, after(ainv_top, sent)))
+    near_tiles = pick(0, after(ainv_top, got))
+    far_other = swap(after(far, near_other, small_other, near_tiles), lows, 0)
+    near_tiles = exchange(after(near_tiles, far_tiles, small_other))
 
     place = ((my_row % lows) * halves + top).reshape(1)
     so_far = [product(place, far_tiles, [far], 0, 1 + children)]
@@ -221,6 +243,7 @@
     last = (len(far_panels) - 1, so_far)
     par_away = product(place, far_tiles, far_panels[-1:], 0, 1, *last)
     par_back = swap(par_away, 0, far_bits)
+    last = (last[0], [after(so_far[0], par_away)])
     kid_away = product(place, far_tiles, far_panels[-1:], 1, 1 + children, *last)
     kid_back = swap(kid_away, 0, far_bits)
 
@@ -235,7 +258,6 @@
     at = jnp.asarray(inverse)[jnp.arange(grid_rows) ^ my_row]
     small = small[at].swapaxes(0, 1).reshape(small.shape[1], width, width)
 
-    sums = product(place, near_tiles, near_panels, 0, 1 + children)
     plinv, pdinv = small[0], small[1]
     kupper = small[2 : 2 + children]
     klinv = small[2 + children : 2 + 2 * children]
@@ -255,7 +277,8 @@
     par_off, part, kid_sum = local(
         parent_kernel,
         [par_panel.shape, terms, kid_panel.shape],
-        sums, par_back, plinv, kupper, kuphat, par_hat, kid_hat,
+        place, near_tiles, par_back, plinv, kupper, kuphat, par_hat, kid_hat, *near_panels,
+        scalars=1,
     )
     band = (1 + 2 * children, band_rows, width)
     kid_off, *bands = local(

time: 109 us -> 108 us (level)
  waiting for transfers between devices: 55.9 us -> 51.3 us
  local copies, waits for them, and re-layouts: 6.25 us -> 9.31 us
    all_to_all x2, waiting for transfers between devices: 27.7 us -> 12.3 us  [exchange(): lax.all_to_all(tiles, 'col', 0, 0, axis_index_groups=groups, tiled=True)]
    ppermute x15, waiting for transfers between devices: 28.2 us -> 39.1 us  [swap(): return lax.ppermute(array, ('row', 'col'), pairs)]
    pallas_call x3, Pallas kernels: 4.67 us -> 8 us  [local(): pl.pallas_call(kernel, out_shape=[jax.ShapeDtypeStruct(shape, jnp.float32...]
    pallas_call x6, Pallas kernels: 10.2 us -> 7.03 us  [the longest x4 5.26 us: product(): pl.pallas_call(functools.partial(product_kernel, (start, len(panels))), o...]
    unnamed x28 -> x40, local copies, waits for them, and re-layouts: 2.75 us -> 5.09 us
  transfers between devices with their start and end apart: 17 -> 17, of which waited for: 7 -> 7; matrix products, arithmetic and copies ran while one was open for 5% -> 5% of each run, Pallas kernels for 10% -> 11%
where the time goes in v4:
time: 108 us; the launch traced here: 107 us
  waiting for transfers between devices  51.3 us (48%)
  starting transfers between devices  27 us (25%)
  Pallas kernels  15 us (14%)
  local copies, waits for them, and re-layouts  9.31 us (9%)
  matrix products  3.09 us (3%)
    ppermute x15, waiting for transfers between devices, swap(): return lax.ppermute(array, ('row', 'col'), pairs)  39.1 us
    ppermute x15, starting transfers between devices, swap(): return lax.ppermute(array, ('row', 'col'), pairs)  14.6 us
    all_to_all x2, starting transfers between devices, exchange(): lax.all_to_all(tiles, 'col', 0, 0, axis_index_groups=groups, tiled=True)  12.4 us
    all_to_all x2, waiting for transfers between devices, exchange(): lax.all_to_all(tiles, 'col', 0, 0, axis_index_groups=groups, tiled=True)  12.3 us
    pallas_call x3, Pallas kernels, local(): pl.pallas_call(kernel, out_shape=[jax.ShapeDtypeStruct(shape, jnp.float32...  8 us
    pallas_call x4, Pallas kernels, product(): pl.pallas_call(functools.partial(product_kernel, (start, len(panels))), o...  5.26 us
    unnamed x40, local copies, waits for them, and re-layouts  5.09 us
    dot_general x9, matrix products, mm(): return jnp.einsum(spec, *operands, precision=precision)  3.09 us
  transfers between devices with their start and end apart: 17, of which 7 were waited for; matrix products, arithmetic and copies ran while one was open for 5% of the time, Pallas kernels for 11%

profile of v4, /device:TPU:0, one launch (start us, length us, event | category | flops | bytes accessed | tf_op | source)
XLA Modules:
  0.0 107.1 jit_solution(13018885002951576881)
XLA Ops:
  0.7 1.2 %constant_dynamic-slice_fusion.1 = (f32[2,2,128,128]{3,2,1,0:T(8,128)S(1)}, f32[2,2,128,128]{3,2,1,0:T(8,128)S(1)}) fusion(f32[2,4,128,128]{3,2,1,0:T(8,128)} %param.15, s32[]{:T(128)S(6)} %select_n.71, s32[]{:T(128)S(6)} %select_n.67), kind=kLoop, calls=%fused_computation.28 | loop fusion | bytes 1048584 | tf_op jit(solution)/shard_map/dynamic_slice | solution.py:217
  1.9 1.0 constant_dynamic-slice_fusion.2
  3.0 0.9 shard_map.138
  3.9 1.3 %copy-done.3 = f32[4,4,2,128,128]{4,3,2,1,0:T(8,128)} copy-done((f32[4,4,2,128,128]{4,3,2,1,0:T(8,128)}, f32[4,4,2,128,128]{4,3,2,1,0:T(8,128)S(1)}, u32[]{:S(2)}) %copy-start.3) | copy-done | bytes 2097176
  5.3 5.4 %all-to-all-start = ((f32[4,4,2,128,128]{4,3,2,1,0:T(8,128)}), f32[4,4,2,128,128]{4,3,2,1,0:T(8,128)S(1)}, u32[]{:S(2)}, u32[]{:S(2)}) async-start(f32[4,4,2,128,128]{4,3,2,1,0:T(8,128)} %copy-done.3), calls=%async_computation | async-start | bytes 4194304 | tf_op jit(solution)/shard_map/all_to_all | solution.py:213
  10.6 1.5 %collective-permute-start = (f32[3,2,128,128]{3,2,1,0:T(8,128)S(1)}, f32[3,2,128,128]{3,2,1,0:T(8,128)S(1)}, u32[]{:S(2)}, u32[]{:S(2)}) collective-permute-start(f32[3,2,128,128]{3,2,1,0:T(8,128)S(1)} %pad_maximum_fusion.1), channel_id=1, source_target_pairs={{0,16},{1,17},{2,18},{3,19},{4,20},{5,21},{6,22},{7,23},{8,24},{9,... | collective-permute-start | bytes 1179656 | tf_op jit(solution)/shard_map/ppermute | solution.py:26
  12.2 9.0 %collective-permute-done = f32[3,2,128,128]{3,2,1,0:T(8,128)S(1)} collective-permute-done((f32[3,2,128,128]{3,2,1,0:T(8,128)S(1)}, f32[3,2,128,128]{3,2,1,0:T(8,128)S(1)}, u32[]{:S(2)}, u32[]{:S(2)}) %collective-permute-start) | collective-permute-done | bytes 393248 | tf_op jit(solution)/shard_map/ppermute | solution.py:26
  21.3 2.8 %collective-permute-start.2 = (f32[3,2,128,128]{3,2,1,0:T(8,128)S(1)}, f32[3,2,128,128]{3,2,1,0:T(8,128)}, u32[]{:S(2)}, u32[]{:S(2)}) collective-permute-start(f32[3,2,128,128]{3,2,1,0:T(8,128)S(1)} %get-tuple-element.48), channel_id=1, source_target_pairs={{0,4},{1,5},{2,6},{3,7},{4,0},{5,1},{6,2},{7,3},{8,12},{9,13},{10,... | collective-permute-start | bytes 1179656 | tf_op jit(solution)/shard_map/ppermute | solution.py:26
  24.1 1.5 %collective-permute-start.3 = (f32[3,2,128,128]{3,2,1,0:T(8,128)S(1)}, f32[3,2,128,128]{3,2,1,0:T(8,128)S(1)}, u32[]{:S(2)}, u32[]{:S(2)}) collective-permute-start(f32[3,2,128,128]{3,2,1,0:T(8,128)S(1)} %get-tuple-element.34.refs_0_), channel_id=1, source_target_pairs={{0,16},{1,17},{2,18},{3,19},{4,20},{5,21},{6,22},{7,23},{8,24},{9,... | collective-permute-start | bytes 1179656 | tf_op jit(solution)/shard_map/ppermute | solution.py:26
  26.3 1.6 %copy-done.1 = f32[1024,512]{1,0:T(8,128)S(1)} copy-done((f32[1024,512]{1,0:T(8,128)S(1)}, f32[1024,512]{1,0:T(8,128)}, u32[]{:S(2)}) %copy-start.1) | copy-done | bytes 2097176
  27.9 0.9 shard_map.137
  28.8 1.4 %copy-done.2 = f32[4,4,2,128,128]{4,3,2,1,0:T(8,128)} copy-done((f32[4,4,2,128,128]{4,3,2,1,0:T(8,128)}, f32[4,4,2,128,128]{4,3,2,1,0:T(8,128)S(1)}, u32[]{:S(2)}) %copy-start.2) | copy-done | bytes 2097176
  30.1 6.4 %collective-permute-done.1 = f32[8,32,128]{2,1,0:T(8,128)S(1)} collective-permute-done((f32[8,32,128]{2,1,0:T(8,128)S(1)}, f32[8,32,128]{2,1,0:T(8,128)S(1)}, u32[]{:S(2)}, u32[]{:S(2)}) %collective-permute-start.1) | collective-permute-done | bytes 131104 | tf_op jit(solution)/shard_map/ppermute | solution.py:26
  36.5 5.2 %collective-permute-done.2.refs_1_ = f32[3,2,128,128]{3,2,1,0:T(8,128)} collective-permute-done((f32[3,2,128,128]{3,2,1,0:T(8,128)S(1)}, f32[3,2,128,128]{3,2,1,0:T(8,128)}, u32[]{:S(2)}, u32[]{:S(2)}) %collective-permute-start.2) | collective-permute-done | bytes 393248 | tf_op jit(solution)/shard_map/ppermute | solution.py:26
  41.7 0.8 copy-done.6
  42.5 1.6 %collective-permute-start.4 = (f32[3,2,128,128]{3,2,1,0:T(8,128)}, f32[3,2,128,128]{3,2,1,0:T(8,128)}, u32[]{:S(2)}, u32[]{:S(2)}) collective-permute-start(f32[3,2,128,128]{3,2,1,0:T(8,128)} %collective-permute-done.2.refs_1_), channel_id=1, source_target_pairs={{0,16},{1,17},{2,18},{3,19},{4,20},{5,21},{6,22},{7,23},{8,24},{9,... | collective-permute-start | bytes 1179656 | tf_op jit(solution)/shard_map/ppermute | solution.py:26
  44.1 7.0 %all-to-all-start.1 = ((f32[4,4,2,128,128]{4,3,2,1,0:T(8,128)}), f32[4,4,2,128,128]{4,3,2,1,0:T(8,128)}, u32[]{:S(2)}, u32[]{:S(2)}) async-start(f32[4,4,2,128,128]{4,3,2,1,0:T(8,128)} %copy-done.2), calls=%async_computation.1 | async-start | bytes 4194304 | tf_op jit(solution)/shard_map/all_to_all | solution.py:213
  51.2 1.6 %shard_map.139.refs_4_ = f32[3,4,128,128]{3,2,1,0:T(8,128)S(1)} custom-call(s32[1]{0:T(128)} %bitcast.place, f32[4,4,2,128,128]{4,3,2,1,0:T(8,128)S(1)} %all-to-all-done.refs_0_.refs_1_, f32[3,2,128,128]{3,2,1,0:T(8,128)} %collective-permute-done.2.refs_1_), custom_call_target="tpu_custom_call" | custom-call | flops 301989888 | bytes 4194304 | tf_op jit(solution)/shard_map/pallas_call | solution.py:87
  53.1 0.6 gather_fusion
  53.8 2.1 %shard_map.140.refs_2_ = f32[3,4,128,128]{3,2,1,0:T(8,128)S(1)} custom-call(s32[1]{0:T(128)} %bitcast.place, f32[4,4,2,128,128]{4,3,2,1,0:T(8,128)S(1)} %all-to-all-done.refs_0_.refs_1_, f32[4,4,2,128,128]{4,3,2,1,0:T(8,128)S(1)} %all-to-all-done.refs_0_.refs_1_, f32[3,2,128,128]{3,2,1,0:T(8,128)} %collective-permute-done.4.refs_2_, ...), custom_call_target="tpu_custom_call" | custom-call | flops 603979776 | bytes 4194304 | tf_op jit(solution)/shard_map/pallas_call | solution.py:87
  56.3 1.2 %shard_map.142 = f32[2,4,128,128]{3,2,1,0:T(8,128)} custom-call(s32[1]{0:T(128)} %bitcast.place, f32[4,4,2,128,128]{4,3,2,1,0:T(8,128)S(1)} %all-to-all-done.refs_0_.refs_1_, f32[3,2,128,128]{3,2,1,0:T(8,128)S(1)} %collective-permute-done.5.refs_1_, f32[3,4,128,128]{3,2,1,0:T(8,128)S(1)} %shard_map.140.refs_2_), custom_call_target="tpu_custom_call" | custom-call | flops 201326592 | bytes 4194304 | tf_op jit(solution)/shard_map/pallas_call | solution.py:87
  57.8 3.5 %collective-permute-start.7 = (f32[1,4,128,128]{3,2,1,0:T(8,128)S(1)}, f32[1,4,128,128]{3,2,1,0:T(8,128)S(1)}, u32[]{:S(2)}, u32[]{:S(2)}) collective-permute-start(f32[1,4,128,128]{3,2,1,0:T(8,128)S(1)} %shard_map.141), channel_id=1, source_target_pairs={{0,4},{1,5},{2,6},{3,7},{4,0},{5,1},{6,2},{7,3},{8,12},{9,13},{10,... | collective-permute-start | bytes 786440 | tf_op jit(solution)/shard_map/ppermute | solution.py:26
  65.2 0.6 convolution_bitcast_fusion.kid_hat
  65.8 14.7 %collective-permute-done.7.back = f32[1,4,128,128]{3,2,1,0:T(8,128)S(1)} collective-permute-done((f32[1,4,128,128]{3,2,1,0:T(8,128)S(1)}, f32[1,4,128,128]{3,2,1,0:T(8,128)S(1)}, u32[]{:S(2)}, u32[]{:S(2)}) %collective-permute-start.7) | collective-permute-done | bytes 262176 | tf_op jit(solution)/shard_map/ppermute | solution.py:26
  80.6 12.3 %all-to-all-done.1.tiles = f32[4,4,2,128,128]{4,3,2,1,0:T(8,128)} async-done(((f32[4,4,2,128,128]{4,3,2,1,0:T(8,128)}), f32[4,4,2,128,128]{4,3,2,1,0:T(8,128)}, u32[]{:S(2)}, u32[]{:S(2)}) %all-to-all-start.1) | async-done | bytes 2097184 | tf_op jit(solution)/shard_map/all_to_all | solution.py:213
  92.8 5.4 %shard_map.143 = (f32[1,4,128,128]{3,2,1,0:T(8,128)}, f32[5,128,128]{2,1,0:T(8,128)S(1)}, f32[2,4,128,128]{3,2,1,0:T(8,128)S(1)}) custom-call(s32[1]{0:T(128)} %bitcast.place, f32[4,4,2,128,128]{4,3,2,1,0:T(8,128)} %all-to-all-done.1.tiles, f32[1,4,128,128]{3,2,1,0:T(8,128)S(1)} %collective-permute-done.7.back, f32[128,128]{1,0:T(8,128)S(1)} %bitcast.66, ...), custom_call_target="tpu_custom_call" | custom-call | flops 100000000 | bytes 2097152 | tf_op jit(solution)/shard_map/pallas_call | solution.py:163
  98.2 1.8 %shard_map.144 = (f32[2,4,128,128]{3,2,1,0:T(8,128)}, f32[5,32,128]{2,1,0:T(8,128)S(1)}, f32[5,32,128]{2,1,0:T(8,128)S(1)}, f32[5,32,128]{2,1,0:T(8,128)S(1)}, f32[5,32,128]{2,1,0:T(8,128)S(1)}) custom-call(s32[1]{0:T(128)} %bitcast.1.place, f32[2,4,128,128]{3,2,1,0:T(8,128)S(1)} %get-tuple-element.37.kid_sum, ...), custom_call_target="tpu_custom_call" | custom-call | flops 100000000 | bytes 2097152 | tf_op jit(solution)/shard_map/pallas_call | solution.py:163
  100.0 1.9 %collective-permute-start.14 = (f32[5,32,128]{2,1,0:T(8,128)S(1)}, f32[5,32,128]{2,1,0:T(8,128)S(1)}, u32[]{:S(2)}, u32[]{:S(2)}) collective-permute-start(f32[5,32,128]{2,1,0:T(8,128)S(1)} %get-tuple-element.42), channel_id=1, source_target_pairs={{0,24},{1,25},{2,26},{3,27},{4,28},{5,29},{6,30},{7,31},{8,16},{9,... | collective-permute-start | bytes 245768 | tf_op jit(solution)/shard_map/ppermute | solution.py:26
  101.8 0.7 constant_dynamic-slice_fusion.par_pivot
  102.6 2.7 %collective-permute-done.13.refs_2_ = f32[5,32,128]{2,1,0:T(8,128)S(1)} collective-permute-done((f32[5,32,128]{2,1,0:T(8,128)S(1)}, f32[5,32,128]{2,1,0:T(8,128)S(1)}, u32[]{:S(2)}, u32[]{:S(2)}) %collective-permute-start.13) | collective-permute-done | bytes 81952 | tf_op jit(solution)/shard_map/ppermute | solution.py:26
  105.2 1.0 collective-permute-done.14.refs_3_
  106.2 0.9 shard_map.145
  (79 shorter events, 5.7 us)
Async XLA Ops:
  0.6 2.4 %copy-start = (f32[1024,512]{1,0:T(8,128)S(1)}, f32[1024,512]{1,0:T(8,128)}, u32[]{:S(2)}) copy-start(f32[1024,512]{1,0:T(8,128)} %ainv.1) | copy-start | bytes 6291460
  0.6 2.4 %copy-start.8 = (s32[8,16]{1,0:T(8,128)S(1)}, s32[8,16]{1,0:T(8,128)}, u32[]{:S(2)}) copy-start(s32[8,16]{1,0:T(8,128)} %struct.3) | copy-start | bytes 1540
  5.2 6.9 %copy-start.16 = (f32[1,32,128]{2,1,0:T(8,128)S(1)}, f32[1,32,128]{2,1,0:T(8,128)}, u32[]{:S(2)}) copy-start(f32[1,32,128]{2,1,0:T(8,128)} %param.13) | copy-start | bytes 49156
  5.3 6.9 %copy-start.17 = (f32[1,32,128]{2,1,0:T(8,128)S(1)}, f32[1,32,128]{2,1,0:T(8,128)}, u32[]{:S(2)}) copy-start(f32[1,32,128]{2,1,0:T(8,128)} %param.14) | copy-start | bytes 49156
  5.3 20.4 %copy-start.13 = (f32[2,32,128]{2,1,0:T(8,128)S(1)}, f32[2,32,128]{2,1,0:T(8,128)}, u32[]{:S(2)}) copy-start(f32[2,32,128]{2,1,0:T(8,128)} %param.16) | copy-start | bytes 98308
  5.3 20.4 %copy-start.14 = (f32[2,32,128]{2,1,0:T(8,128)S(1)}, f32[2,32,128]{2,1,0:T(8,128)}, u32[]{:S(2)}) copy-start(f32[2,32,128]{2,1,0:T(8,128)} %param.17) | copy-start | bytes 98308
  5.3 20.4 %copy-start.15 = (f32[2,32,128]{2,1,0:T(8,128)S(1)}, f32[2,32,128]{2,1,0:T(8,128)}, u32[]{:S(2)}) copy-start(f32[2,32,128]{2,1,0:T(8,128)} %param.18) | copy-start | bytes 98308
  5.3 38.8 %all-to-all-start = ((f32[4,4,2,128,128]{4,3,2,1,0:T(8,128)}), f32[4,4,2,128,128]{4,3,2,1,0:T(8,128)S(1)}, u32[]{:S(2)}, u32[]{:S(2)}) async-start(f32[4,4,2,128,128]{4,3,2,1,0:T(8,128)} %copy-done.3), calls=%async_computation | async-start | bytes 4194304 | tf_op jit(solution)/shard_map/all_to_all | solution.py:213
  10.6 10.6 %collective-permute-start = (f32[3,2,128,128]{3,2,1,0:T(8,128)S(1)}, f32[3,2,128,128]{3,2,1,0:T(8,128)S(1)}, u32[]{:S(2)}, u32[]{:S(2)}) collective-permute-start(f32[3,2,128,128]{3,2,1,0:T(8,128)S(1)} %pad_maximum_fusion.1), channel_id=1, source_target_pairs={{0,16},{1,17},{2,18},{3,19},{4,20},{5,21},{6,22},{7,23},{8,24},{9,... | collective-permute-start | bytes 1179656 | tf_op jit(solution)/shard_map/ppermute | solution.py:26
  21.3 7.5 %copy-start.4 = (f32[3,2,128,128]{3,2,1,0:T(8,128)}, f32[3,2,128,128]{3,2,1,0:T(8,128)S(1)}, u32[]{:S(2)}) copy-start(f32[3,2,128,128]{3,2,1,0:T(8,128)S(1)} %get-tuple-element.34.refs_0_) | copy-start | bytes 1179652
  21.3 20.4 %collective-permute-start.2 = (f32[3,2,128,128]{3,2,1,0:T(8,128)S(1)}, f32[3,2,128,128]{3,2,1,0:T(8,128)}, u32[]{:S(2)}, u32[]{:S(2)}) collective-permute-start(f32[3,2,128,128]{3,2,1,0:T(8,128)S(1)} %get-tuple-element.48), channel_id=1, source_target_pairs={{0,4},{1,5},{2,6},{3,7},{4,0},{5,1},{6,2},{7,3},{8,12},{9,13},{10,... | collective-permute-start | bytes 1179656 | tf_op jit(solution)/shard_map/ppermute | solution.py:26
  24.1 17.6 %collective-permute-start.3 = (f32[3,2,128,128]{3,2,1,0:T(8,128)S(1)}, f32[3,2,128,128]{3,2,1,0:T(8,128)S(1)}, u32[]{:S(2)}, u32[]{:S(2)}) collective-permute-start(f32[3,2,128,128]{3,2,1,0:T(8,128)S(1)} %get-tuple-element.34.refs_0_), channel_id=1, source_target_pairs={{0,16},{1,17},{2,18},{3,19},{4,20},{5,21},{6,22},{7,23},{8,24},{9,... | collective-permute-start | bytes 1179656 | tf_op jit(solution)/shard_map/ppermute | solution.py:26
  25.7 10.8 %collective-permute-start.1 = (f32[8,32,128]{2,1,0:T(8,128)S(1)}, f32[8,32,128]{2,1,0:T(8,128)S(1)}, u32[]{:S(2)}, u32[]{:S(2)}) collective-permute-start(f32[8,32,128]{2,1,0:T(8,128)S(1)} %constant_dynamic-update-slice_fusion), channel_id=1, source_target_pairs={{0,16},{1,17},{2,18},{3,19},{4,20},{5,21},{6,22},{7,23},{8,24},{9,... | collective-permute-start | bytes 393224 | tf_op jit(solution)/shard_map/ppermute | solution.py:26
  26.3 1.6 %copy-start.1 = (f32[1024,512]{1,0:T(8,128)S(1)}, f32[1024,512]{1,0:T(8,128)}, u32[]{:S(2)}) copy-start(f32[1024,512]{1,0:T(8,128)} %ainv.1) | copy-start | bytes 6291460
  42.5 10.3 %collective-permute-start.4 = (f32[3,2,128,128]{3,2,1,0:T(8,128)}, f32[3,2,128,128]{3,2,1,0:T(8,128)}, u32[]{:S(2)}, u32[]{:S(2)}) collective-permute-start(f32[3,2,128,128]{3,2,1,0:T(8,128)} %collective-permute-done.2.refs_1_), channel_id=1, source_target_pairs={{0,16},{1,17},{2,18},{3,19},{4,20},{5,21},{6,22},{7,23},{8,24},{9,... | collective-permute-start | bytes 1179656 | tf_op jit(solution)/shard_map/ppermute | solution.py:26
  44.1 9.6 %collective-permute-start.6 = (f32[3,2,128,128]{3,2,1,0:T(8,128)}, f32[3,2,128,128]{3,2,1,0:T(8,128)}, u32[]{:S(2)}, u32[]{:S(2)}) collective-permute-start(f32[3,2,128,128]{3,2,1,0:T(8,128)} %collective-permute-done.2.refs_1_), channel_id=1, source_target_pairs={{0,8},{1,9},{2,10},{3,11},{4,12},{5,13},{6,14},{7,15},{8,0},{9,1},... | collective-permute-start | bytes 1179656 | tf_op jit(solution)/shard_map/ppermute | solution.py:26
  44.1 48.7 %all-to-all-start.1 = ((f32[4,4,2,128,128]{4,3,2,1,0:T(8,128)}), f32[4,4,2,128,128]{4,3,2,1,0:T(8,128)}, u32[]{:S(2)}, u32[]{:S(2)}) async-start(f32[4,4,2,128,128]{4,3,2,1,0:T(8,128)} %copy-done.2), calls=%async_computation.1 | async-start | bytes 4194304 | tf_op jit(solution)/shard_map/all_to_all | solution.py:213
  51.2 1.9 %copy-start.9 = (s32[4]{0:T(128)S(1)}, s32[4]{0:T(128)}, u32[]{:S(2)}) copy-start(s32[4]{0:T(128)} %constant.67.clone) | copy-start | bytes 52
  52.8 3.1 %collective-permute-start.5 = (f32[3,2,128,128]{3,2,1,0:T(8,128)}, f32[3,2,128,128]{3,2,1,0:T(8,128)S(1)}, u32[]{:S(2)}, u32[]{:S(2)}) collective-permute-start(f32[3,2,128,128]{3,2,1,0:T(8,128)} %collective-permute-done.4.refs_2_), channel_id=1, source_target_pairs={{0,8},{1,9},{2,10},{3,11},{4,12},{5,13},{6,14},{7,15},{8,0},{9,1},... | collective-permute-start | bytes 1179656 | tf_op jit(solution)/shard_map/ppermute | solution.py:26
  56.3 5.1 %copy-start.5 = (f32[3,2,128,128]{3,2,1,0:T(8,128)S(1)}, f32[3,2,128,128]{3,2,1,0:T(8,128)}, u32[]{:S(2)}) copy-start(f32[3,2,128,128]{3,2,1,0:T(8,128)} %copy-done.4) | copy-start | bytes 1179652
  56.3 5.1 %copy-start.7 = (f32[3,2,128,128]{3,2,1,0:T(8,128)S(1)}, f32[3,2,128,128]{3,2,1,0:T(8,128)}, u32[]{:S(2)}) copy-start(f32[3,2,128,128]{3,2,1,0:T(8,128)} %copy-done.6) | copy-start | bytes 1179652
  57.5 4.4 %collective-permute-start.8 = (f32[2,8,32,128]{3,2,1,0:T(8,128)S(1)}, f32[2,8,32,128]{3,2,1,0:T(8,128)S(1)}, u32[]{:S(2)}, u32[]{:S(2)}) collective-permute-start(f32[2,8,32,128]{3,2,1,0:T(8,128)S(1)} %pad_maximum_fusion.3), channel_id=1, source_target_pairs={{0,8},{1,9},{2,10},{3,11},{4,12},{5,13},{6,14},{7,15},{8,0},{9,1},... | collective-permute-start | bytes 786440 | tf_op jit(solution)/shard_map/ppermute | solution.py:26
  57.8 22.8 %collective-permute-start.7 = (f32[1,4,128,128]{3,2,1,0:T(8,128)S(1)}, f32[1,4,128,128]{3,2,1,0:T(8,128)S(1)}, u32[]{:S(2)}, u32[]{:S(2)}) collective-permute-start(f32[1,4,128,128]{3,2,1,0:T(8,128)S(1)} %shard_map.141), channel_id=1, source_target_pairs={{0,4},{1,5},{2,6},{3,7},{4,0},{5,1},{6,2},{7,3},{8,12},{9,13},{10,... | collective-permute-start | bytes 786440 | tf_op jit(solution)/shard_map/ppermute | solution.py:26
  61.3 36.9 %collective-permute-start.11 = (f32[2,4,128,128]{3,2,1,0:T(8,128)}, f32[2,4,128,128]{3,2,1,0:T(8,128)S(1)}, u32[]{:S(2)}, u32[]{:S(2)}) collective-permute-start(f32[2,4,128,128]{3,2,1,0:T(8,128)} %shard_map.142), channel_id=1, source_target_pairs={{0,4},{1,5},{2,6},{3,7},{4,0},{5,1},{6,2},{7,3},{8,12},{9,13},{10,... | collective-permute-start | bytes 1572872 | tf_op jit(solution)/shard_map/ppermute | solution.py:26
  61.3 19.2 %collective-permute-start.9 = (f32[3,2,128,128]{3,2,1,0:T(8,128)S(1)}, f32[3,2,128,128]{3,2,1,0:T(8,128)S(1)}, u32[]{:S(2)}, u32[]{:S(2)}) collective-permute-start(f32[3,2,128,128]{3,2,1,0:T(8,128)S(1)} %copy-done.5), channel_id=1, source_target_pairs={{0,8},{1,9},{2,10},{3,11},{4,12},{5,13},{6,14},{7,15},{8,0},{9,1},... | collective-permute-start | bytes 1179656 | tf_op jit(solution)/shard_map/ppermute | solution.py:26
  61.4 19.2 %collective-permute-start.10 = (f32[3,2,128,128]{3,2,1,0:T(8,128)S(1)}, f32[3,2,128,128]{3,2,1,0:T(8,128)}, u32[]{:S(2)}, u32[]{:S(2)}) collective-permute-start(f32[3,2,128,128]{3,2,1,0:T(8,128)S(1)} %copy-done.7), channel_id=1, source_target_pairs={{0,8},{1,9},{2,10},{3,11},{4,12},{5,13},{6,14},{7,15},{8,0},{9,1},... | collective-permute-start | bytes 1179656 | tf_op jit(solution)/shard_map/ppermute | solution.py:26
  62.5 2.0 %copy-start.11 = (f32[1,4,128,128]{3,2,1,0:T(8,128)S(1)}, f32[1,4,128,128]{3,2,1,0:T(8,128)}, u32[]{:S(2)}) copy-start(f32[1,4,128,128]{3,2,1,0:T(8,128)} %param.12) | copy-start | bytes 786436
  62.6 2.7 %copy-start.10 = (f32[2,4,128,128]{3,2,1,0:T(8,128)S(1)}, f32[2,4,128,128]{3,2,1,0:T(8,128)}, u32[]{:S(2)}) copy-start(f32[2,4,128,128]{3,2,1,0:T(8,128)} %param.15) | copy-start | bytes 1572868
  63.2 1.8 %copy-start.12 = (f32[128,128]{1,0:T(8,128)}, f32[128,128]{1,0:T(8,128)S(1)}, u32[]{:S(2)}) copy-start(f32[128,128]{1,0:T(8,128)S(1)} %fusion.11) | copy-start | bytes 196612
  100.0 2.6 %collective-permute-start.12 = (f32[5,32,128]{2,1,0:T(8,128)S(1)}, f32[5,32,128]{2,1,0:T(8,128)S(1)}, u32[]{:S(2)}, u32[]{:S(2)}) collective-permute-start(f32[5,32,128]{2,1,0:T(8,128)S(1)} %get-tuple-element.40), channel_id=1, source_target_pairs={{0,8},{1,9},{2,10},{3,11},{4,12},{5,13},{6,14},{7,15},{8,0},{9,1},... | collective-permute-start | bytes 245768 | tf_op jit(solution)/shard_map/ppermute | solution.py:26
  100.0 5.2 %collective-permute-start.13 = (f32[5,32,128]{2,1,0:T(8,128)S(1)}, f32[5,32,128]{2,1,0:T(8,128)S(1)}, u32[]{:S(2)}, u32[]{:S(2)}) collective-permute-start(f32[5,32,128]{2,1,0:T(8,128)S(1)} %get-tuple-element.41), channel_id=1, source_target_pairs={{0,16},{1,17},{2,18},{3,19},{4,20},{5,21},{6,22},{7,23},{8,24},{9,... | collective-permute-start | bytes 245768 | tf_op jit(solution)/shard_map/ppermute | solution.py:26
  100.0 6.2 %collective-permute-start.14 = (f32[5,32,128]{2,1,0:T(8,128)S(1)}, f32[5,32,128]{2,1,0:T(8,128)S(1)}, u32[]{:S(2)}, u32[]{:S(2)}) collective-permute-start(f32[5,32,128]{2,1,0:T(8,128)S(1)} %get-tuple-element.42), channel_id=1, source_target_pairs={{0,24},{1,25},{2,26},{3,27},{4,28},{5,29},{6,30},{7,31},{8,16},{9,... | collective-permute-start | bytes 245768 | tf_op jit(solution)/shard_map/ppermute | solution.py:26
  (3 other events, 3.4 us)

commit v5 on v4

--- a/solution.py
+++ b/solution.py
@@ -55,10 +55,7 @@
             lhs.append(jnp.concatenate([tile[j, k] for j in range(slot_share)], axis=0))
             blocks = [panel[n, k] for n in range(start, start + count)]
             rhs.append(jnp.concatenate(blocks, axis=1))
-    lhs_top, lhs_rest = split(jnp.concatenate(lhs, axis=1))
-    rhs_top, rhs_rest = split(jnp.concatenate(rhs, axis=0))
-    mul = functools.partial(jnp.dot, preferred_element_type=jnp.float32)
-    return mul(lhs_top, rhs_rest) + mul(lhs_rest, rhs_top) + mul(lhs_top, rhs_top)
+    return dot(jnp.concatenate(lhs, axis=1), jnp.concatenate(rhs, axis=0))
 
 
 def product_kernel(plan, place, *refs):
@@ -100,7 +97,9 @@
 
 
 def dot(a, b):
-    return jnp.dot(a, b, precision=highest, preferred_element_type=jnp.float32)
+    (a_top, a_rest), (b_top, b_rest) = split(a), split(b)
+    mul = functools.partial(jnp.dot, preferred_element_type=jnp.float32)
+    return mul(a_top, b_rest) + mul(a_rest, b_top) + mul(a_top, b_top)
 
 
 def rows_of(ref, *at):

time: 108 us -> 106 us (0.981)
  Pallas kernels: 15 us -> 13.8 us
    pallas_call x3, Pallas kernels: 8 us -> 6.73 us  [local(): pl.pallas_call(kernel, out_shape=[jax.ShapeDtypeStruct(shape, jnp.float32...]
  transfers between devices with their start and end apart: 17 -> 17, of which waited for: 7 -> 7; matrix products, arithmetic and copies ran while one was open for 5% -> 5% of each run, Pallas kernels for 11% -> 10%
where the time goes in v5:
time: 106 us
  waiting for transfers between devices  51.3 us (48%)
  starting transfers between devices  27 us (25%)
  Pallas kernels  13.8 us (13%)
  local copies, waits for them, and re-layouts  9.31 us (9%)
  matrix products  3.09 us (3%)
  between operations  1.06 us (1%)
    ppermute x15, waiting for transfers between devices, swap(): return lax.ppermute(array, ('row', 'col'), pairs)  39.1 us
    ppermute x15, starting transfers between devices, swap(): return lax.ppermute(array, ('row', 'col'), pairs)  14.6 us
    all_to_all x2, starting transfers between devices, exchange(): lax.all_to_all(tiles, 'col', 0, 0, axis_index_groups=groups, tiled=True)  12.4 us
    all_to_all x2, waiting for transfers between devices, exchange(): lax.all_to_all(tiles, 'col', 0, 0, axis_index_groups=groups, tiled=True)  12.3 us
    pallas_call x3, Pallas kernels, local(): pl.pallas_call(kernel, out_shape=[jax.ShapeDtypeStruct(shape, jnp.float32...  6.73 us
    pallas_call x4, Pallas kernels, product(): pl.pallas_call(functools.partial(product_kernel, (start, len(panels))), o...  5.26 us
    unnamed x40, local copies, waits for them, and re-layouts  5.09 us
    dot_general x9, matrix products, mm(): return jnp.einsum(spec, *operands, precision=precision)  3.09 us
  transfers between devices with their start and end apart: 17, of which 7 were waited for; matrix products, arithmetic and copies ran while one was open for 5% of the time, Pallas kernels for 10%

profile of v5, /device:TPU:0, one launch (start us, length us, event | category | flops | bytes accessed | tf_op | source)
XLA Modules:
  0.0 105.8 jit_solution(8708189742717101990)
XLA Ops:
  0.7 1.2 %constant_dynamic-slice_fusion.1 = (f32[2,2,128,128]{3,2,1,0:T(8,128)S(1)}, f32[2,2,128,128]{3,2,1,0:T(8,128)S(1)}) fusion(f32[2,4,128,128]{3,2,1,0:T(8,128)} %param.15, s32[]{:T(128)S(6)} %select_n.71, s32[]{:T(128)S(6)} %select_n.67), kind=kLoop, calls=%fused_computation.28 | loop fusion | bytes 1048584 | tf_op jit(solution)/shard_map/dynamic_slice | solution.py:216
  1.9 1.0 constant_dynamic-slice_fusion.2
  3.0 0.9 shard_map.138
  3.9 1.3 %copy-done.3 = f32[4,4,2,128,128]{4,3,2,1,0:T(8,128)} copy-done((f32[4,4,2,128,128]{4,3,2,1,0:T(8,128)}, f32[4,4,2,128,128]{4,3,2,1,0:T(8,128)S(1)}, u32[]{:S(2)}) %copy-start.3) | copy-done | bytes 2097176
  5.3 5.4 %all-to-all-start = ((f32[4,4,2,128,128]{4,3,2,1,0:T(8,128)}), f32[4,4,2,128,128]{4,3,2,1,0:T(8,128)S(1)}, u32[]{:S(2)}, u32[]{:S(2)}) async-start(f32[4,4,2,128,128]{4,3,2,1,0:T(8,128)} %copy-done.3), calls=%async_computation | async-start | bytes 4194304 | tf_op jit(solution)/shard_map/all_to_all | solution.py:212
  10.6 1.5 %collective-permute-start = (f32[3,2,128,128]{3,2,1,0:T(8,128)S(1)}, f32[3,2,128,128]{3,2,1,0:T(8,128)S(1)}, u32[]{:S(2)}, u32[]{:S(2)}) collective-permute-start(f32[3,2,128,128]{3,2,1,0:T(8,128)S(1)} %pad_maximum_fusion.1), channel_id=1, source_target_pairs={{0,16},{1,17},{2,18},{3,19},{4,20},{5,21},{6,22},{7,23},{8,24},{9,... | collective-permute-start | bytes 1179656 | tf_op jit(solution)/shard_map/ppermute | solution.py:26
  12.2 9.0 %collective-permute-done = f32[3,2,128,128]{3,2,1,0:T(8,128)S(1)} collective-permute-done((f32[3,2,128,128]{3,2,1,0:T(8,128)S(1)}, f32[3,2,128,128]{3,2,1,0:T(8,128)S(1)}, u32[]{:S(2)}, u32[]{:S(2)}) %collective-permute-start) | collective-permute-done | bytes 393248 | tf_op jit(solution)/shard_map/ppermute | solution.py:26
  21.3 2.8 %collective-permute-start.2 = (f32[3,2,128,128]{3,2,1,0:T(8,128)S(1)}, f32[3,2,128,128]{3,2,1,0:T(8,128)}, u32[]{:S(2)}, u32[]{:S(2)}) collective-permute-start(f32[3,2,128,128]{3,2,1,0:T(8,128)S(1)} %get-tuple-element.48), channel_id=1, source_target_pairs={{0,4},{1,5},{2,6},{3,7},{4,0},{5,1},{6,2},{7,3},{8,12},{9,13},{10,... | collective-permute-start | bytes 1179656 | tf_op jit(solution)/shard_map/ppermute | solution.py:26
  24.1 1.5 %collective-permute-start.3 = (f32[3,2,128,128]{3,2,1,0:T(8,128)S(1)}, f32[3,2,128,128]{3,2,1,0:T(8,128)S(1)}, u32[]{:S(2)}, u32[]{:S(2)}) collective-permute-start(f32[3,2,128,128]{3,2,1,0:T(8,128)S(1)} %get-tuple-element.34.refs_0_), channel_id=1, source_target_pairs={{0,16},{1,17},{2,18},{3,19},{4,20},{5,21},{6,22},{7,23},{8,24},{9,... | collective-permute-start | bytes 1179656 | tf_op jit(solution)/shard_map/ppermute | solution.py:26
  26.3 1.6 %copy-done.1 = f32[1024,512]{1,0:T(8,128)S(1)} copy-done((f32[1024,512]{1,0:T(8,128)S(1)}, f32[1024,512]{1,0:T(8,128)}, u32[]{:S(2)}) %copy-start.1) | copy-done | bytes 2097176
  27.9 0.9 shard_map.137
  28.8 1.4 %copy-done.2 = f32[4,4,2,128,128]{4,3,2,1,0:T(8,128)} copy-done((f32[4,4,2,128,128]{4,3,2,1,0:T(8,128)}, f32[4,4,2,128,128]{4,3,2,1,0:T(8,128)S(1)}, u32[]{:S(2)}) %copy-start.2) | copy-done | bytes 2097176
  30.1 6.4 %collective-permute-done.1 = f32[8,32,128]{2,1,0:T(8,128)S(1)} collective-permute-done((f32[8,32,128]{2,1,0:T(8,128)S(1)}, f32[8,32,128]{2,1,0:T(8,128)S(1)}, u32[]{:S(2)}, u32[]{:S(2)}) %collective-permute-start.1) | collective-permute-done | bytes 131104 | tf_op jit(solution)/shard_map/ppermute | solution.py:26
  36.5 5.2 %collective-permute-done.2.refs_1_ = f32[3,2,128,128]{3,2,1,0:T(8,128)} collective-permute-done((f32[3,2,128,128]{3,2,1,0:T(8,128)S(1)}, f32[3,2,128,128]{3,2,1,0:T(8,128)}, u32[]{:S(2)}, u32[]{:S(2)}) %collective-permute-start.2) | collective-permute-done | bytes 393248 | tf_op jit(solution)/shard_map/ppermute | solution.py:26
  41.7 0.8 copy-done.6
  42.5 1.6 %collective-permute-start.4 = (f32[3,2,128,128]{3,2,1,0:T(8,128)}, f32[3,2,128,128]{3,2,1,0:T(8,128)}, u32[]{:S(2)}, u32[]{:S(2)}) collective-permute-start(f32[3,2,128,128]{3,2,1,0:T(8,128)} %collective-permute-done.2.refs_1_), channel_id=1, source_target_pairs={{0,16},{1,17},{2,18},{3,19},{4,20},{5,21},{6,22},{7,23},{8,24},{9,... | collective-permute-start | bytes 1179656 | tf_op jit(solution)/shard_map/ppermute | solution.py:26
  44.1 7.0 %all-to-all-start.1 = ((f32[4,4,2,128,128]{4,3,2,1,0:T(8,128)}), f32[4,4,2,128,128]{4,3,2,1,0:T(8,128)}, u32[]{:S(2)}, u32[]{:S(2)}) async-start(f32[4,4,2,128,128]{4,3,2,1,0:T(8,128)} %copy-done.2), calls=%async_computation.1 | async-start | bytes 4194304 | tf_op jit(solution)/shard_map/all_to_all | solution.py:212
  51.2 1.6 %shard_map.139.refs_4_ = f32[3,4,128,128]{3,2,1,0:T(8,128)S(1)} custom-call(s32[1]{0:T(128)} %bitcast.place, f32[4,4,2,128,128]{4,3,2,1,0:T(8,128)S(1)} %all-to-all-done.refs_0_.refs_1_, f32[3,2,128,128]{3,2,1,0:T(8,128)} %collective-permute-done.2.refs_1_), custom_call_target="tpu_custom_call" | custom-call | flops 301989888 | bytes 4194304 | tf_op jit(solution)/shard_map/pallas_call | solution.py:84
  53.1 0.6 gather_fusion
  53.8 2.1 %shard_map.140.refs_2_ = f32[3,4,128,128]{3,2,1,0:T(8,128)S(1)} custom-call(s32[1]{0:T(128)} %bitcast.place, f32[4,4,2,128,128]{4,3,2,1,0:T(8,128)S(1)} %all-to-all-done.refs_0_.refs_1_, f32[4,4,2,128,128]{4,3,2,1,0:T(8,128)S(1)} %all-to-all-done.refs_0_.refs_1_, f32[3,2,128,128]{3,2,1,0:T(8,128)} %collective-permute-done.4.refs_2_, ...), custom_call_target="tpu_custom_call" | custom-call | flops 603979776 | bytes 4194304 | tf_op jit(solution)/shard_map/pallas_call | solution.py:84
  56.3 1.2 %shard_map.142 = f32[2,4,128,128]{3,2,1,0:T(8,128)} custom-call(s32[1]{0:T(128)} %bitcast.place, f32[4,4,2,128,128]{4,3,2,1,0:T(8,128)S(1)} %all-to-all-done.refs_0_.refs_1_, f32[3,2,128,128]{3,2,1,0:T(8,128)S(1)} %collective-permute-done.5.refs_1_, f32[3,4,128,128]{3,2,1,0:T(8,128)S(1)} %shard_map.140.refs_2_), custom_call_target="tpu_custom_call" | custom-call | flops 201326592 | bytes 4194304 | tf_op jit(solution)/shard_map/pallas_call | solution.py:84
  57.8 3.5 %collective-permute-start.7 = (f32[1,4,128,128]{3,2,1,0:T(8,128)S(1)}, f32[1,4,128,128]{3,2,1,0:T(8,128)S(1)}, u32[]{:S(2)}, u32[]{:S(2)}) collective-permute-start(f32[1,4,128,128]{3,2,1,0:T(8,128)S(1)} %shard_map.141), channel_id=1, source_target_pairs={{0,4},{1,5},{2,6},{3,7},{4,0},{5,1},{6,2},{7,3},{8,12},{9,13},{10,... | collective-permute-start | bytes 786440 | tf_op jit(solution)/shard_map/ppermute | solution.py:26
  65.2 0.6 convolution_bitcast_fusion.kid_hat
  65.8 14.7 %collective-permute-done.7.back = f32[1,4,128,128]{3,2,1,0:T(8,128)S(1)} collective-permute-done((f32[1,4,128,128]{3,2,1,0:T(8,128)S(1)}, f32[1,4,128,128]{3,2,1,0:T(8,128)S(1)}, u32[]{:S(2)}, u32[]{:S(2)}) %collective-permute-start.7) | collective-permute-done | bytes 262176 | tf_op jit(solution)/shard_map/ppermute | solution.py:26
  80.6 12.3 %all-to-all-done.1.tiles = f32[4,4,2,128,128]{4,3,2,1,0:T(8,128)} async-done(((f32[4,4,2,128,128]{4,3,2,1,0:T(8,128)}), f32[4,4,2,128,128]{4,3,2,1,0:T(8,128)}, u32[]{:S(2)}, u32[]{:S(2)}) %all-to-all-start.1) | async-done | bytes 2097184 | tf_op jit(solution)/shard_map/all_to_all | solution.py:212
  92.8 4.6 %shard_map.143 = (f32[1,4,128,128]{3,2,1,0:T(8,128)}, f32[5,128,128]{2,1,0:T(8,128)S(1)}, f32[2,4,128,128]{3,2,1,0:T(8,128)S(1)}) custom-call(s32[1]{0:T(128)} %bitcast.place, f32[4,4,2,128,128]{4,3,2,1,0:T(8,128)} %all-to-all-done.1.tiles, f32[1,4,128,128]{3,2,1,0:T(8,128)S(1)} %collective-permute-done.7.back, f32[128,128]{1,0:T(8,128)S(1)} %bitcast.66, ...), custom_call_target="tpu_custom_call" | custom-call | flops 100000000 | bytes 2097152 | tf_op jit(solution)/shard_map/pallas_call | solution.py:162
  97.4 1.4 %shard_map.144 = (f32[2,4,128,128]{3,2,1,0:T(8,128)}, f32[5,32,128]{2,1,0:T(8,128)S(1)}, f32[5,32,128]{2,1,0:T(8,128)S(1)}, f32[5,32,128]{2,1,0:T(8,128)S(1)}, f32[5,32,128]{2,1,0:T(8,128)S(1)}) custom-call(s32[1]{0:T(128)} %bitcast.1.place, f32[2,4,128,128]{3,2,1,0:T(8,128)S(1)} %get-tuple-element.37.kid_sum, ...), custom_call_target="tpu_custom_call" | custom-call | flops 100000000 | bytes 2097152 | tf_op jit(solution)/shard_map/pallas_call | solution.py:162
  99.0 1.7 %collective-permute-start.14 = (f32[5,32,128]{2,1,0:T(8,128)S(1)}, f32[5,32,128]{2,1,0:T(8,128)S(1)}, u32[]{:S(2)}, u32[]{:S(2)}) collective-permute-start(f32[5,32,128]{2,1,0:T(8,128)S(1)} %get-tuple-element.42), channel_id=1, source_target_pairs={{0,24},{1,25},{2,26},{3,27},{4,28},{5,29},{6,30},{7,31},{8,16},{9,... | collective-permute-start | bytes 245768 | tf_op jit(solution)/shard_map/ppermute | solution.py:26
  100.6 0.7 constant_dynamic-slice_fusion.par_pivot
  101.3 2.7 %collective-permute-done.13.refs_2_ = f32[5,32,128]{2,1,0:T(8,128)S(1)} collective-permute-done((f32[5,32,128]{2,1,0:T(8,128)S(1)}, f32[5,32,128]{2,1,0:T(8,128)S(1)}, u32[]{:S(2)}, u32[]{:S(2)}) %collective-permute-start.13) | collective-permute-done | bytes 81952 | tf_op jit(solution)/shard_map/ppermute | solution.py:26
  104.0 1.0 collective-permute-done.14.refs_3_
  105.0 0.8 shard_map.145
  (79 shorter events, 5.9 us)
Async XLA Ops:
  0.6 2.4 %copy-start = (f32[1024,512]{1,0:T(8,128)S(1)}, f32[1024,512]{1,0:T(8,128)}, u32[]{:S(2)}) copy-start(f32[1024,512]{1,0:T(8,128)} %ainv.1) | copy-start | bytes 6291460
  0.6 2.4 %copy-start.8 = (s32[8,16]{1,0:T(8,128)S(1)}, s32[8,16]{1,0:T(8,128)}, u32[]{:S(2)}) copy-start(s32[8,16]{1,0:T(8,128)} %struct.3) | copy-start | bytes 1540
  5.2 6.9 %copy-start.16 = (f32[1,32,128]{2,1,0:T(8,128)S(1)}, f32[1,32,128]{2,1,0:T(8,128)}, u32[]{:S(2)}) copy-start(f32[1,32,128]{2,1,0:T(8,128)} %param.13) | copy-start | bytes 49156
  5.3 6.9 %copy-start.17 = (f32[1,32,128]{2,1,0:T(8,128)S(1)}, f32[1,32,128]{2,1,0:T(8,128)}, u32[]{:S(2)}) copy-start(f32[1,32,128]{2,1,0:T(8,128)} %param.14) | copy-start | bytes 49156
  5.3 20.4 %copy-start.13 = (f32[2,32,128]{2,1,0:T(8,128)S(1)}, f32[2,32,128]{2,1,0:T(8,128)}, u32[]{:S(2)}) copy-start(f32[2,32,128]{2,1,0:T(8,128)} %param.16) | copy-start | bytes 98308
  5.3 20.4 %copy-start.14 = (f32[2,32,128]{2,1,0:T(8,128)S(1)}, f32[2,32,128]{2,1,0:T(8,128)}, u32[]{:S(2)}) copy-start(f32[2,32,128]{2,1,0:T(8,128)} %param.17) | copy-start | bytes 98308
  5.3 20.4 %copy-start.15 = (f32[2,32,128]{2,1,0:T(8,128)S(1)}, f32[2,32,128]{2,1,0:T(8,128)}, u32[]{:S(2)}) copy-start(f32[2,32,128]{2,1,0:T(8,128)} %param.18) | copy-start | bytes 98308
  5.3 38.8 %all-to-all-start = ((f32[4,4,2,128,128]{4,3,2,1,0:T(8,128)}), f32[4,4,2,128,128]{4,3,2,1,0:T(8,128)S(1)}, u32[]{:S(2)}, u32[]{:S(2)}) async-start(f32[4,4,2,128,128]{4,3,2,1,0:T(8,128)} %copy-done.3), calls=%async_computation | async-start | bytes 4194304 | tf_op jit(solution)/shard_map/all_to_all | solution.py:212
  10.6 10.6 %collective-permute-start = (f32[3,2,128,128]{3,2,1,0:T(8,128)S(1)}, f32[3,2,128,128]{3,2,1,0:T(8,128)S(1)}, u32[]{:S(2)}, u32[]{:S(2)}) collective-permute-start(f32[3,2,128,128]{3,2,1,0:T(8,128)S(1)} %pad_maximum_fusion.1), channel_id=1, source_target_pairs={{0,16},{1,17},{2,18},{3,19},{4,20},{5,21},{6,22},{7,23},{8,24},{9,... | collective-permute-start | bytes 1179656 | tf_op jit(solution)/shard_map/ppermute | solution.py:26
  21.3 7.5 %copy-start.4 = (f32[3,2,128,128]{3,2,1,0:T(8,128)}, f32[3,2,128,128]{3,2,1,0:T(8,128)S(1)}, u32[]{:S(2)}) copy-start(f32[3,2,128,128]{3,2,1,0:T(8,128)S(1)} %get-tuple-element.34.refs_0_) | copy-start | bytes 1179652
  21.3 20.4 %collective-permute-start.2 = (f32[3,2,128,128]{3,2,1,0:T(8,128)S(1)}, f32[3,2,128,128]{3,2,1,0:T(8,128)}, u32[]{:S(2)}, u32[]{:S(2)}) collective-permute-start(f32[3,2,128,128]{3,2,1,0:T(8,128)S(1)} %get-tuple-element.48), channel_id=1, source_target_pairs={{0,4},{1,5},{2,6},{3,7},{4,0},{5,1},{6,2},{7,3},{8,12},{9,13},{10,... | collective-permute-start | bytes 1179656 | tf_op jit(solution)/shard_map/ppermute | solution.py:26
  24.1 17.6 %collective-permute-start.3 = (f32[3,2,128,128]{3,2,1,0:T(8,128)S(1)}, f32[3,2,128,128]{3,2,1,0:T(8,128)S(1)}, u32[]{:S(2)}, u32[]{:S(2)}) collective-permute-start(f32[3,2,128,128]{3,2,1,0:T(8,128)S(1)} %get-tuple-element.34.refs_0_), channel_id=1, source_target_pairs={{0,16},{1,17},{2,18},{3,19},{4,20},{5,21},{6,22},{7,23},{8,24},{9,... | collective-permute-start | bytes 1179656 | tf_op jit(solution)/shard_map/ppermute | solution.py:26
  25.7 10.8 %collective-permute-start.1 = (f32[8,32,128]{2,1,0:T(8,128)S(1)}, f32[8,32,128]{2,1,0:T(8,128)S(1)}, u32[]{:S(2)}, u32[]{:S(2)}) collective-permute-start(f32[8,32,128]{2,1,0:T(8,128)S(1)} %constant_dynamic-update-slice_fusion), channel_id=1, source_target_pairs={{0,16},{1,17},{2,18},{3,19},{4,20},{5,21},{6,22},{7,23},{8,24},{9,... | collective-permute-start | bytes 393224 | tf_op jit(solution)/shard_map/ppermute | solution.py:26
  26.3 1.6 %copy-start.1 = (f32[1024,512]{1,0:T(8,128)S(1)}, f32[1024,512]{1,0:T(8,128)}, u32[]{:S(2)}) copy-start(f32[1024,512]{1,0:T(8,128)} %ainv.1) | copy-start | bytes 6291460
  42.5 10.3 %collective-permute-start.4 = (f32[3,2,128,128]{3,2,1,0:T(8,128)}, f32[3,2,128,128]{3,2,1,0:T(8,128)}, u32[]{:S(2)}, u32[]{:S(2)}) collective-permute-start(f32[3,2,128,128]{3,2,1,0:T(8,128)} %collective-permute-done.2.refs_1_), channel_id=1, source_target_pairs={{0,16},{1,17},{2,18},{3,19},{4,20},{5,21},{6,22},{7,23},{8,24},{9,... | collective-permute-start | bytes 1179656 | tf_op jit(solution)/shard_map/ppermute | solution.py:26
  44.1 9.6 %collective-permute-start.6 = (f32[3,2,128,128]{3,2,1,0:T(8,128)}, f32[3,2,128,128]{3,2,1,0:T(8,128)}, u32[]{:S(2)}, u32[]{:S(2)}) collective-permute-start(f32[3,2,128,128]{3,2,1,0:T(8,128)} %collective-permute-done.2.refs_1_), channel_id=1, source_target_pairs={{0,8},{1,9},{2,10},{3,11},{4,12},{5,13},{6,14},{7,15},{8,0},{9,1},... | collective-permute-start | bytes 1179656 | tf_op jit(solution)/shard_map/ppermute | solution.py:26
  44.1 48.7 %all-to-all-start.1 = ((f32[4,4,2,128,128]{4,3,2,1,0:T(8,128)}), f32[4,4,2,128,128]{4,3,2,1,0:T(8,128)}, u32[]{:S(2)}, u32[]{:S(2)}) async-start(f32[4,4,2,128,128]{4,3,2,1,0:T(8,128)} %copy-done.2), calls=%async_computation.1 | async-start | bytes 4194304 | tf_op jit(solution)/shard_map/all_to_all | solution.py:212
  51.2 1.9 %copy-start.9 = (s32[4]{0:T(128)S(1)}, s32[4]{0:T(128)}, u32[]{:S(2)}) copy-start(s32[4]{0:T(128)} %constant.67.clone) | copy-start | bytes 52
  52.8 3.1 %collective-permute-start.5 = (f32[3,2,128,128]{3,2,1,0:T(8,128)}, f32[3,2,128,128]{3,2,1,0:T(8,128)S(1)}, u32[]{:S(2)}, u32[]{:S(2)}) collective-permute-start(f32[3,2,128,128]{3,2,1,0:T(8,128)} %collective-permute-done.4.refs_2_), channel_id=1, source_target_pairs={{0,8},{1,9},{2,10},{3,11},{4,12},{5,13},{6,14},{7,15},{8,0},{9,1},... | collective-permute-start | bytes 1179656 | tf_op jit(solution)/shard_map/ppermute | solution.py:26
  56.3 5.1 %copy-start.5 = (f32[3,2,128,128]{3,2,1,0:T(8,128)S(1)}, f32[3,2,128,128]{3,2,1,0:T(8,128)}, u32[]{:S(2)}) copy-start(f32[3,2,128,128]{3,2,1,0:T(8,128)} %copy-done.4) | copy-start | bytes 1179652
  56.3 5.1 %copy-start.7 = (f32[3,2,128,128]{3,2,1,0:T(8,128)S(1)}, f32[3,2,128,128]{3,2,1,0:T(8,128)}, u32[]{:S(2)}) copy-start(f32[3,2,128,128]{3,2,1,0:T(8,128)} %copy-done.6) | copy-start | bytes 1179652
  57.5 4.4 %collective-permute-start.8 = (f32[2,8,32,128]{3,2,1,0:T(8,128)S(1)}, f32[2,8,32,128]{3,2,1,0:T(8,128)S(1)}, u32[]{:S(2)}, u32[]{:S(2)}) collective-permute-start(f32[2,8,32,128]{3,2,1,0:T(8,128)S(1)} %pad_maximum_fusion.3), channel_id=1, source_target_pairs={{0,8},{1,9},{2,10},{3,11},{4,12},{5,13},{6,14},{7,15},{8,0},{9,1},... | collective-permute-start | bytes 786440 | tf_op jit(solution)/shard_map/ppermute | solution.py:26
  57.8 22.8 %collective-permute-start.7 = (f32[1,4,128,128]{3,2,1,0:T(8,128)S(1)}, f32[1,4,128,128]{3,2,1,0:T(8,128)S(1)}, u32[]{:S(2)}, u32[]{:S(2)}) collective-permute-start(f32[1,4,128,128]{3,2,1,0:T(8,128)S(1)} %shard_map.141), channel_id=1, source_target_pairs={{0,4},{1,5},{2,6},{3,7},{4,0},{5,1},{6,2},{7,3},{8,12},{9,13},{10,... | collective-permute-start | bytes 786440 | tf_op jit(solution)/shard_map/ppermute | solution.py:26
  61.3 36.1 %collective-permute-start.11 = (f32[2,4,128,128]{3,2,1,0:T(8,128)}, f32[2,4,128,128]{3,2,1,0:T(8,128)S(1)}, u32[]{:S(2)}, u32[]{:S(2)}) collective-permute-start(f32[2,4,128,128]{3,2,1,0:T(8,128)} %shard_map.142), channel_id=1, source_target_pairs={{0,4},{1,5},{2,6},{3,7},{4,0},{5,1},{6,2},{7,3},{8,12},{9,13},{10,... | collective-permute-start | bytes 1572872 | tf_op jit(solution)/shard_map/ppermute | solution.py:26
  61.3 19.2 %collective-permute-start.9 = (f32[3,2,128,128]{3,2,1,0:T(8,128)S(1)}, f32[3,2,128,128]{3,2,1,0:T(8,128)S(1)}, u32[]{:S(2)}, u32[]{:S(2)}) collective-permute-start(f32[3,2,128,128]{3,2,1,0:T(8,128)S(1)} %copy-done.5), channel_id=1, source_target_pairs={{0,8},{1,9},{2,10},{3,11},{4,12},{5,13},{6,14},{7,15},{8,0},{9,1},... | collective-permute-start | bytes 1179656 | tf_op jit(solution)/shard_map/ppermute | solution.py:26
  61.4 19.2 %collective-permute-start.10 = (f32[3,2,128,128]{3,2,1,0:T(8,128)S(1)}, f32[3,2,128,128]{3,2,1,0:T(8,128)}, u32[]{:S(2)}, u32[]{:S(2)}) collective-permute-start(f32[3,2,128,128]{3,2,1,0:T(8,128)S(1)} %copy-done.7), channel_id=1, source_target_pairs={{0,8},{1,9},{2,10},{3,11},{4,12},{5,13},{6,14},{7,15},{8,0},{9,1},... | collective-permute-start | bytes 1179656 | tf_op jit(solution)/shard_map/ppermute | solution.py:26
  62.5 2.0 %copy-start.11 = (f32[1,4,128,128]{3,2,1,0:T(8,128)S(1)}, f32[1,4,128,128]{3,2,1,0:T(8,128)}, u32[]{:S(2)}) copy-start(f32[1,4,128,128]{3,2,1,0:T(8,128)} %param.12) | copy-start | bytes 786436
  62.6 2.7 %copy-start.10 = (f32[2,4,128,128]{3,2,1,0:T(8,128)S(1)}, f32[2,4,128,128]{3,2,1,0:T(8,128)}, u32[]{:S(2)}) copy-start(f32[2,4,128,128]{3,2,1,0:T(8,128)} %param.15) | copy-start | bytes 1572868
  63.2 1.8 %copy-start.12 = (f32[128,128]{1,0:T(8,128)}, f32[128,128]{1,0:T(8,128)S(1)}, u32[]{:S(2)}) copy-start(f32[128,128]{1,0:T(8,128)S(1)} %fusion.11) | copy-start | bytes 196612
  98.8 2.6 %collective-permute-start.12 = (f32[5,32,128]{2,1,0:T(8,128)S(1)}, f32[5,32,128]{2,1,0:T(8,128)S(1)}, u32[]{:S(2)}, u32[]{:S(2)}) collective-permute-start(f32[5,32,128]{2,1,0:T(8,128)S(1)} %get-tuple-element.40), channel_id=1, source_target_pairs={{0,8},{1,9},{2,10},{3,11},{4,12},{5,13},{6,14},{7,15},{8,0},{9,1},... | collective-permute-start | bytes 245768 | tf_op jit(solution)/shard_map/ppermute | solution.py:26
  98.8 5.2 %collective-permute-start.13 = (f32[5,32,128]{2,1,0:T(8,128)S(1)}, f32[5,32,128]{2,1,0:T(8,128)S(1)}, u32[]{:S(2)}, u32[]{:S(2)}) collective-permute-start(f32[5,32,128]{2,1,0:T(8,128)S(1)} %get-tuple-element.41), channel_id=1, source_target_pairs={{0,16},{1,17},{2,18},{3,19},{4,20},{5,21},{6,22},{7,23},{8,24},{9,... | collective-permute-start | bytes 245768 | tf_op jit(solution)/shard_map/ppermute | solution.py:26
  99.0 6.0 %collective-permute-start.14 = (f32[5,32,128]{2,1,0:T(8,128)S(1)}, f32[5,32,128]{2,1,0:T(8,128)S(1)}, u32[]{:S(2)}, u32[]{:S(2)}) collective-permute-start(f32[5,32,128]{2,1,0:T(8,128)S(1)} %get-tuple-element.42), channel_id=1, source_target_pairs={{0,24},{1,25},{2,26},{3,27},{4,28},{5,29},{6,30},{7,31},{8,16},{9,... | collective-permute-start | bytes 245768 | tf_op jit(solution)/shard_map/ppermute | solution.py:26
  (3 other events, 3.4 us)
